TPU v7x, 128 devices: a whole 4x4x4 slice. The times are simulated.
128 devices in a mesh: seq: 32 (over x, y, core), tensor: 4 (over z).
Axes of the slice: x: 4, y: 4, z: 4, core: 2. Of those that a mesh axis runs over, the one named last changes fastest.
Arguments:
- inputs: bfloat16 [131072, 2048], P('seq', 'tensor'), may hold values from -6 to 6
- out_grad: bfloat16 [131072, 2048], P('seq', 'tensor'), may hold values from -6 to 6
- router_score: float32 [131072], P('seq'), may hold values from 0.1 to 1
- route_index: int32 [32, 512], P('seq'), may hold values from 0 to 4095, as said below
- block_count: int32 [32], P('seq'), may hold values from 1 to 4, 64 in all
- w_in: bfloat16 [2048, 8192], P('seq', 'tensor'), may hold values from -0.125 to 0.125
- w_out: bfloat16 [8192, 2048], P('tensor', 'seq'), may hold values from -0.0625 to 0.0625
Outputs:
- input_grad: bfloat16 [131072, 2048], P('seq', 'tensor')
- score_grad: float32 [131072], P('seq')
Inputs may be any that keep to these rules, and one draw needn't show every extreme that they name: `route_index`: row j holds 512 distinct positions within shard j; its first block_count[j] * 128 entries are the routed tokens, the rest padding. `block_count`: the counts sum to exactly 64.
All inputs are finite; a program needn't handle non-finite values.
Results may differ from a plain program's by a relative error of at most 0.012.
Values may be sent and summed in bfloat16 or wider, within the bound.
No kernel may reach another device: no remote copies, remote signals or barrier semaphores. Data moves between devices by JAX's collectives and lax.ppermute only.
A program may use at most 128 MiB of HBM per device.

v0:
```python
import jax
import jax.numpy as jnp
from jax import lax
from jax.sharding import PartitionSpec as P

BLK = 128


gelu_coeff = 0.7978845608028654
cubic_coeff = 0.044715


def gelu_pair(values):
    inner = gelu_coeff * (values + cubic_coeff * values * values * values)
    tangent = jnp.tanh(inner)
    forward = 0.5 * values * (1.0 + tangent)
    slope = 0.5 * (1.0 + tangent) + 0.5 * values * (1.0 - tangent * tangent) * gelu_coeff * (
        1.0 + 3.0 * cubic_coeff * values * values
    )
    return (forward, slope)


def heavy_backward(chosen, grads, scores, w_in, w_out):
    full_inputs, full_grads = (
        lax.all_gather(chosen, "tensor", axis=1, tiled=True),
        lax.all_gather(grads, "tensor", axis=1, tiled=True),
    )
    weight_rows = lax.all_gather(w_in, "seq", axis=0, tiled=True)
    hidden = jnp.dot(full_inputs, weight_rows, preferred_element_type=jnp.float32)
    upstream = lax.dot_general(
        full_grads,
        lax.all_gather(w_out, "seq", axis=1, tiled=True),
        (((1,), (1,)), ((), ())),
        preferred_element_type=jnp.float32,
    )
    forward, slope = gelu_pair(hidden)
    active = forward.astype(jnp.bfloat16)
    score_part = jnp.sum(upstream * active.astype(jnp.float32), axis=1)
    row_scores = lax.psum(score_part, "tensor")
    hidden_grad = (scores[:, None] * upstream * slope).astype(jnp.bfloat16)
    input_part = lax.dot_general(
        hidden_grad, weight_rows, (((1,), (1,)), ((), ())), preferred_element_type=jnp.float32
    )
    row_grads = lax.psum_scatter(
        input_part.astype(jnp.bfloat16), "tensor", scatter_dimension=1, tiled=True
    )
    return (row_grads, row_scores)


def per_device(inputs, out_grad, router_score, route_index, block_count, w_in, w_out):
    route_rows = route_index.shape[1]
    picked = route_index[0]
    own_count = block_count[0]
    sel_inputs = jnp.take(inputs, picked, axis=0)
    sel_grads = jnp.take(out_grad, picked, axis=0)
    sel_score = jnp.take(router_score, picked, axis=0)
    slot_ids = jnp.arange(route_rows, dtype=jnp.int32)
    mine_grads, mine_scores = heavy_backward(sel_inputs, sel_grads, sel_score, w_in, w_out)
    is_mine = slot_ids < own_count * BLK
    mine_grads = jnp.where(is_mine[:, None], mine_grads, jnp.zeros((), jnp.bfloat16))
    mine_scores = jnp.where(is_mine, mine_scores, 0.0)
    input_grad = jnp.zeros(inputs.shape, jnp.bfloat16).at[picked].set(mine_grads)
    score_grad = jnp.zeros(router_score.shape, jnp.float32).at[picked].set(mine_scores)
    return (input_grad, score_grad)


def solution(mesh):
    placed = (
        P("seq", "tensor"),
        P("seq", "tensor"),
        P("seq"),
        P("seq", None),
        P("seq"),
        P("seq", "tensor"),
        P("tensor", "seq"),
    )
    return jax.shard_map(
        per_device,
        mesh=mesh,
        in_specs=placed,
        out_specs=(P("seq", "tensor"), P("seq")),
        check_vma=False,
    )
```

profile of v0, /device:TPU:1, one launch (start us, length us, event | category | flops | bytes accessed | tf_op | source)
XLA Modules:
  0.0 262.5 jit_solution(4947731733306558388)
XLA Ops:
  7.2 0.0 copy-start
  7.2 0.0 all-gather.9.cloned.1.call-start
  7.2 0.7 compare_select_fusion
  7.9 0.7 compare_select_fusion.1
  8.6 0.0 copy-done
  8.6 3.1 %gather_fusion = f32[512]{0:T(512)S(1)} fusion(f32[4096]{0:T(1024)S(1)} %copy-done, s32[1024]{0:T(1024)S(1)} %pad_clamp_fusion.1), kind=kCustom, calls=%fused_computation.2 | custom fusion | bytes 6144 | tf_op jit(solution)/shard_map/jit(_take)/gather | solution.py:56
  11.8 0.7 broadcast_select_fusion.3
  12.5 4.7 %gather_fusion.1 = bf16[512,512]{1,0:T(8,128)(2,1)S(1)} fusion(bf16[4096,512]{1,0:T(8,128)(2,1)} %param.10, s32[1024]{0:T(1024)S(1)} %pad_clamp_fusion), kind=kCustom, calls=%fused_computation.clone | custom fusion | bytes 1050624 | tf_op jit(solution)/shard_map/jit(_take)/gather | solution.py:55
  17.2 4.7 %gather_fusion.2 = bf16[512,512]{1,0:T(8,128)(2,1)S(1)} fusion(bf16[4096,512]{1,0:T(8,128)(2,1)} %param.9, s32[1024]{0:T(1024)S(1)} %pad_clamp_fusion), kind=kCustom, calls=%fused_computation.1.clone | custom fusion | bytes 1050624 | tf_op jit(solution)/shard_map/jit(_take)/gather | solution.py:54
  21.9 1.1 broadcast_select_fusion.1
  23.0 0.0 all-gather.9.cloned.1.call-update
  23.1 0.0 all-gather.11.cloned.1.call-start
  23.1 0.7 all-gather.11.cloned.1.call-update
  23.8 0.0 all-gather.5.cloned.1.call-start
  23.9 0.7 all-gather.5.cloned.1.call-update
  24.5 0.0 all-gather.7.cloned.1.call-start
  24.6 0.5 all-gather.7.cloned.1.call-update
  25.1 0.2 reduce-scatter.2.cloned.1.call-start
  25.3 31.9 %all-gather.9.cloned.1.call-done = bf16[512,2048]{1,0:T(8,128)(2,1)} async-done(((bf16[512,512]{1,0:T(8,128)(2,1)}), bf16[512,2048]{1,0:T(8,128)(2,1)}) %all-gather.9.cloned.1.call-update) | async-done | bytes 2097168 | tf_op jit(solution)/shard_map/all_gather | solution.py:25
  57.2 55.4 %all-gather.11.cloned.1.call-done = bf16[2048,2048]{1,0:T(8,128)(2,1)} async-done(((bf16[64,2048]{1,0:T(8,128)(2,1)}), bf16[2048,2048]{1,0:T(8,128)(2,1)}) %all-gather.11.cloned.1.call-update) | async-done | bytes 8388624 | tf_op jit(solution)/shard_map/all_gather | solution.py:28
  112.6 10.5 %fusion.25 = f32[512,2048]{1,0:T(8,128)} fusion(bf16[512,2048]{1,0:T(8,128)(2,1)} %all-gather.9.cloned.1.call-done, bf16[2048,2048]{1,0:T(8,128)(2,1)} %all-gather.11.cloned.1.call-done), kind=kOutput, calls=%fused_computation.44 | convolution fusion | flops 4294967296 | bytes 14680064 | tf_op jit(solution)/shard_map/dot_general | solution.py:29
  123.1 21.2 %all-gather.5.cloned.1.call-done = bf16[512,2048]{1,0:T(8,128)(2,1)} async-done(((bf16[512,512]{1,0:T(8,128)(2,1)}), bf16[512,2048]{1,0:T(8,128)(2,1)}) %all-gather.5.cloned.1.call-update) | async-done | bytes 2097168 | tf_op jit(solution)/shard_map/all_gather | solution.py:26
  144.4 55.2 %all-gather.7.cloned.1.call-done = bf16[2048,2048]{0,1:T(8,128)(2,1)} async-done(((bf16[2048,64]{0,1:T(8,128)(2,1)}), bf16[2048,2048]{0,1:T(8,128)(2,1)}) %all-gather.7.cloned.1.call-update) | async-done | bytes 8388624 | tf_op jit(solution)/shard_map/all_gather | solution.py:32
  199.6 0.0 copy-start.1
  199.6 0.0 copy-start.2
  199.6 12.0 %multiply_reduce_fusion = (f32[512]{0:T(512)S(1)}, f32[512,2048]{1,0:T(8,128)}) fusion(f32[512,2048]{1,0:T(8,128)} %fusion.25, bf16[512,2048]{1,0:T(8,128)(2,1)} %all-gather.5.cloned.1.call-done, bf16[2048,2048]{0,1:T(8,128)(2,1)} %all-gather.7.cloned.1.call-done), kind=kOutput, calls=%fused_computation.14 | convolution fusion | flops 4307549696 | bytes 18876416 | tf_op jit(solution)/shard_map/dot_general | solution.py:30
  211.6 0.0 copy-done.1
  211.6 0.0 copy-done.2
  211.7 9.3 %convolution_convert_fusion = bf16[512,2048]{1,0:T(8,128)(2,1)} fusion(bf16[2048,2048]{1,0:T(8,128)(2,1)S(1)} %copy-done.1, f32[512,2048]{1,0:T(8,128)S(1)} %copy-done.2, f32[512,2048]{1,0:T(8,128)} %get-tuple-element.8, f32[512]{0:T(512)S(1)} %get-tuple-element.3), kind=kOutput, calls=%fused_computation.16 | convolution fusion | flops 4316987392 | bytes 18876416 | tf_op jit(solution)/shard_map/dot_general | solution.py:41
  221.0 0.0 reduce-scatter.2.cloned.1.call-update
  221.7 8.7 %psum.7 = f32[512]{0:T(512)S(1)} all-reduce(f32[512]{0:T(512)S(1)} %get-tuple-element.7), channel_id=1, replica_groups=mesh['seq'=32,'tensor'=4] {'tensor'}, use_global_device_ids=true, to_apply=%region_3.5 | all-reduce | flops 512 | bytes 4096 | tf_op jit(solution)/shard_map/psum | solution.py:39
  230.3 3.0 %scatter_custom_fusion.1 = f32[4096]{0:T(1024)} fusion(s32[512]{0:T(512)S(1)} %bitcast.13, f32[512]{0:T(512)S(1)} %broadcast_select_fusion.2, f32[]{:T(128)} %constant.16.clone.1), kind=kCustom, calls=%fused_computation.30 | custom fusion | bytes 16388 | tf_op jit(solution)/shard_map/scatter | solution.py:63
  233.4 16.9 %reduce-scatter.2.cloned.1.call-done = bf16[512,512]{1,0:T(8,128)(2,1)} async-done(((bf16[512,2048]{1,0:T(8,128)(2,1)}), bf16[512,512]{1,0:T(8,128)(2,1)}) %reduce-scatter.2.cloned.1.call-update) | async-done | bytes 524304 | tf_op jit(solution)/shard_map/reduce_scatter | solution.py:44
  250.2 5.8 %scatter_custom_fusion = bf16[4096,512]{1,0:T(8,128)(2,1)} fusion(s32[512]{0:T(512)S(1)} %bitcast.14, bf16[]{:T(256)} %constant.7.clone.1, bf16[512,512]{1,0:T(8,128)(2,1)} %reduce-scatter.2.cloned.1.call-done, pred[512]{0:T(512)(128)(4,1)S(1)} %iota_compare_fusion), kind=kCustom, calls=%fused_computation.22 | custom fusion | flops 262144 | bytes 4720128 | tf_op jit(solution)/shard_map/scatter | solution.py:62
  (4 shorter events, 0.0 us)
Async XLA Ops:
  7.2 1.4 copy-start
  7.2 50.1 %all-gather.9.cloned.1.call-start = ((), (), s32[]{:S(2)}) async-start(), calls=%async_computation.3 | async-start | bytes 2621440 | tf_op jit(solution)/shard_map/all_gather | solution.py:25
  23.1 89.6 %all-gather.11.cloned.1.call-start = ((), (), s32[]{:S(2)}) async-start(), calls=%async_computation.4 | async-start | bytes 8650752 | tf_op jit(solution)/shard_map/all_gather | solution.py:28
  23.8 120.6 %all-gather.5.cloned.1.call-start = ((), (), s32[]{:S(2)}) async-start(), calls=%async_computation.1 | async-start | bytes 2621440 | tf_op jit(solution)/shard_map/all_gather | solution.py:26
  24.5 175.1 %all-gather.7.cloned.1.call-start = ((), (), s32[]{:S(2)}) async-start(), calls=%async_computation.2 | async-start | bytes 8650752 | tf_op jit(solution)/shard_map/all_gather | solution.py:32
  25.1 225.1 %reduce-scatter.2.cloned.1.call-start = ((), (), s32[]{:S(2)}) async-start(), calls=%async_computation.5 | async-start | bytes 2621440 | tf_op jit(solution)/shard_map/reduce_scatter | solution.py:44
  199.6 12.1 %copy-start.1 = (bf16[2048,2048]{1,0:T(8,128)(2,1)S(1)}, bf16[2048,2048]{1,0:T(8,128)(2,1)}, u32[]{:S(2)}) copy-start(bf16[2048,2048]{1,0:T(8,128)(2,1)} %all-gather.11.cloned.1.call-done) | copy-start | bytes 25165828
  199.6 12.1 %copy-start.2 = (f32[512,2048]{1,0:T(8,128)S(1)}, f32[512,2048]{1,0:T(8,128)}, u32[]{:S(2)}) copy-start(f32[512,2048]{1,0:T(8,128)} %fusion.25) | copy-start | bytes 12582916
Sparse Core Ops, SparseCore 0:
  23.2 34.0 all-gather.8
  59.5 53.0 all-gather.10
  114.3 30.0 all-gather.4
  146.5 53.0 all-gather.6
  221.1 29.0 reduce-scatter.1
where the time goes:
time: 263 us
  waiting for transfers between devices  183 us (70%)
  matrix products  31.9 us (12%)
  local copies, waits for them, and re-layouts  15.6 us (6%)
  between operations  14.5 us (6%)
  other arithmetic  9.01 us (3%)
  blocking collectives  8.67 us (3%)
    all_gather x1, waiting for transfers between devices, heavy_backward(): weight_rows = lax.all_gather(w_in, 'seq', axis=0, tiled=True)  55.4 us
    all_gather x1, waiting for transfers between devices, heavy_backward(): lax.all_gather(w_out, 'seq', axis=1, tiled=True)  55.2 us
    all_gather x1, waiting for transfers between devices, heavy_backward(): lax.all_gather(chosen, 'tensor', axis=1, tiled=True)  31.9 us
    all_gather x1, waiting for transfers between devices, heavy_backward(): lax.all_gather(grads, 'tensor', axis=1, tiled=True)  21.2 us
    reduce_scatter x1, waiting for transfers between devices, heavy_backward(): lax.psum_scatter(input_part.astype(jnp.bfloat16), 'tensor', scatter_dimen...  16.9 us
    dot_general x1, matrix products, heavy_backward(): lax.dot_general(full_grads, lax.all_gather(w_out, 'seq', axis=1, tiled=Tr...  12 us
    dot_general x1, matrix products, heavy_backward(): jnp.dot(full_inputs, weight_rows, preferred_element_type=jnp.float32)  10.5 us
    dot_general x1, matrix products, heavy_backward(): lax.dot_general(hidden_grad, weight_rows, (((1,), (1,)), ((), ())), prefe...  9.32 us
  transfers between devices with their start and end apart: 5, of which 5 were waited for; matrix products, arithmetic and copies ran while one was open for 5% of the time, Pallas kernels for 0%

commit v1 on v0

v1 whole, which is shorter than its diff:
```python
import functools

import jax
import jax.numpy as jnp
from jax import lax
from jax.experimental import pallas as pl
from jax.experimental.pallas import tpu as pltpu
from jax.sharding import PartitionSpec as P


BLK = 128
SIDE = 4
CHIPS = SIDE * SIDE

gelu_coeff = 0.7978845608028654
cubic_coeff = 0.044715

RELS = (0, -1, 1, 2)


def gelu_pair(values):
    square = values * values
    inner = values * (gelu_coeff + gelu_coeff * cubic_coeff * square)
    h = 0.5 * jnp.tanh(inner) + 0.5
    forward = values * h
    bend = values * (2.0 * gelu_coeff + 6.0 * gelu_coeff * cubic_coeff * square)
    slope = h + h * ((1.0 - h) * bend)
    return (forward, slope)


def seq_pairs(target):
    pairs = []
    for x in range(SIDE):
        for y in range(SIDE):
            for c in range(2):
                tx, ty, tc = target(x, y, c)
                pairs.append((((x * SIDE) + y) * 2 + c, ((tx % SIDE) * SIDE + ty % SIDE) * 2 + tc))
    return pairs


def ring(step, phase):
    return seq_pairs(lambda x, y, c: (x + step, y, c) if (c == phase) else (x, y + step, c))


SWAP = seq_pairs(lambda x, y, c: (x, y, 1 - c))


def swap(value):
    return lax.ppermute(value, "seq", SWAP)


def hop(value, step, phase):
    return lax.ppermute(value, "seq", ring(step, phase))


ZPAIRS = []
for z_at in range(SIDE):
    for s_at in range(2 * CHIPS):
        to = (z_at + (1 if s_at % 2 == 0 else -1)) % SIDE
        ZPAIRS.append((s_at * SIDE + z_at, s_at * SIDE + to))


def zdir(value):
    return lax.ppermute(value, ("seq", "tensor"), ZPAIRS)


def zhop(value, step):
    return lax.ppermute(value, "tensor", [(i, (i + step) % SIDE) for i in range(SIDE)])


TILE = 256
ROWS = 512
TOK = 4096
SPAN = 1024
DOT = functools.partial(lax.dot_general, preferred_element_type=jnp.float32)
NN = (((1,), (0,)), ((), ()))
NT = (((1,), (1,)), ((), ()))
ANY = pl.BlockSpec(memory_space=pl.ANY)
HBM = pl.BlockSpec(memory_space=pltpu.MemorySpace.HBM)


def params(mib):
    return pltpu.CompilerParams(vmem_limit_bytes=mib << 20)


def whole(shape):
    return pl.BlockSpec(shape, lambda m, meta: (0,) * len(shape))


def pick_kernel(count, idx_hbm, score_hbm, x_hbm, g_hbm, out, s_out, idx, score, xv, gv, hot, sems):
    small = [
        pltpu.make_async_copy(idx_hbm, idx, sems.at[2]),
        pltpu.make_async_copy(score_hbm, score, sems.at[3]),
    ]
    copies = [
        pltpu.make_async_copy(x_hbm, xv, sems.at[0]),
        pltpu.make_async_copy(g_hbm, gv, sems.at[1]),
    ]
    for copy in small + copies:
        copy.start()
    for copy in small:
        copy.wait()
    column = jnp.broadcast_to(idx[...], (BLK, ROWS)).T
    for r in range(ROWS // BLK):

        @pl.when(r < count[0])
        def _(r=r):
            at = jnp.broadcast_to(column[r * BLK : (r + 1) * BLK, :1], (BLK, TOK))
            same = lax.broadcasted_iota(jnp.int32, (BLK, TOK), 1) == at
            hot[r * BLK : (r + 1) * BLK, :] = jnp.where(same, 1.0, 0.0).astype(jnp.bfloat16)
            s_out[r * BLK : (r + 1) * BLK, :] = jnp.sum(
                jnp.where(same, score[...], 0.0), axis=1, keepdims=True
            )

    for k, (copy, rows) in enumerate(zip(copies, (xv, gv))):
        copy.wait()

        @pl.when(count[0] <= 2)
        def _(k=k, rows=rows):
            at = pl.ds(0, TILE)
            out[k, at, :] = DOT(hot[at, :], rows[...], NN).astype(jnp.bfloat16)

        @pl.when(count[0] > 2)
        def _(k=k, rows=rows):
            out[k] = DOT(hot[...], rows[...], NN).astype(jnp.bfloat16)


def pick(count, idx, score, inputs, out_grad):
    return pl.pallas_call(
        pick_kernel,
        grid_spec=pltpu.PrefetchScalarGridSpec(
            num_scalar_prefetch=1,
            grid=(1,),
            in_specs=[HBM] * 4,
            out_specs=[whole((2, ROWS, 512)), whole((ROWS, 1))],
            scratch_shapes=[
                pltpu.VMEM((1, ROWS), jnp.int32),
                pltpu.VMEM((1, TOK), jnp.float32),
                pltpu.VMEM((TOK, 512), jnp.bfloat16),
                pltpu.VMEM((TOK, 512), jnp.bfloat16),
                pltpu.VMEM((ROWS, TOK), jnp.bfloat16),
                pltpu.SemaphoreType.DMA((4,)),
            ],
        ),
        out_shape=[
            jax.ShapeDtypeStruct((2, ROWS, 512), jnp.bfloat16),
            jax.ShapeDtypeStruct((ROWS, 1), jnp.float32),
        ],
        compiler_params=params(62),
        name="pick",
    )(count, idx, score, inputs, out_grad)


def tile_live(meta, half, tile):
    return tile * (TILE // BLK) < meta[48 + half]


def half_kernel(half, meta, *refs):
    rows, scale_ref = refs[:4], refs[4]
    (sw, p_f, p_b, h_in, h_out, y0f, y0b, yrf, yrb, yhf, yhb) = refs[5:16]
    last = (refs[16:19], refs[19:22])
    out, out_0, score, rv, wi, wo, hg, row_sems, sems = refs[22:]
    tile = pl.program_id(0)
    row_copies = [
        pltpu.make_async_copy(rows[r], rv.at[:, meta[54 + r]], row_sems.at[r]) for r in range(4)
    ]
    groups = [[], [], [], []]
    for w, target in ((0, wi), (1, wo)):
        line = [sw.at[w], p_f.at[w], p_b.at[w], (h_in, h_out)[w]]
        for y0, yr, yh in ((y0f, yrf, yhf), (y0b, yrb, yhb)):
            line += [y0.at[w], yr.at[pl.ds(2 * w, 2)], None, yh.at[w]]
        line += [last[w][0], last[w][1], None, last[w][2]]
        for k in range(CHIPS):
            if line[k] is not None:
                to = target.at[pl.ds(k, 2)] if k % 4 == 1 and k > 4 else target.at[k]
                groups[k // 4].append(pltpu.make_async_copy(line[k], to, sems.at[w, k]))

    @pl.when(tile == 0)
    def _():
        for copy in row_copies + groups[0] + groups[1] + groups[2] + groups[3]:
            copy.start()
        for copy in row_copies + groups[0] + groups[1]:
            copy.wait()

    at = pl.ds(pl.multiple_of(tile * TILE, TILE), TILE)

    def columns(which, first, last):
        parts = []
        for k in range(first, last):
            lanes = pl.ds(pl.multiple_of(meta[16 + k] * BLK, BLK), BLK)
            parts.append(rv[which, meta[k], at, lanes])
        return jnp.concatenate(parts, axis=1)

    live = tile_live(meta, half, tile)

    @pl.when(tile == 0)
    def _():
        for copy in groups[2] + groups[3]:
            copy.wait()

    @pl.when(live)
    def _():
        xs, gs, scale = columns(0, 0, CHIPS), columns(1, 0, CHIPS), scale_ref[...]
        total = None
        for n in range(4):
            cols = pl.ds(n * 256, 256)
            hidden = DOT(xs, wi[:, :, cols].reshape(CHIPS * BLK, 256), NN)
            upstream = DOT(gs, wo[:, :, cols].reshape(CHIPS * BLK, 256), NN)
            forward, slope = gelu_pair(hidden)
            active = forward.astype(jnp.bfloat16).astype(jnp.float32)
            term = jnp.sum(upstream * active, axis=1, keepdims=True)
            total = term if total is None else total + term
            hg[:, cols] = (scale * upstream * slope).astype(jnp.bfloat16)
        score[...] = total
        for q in range(4):
            where = meta[50 + q] * SIDE
            quarter = jnp.concatenate([wi[meta[32 + where + b]] for b in range(SIDE)], axis=0)
            result = DOT(hg[...], quarter, NT).astype(jnp.bfloat16)
            if q < 3:
                out[q] = result
            else:
                out_0[...] = result


def half_stage(half, meta, rows, s, pieces):
    col = pl.BlockSpec((TILE, 1), lambda m, meta: (m, 0))
    return pl.pallas_call(
        functools.partial(half_kernel, half),
        grid_spec=pltpu.PrefetchScalarGridSpec(
            num_scalar_prefetch=1,
            grid=(2,),
            in_specs=[ANY] * 4 + [col] + [ANY] * 17,
            out_specs=[
                pl.BlockSpec((3, TILE, 512), lambda m, meta: (0, m, 0)),
                pl.BlockSpec((TILE, 512), lambda m, meta: (m, 0)),
                col,
            ],
            scratch_shapes=[
                pltpu.VMEM((2, SIDE, ROWS, 512), jnp.bfloat16),
                pltpu.VMEM((CHIPS, BLK, 1024), jnp.bfloat16),
                pltpu.VMEM((CHIPS, BLK, 1024), jnp.bfloat16),
                pltpu.VMEM((TILE, 1024), jnp.bfloat16),
                pltpu.SemaphoreType.DMA((4,)),
                pltpu.SemaphoreType.DMA((2, CHIPS)),
            ],
        ),
        out_shape=[
            jax.ShapeDtypeStruct((3, ROWS, 512), jnp.bfloat16),
            jax.ShapeDtypeStruct((ROWS, 512), jnp.bfloat16),
            jax.ShapeDtypeStruct((ROWS, 1), jnp.float32),
        ],
        compiler_params=params(62),
        name="half_stage",
    )(meta, *rows, s, *pieces)


def marks_kernel(idx, out):
    token = lax.broadcasted_iota(jnp.int32, (SPAN, ROWS), 0) + pl.program_id(0) * SPAN
    hot = jnp.where(token == jnp.broadcast_to(idx[...], (SPAN, ROWS)), 1.0, 0.0)
    out[...] = hot.astype(jnp.bfloat16)


def marks(idx):
    return pl.pallas_call(
        marks_kernel,
        grid=(TOK // SPAN,),
        in_specs=[pl.BlockSpec((1, ROWS), lambda m: (0, 0))],
        out_specs=pl.BlockSpec((SPAN, ROWS), lambda m: (m, 0)),
        out_shape=jax.ShapeDtypeStruct((TOK, ROWS), jnp.bfloat16),
        compiler_params=params(62),
        name="marks",
    )(idx)


def place_kernel(count, hot, own, other, full_a, full_b, low_a, low_b, out, rows):
    step = pl.program_id(0)
    mid = ROWS // 2

    @pl.when(step == 0)
    def _():
        for at, parts in ((0, (full_a, low_a)), (mid, (full_b, low_b))):
            here = pl.ds(at, mid)
            total = own[here, :].astype(jnp.float32) + other[here, :].astype(jnp.float32)
            for part in parts:
                total = total + part[...].astype(jnp.float32)
            at_row = lax.broadcasted_iota(jnp.int32, (mid, 512), 0) + at
            total = jnp.where(at_row < count[0] * BLK, total, 0.0)
            rows[here, :] = total.astype(jnp.bfloat16)

    out[...] = DOT(hot[...], rows[...], NN).astype(jnp.bfloat16)


def place(count, hot, own, other, full_a, full_b, low_a, low_b):
    return pl.pallas_call(
        place_kernel,
        grid_spec=pltpu.PrefetchScalarGridSpec(
            num_scalar_prefetch=1,
            grid=(TOK // SPAN,),
            in_specs=[pl.BlockSpec((SPAN, ROWS), lambda m, count: (m, 0))] + [whole((ROWS, 512))] * 2 + [whole((ROWS // 2, 512))] * 4,
            out_specs=pl.BlockSpec((SPAN, 512), lambda m, count: (m, 0)),
            scratch_shapes=[pltpu.VMEM((ROWS, 512), jnp.bfloat16)],
        ),
        out_shape=jax.ShapeDtypeStruct((TOK, 512), jnp.bfloat16),
        compiler_params=params(62),
        name="place",
    )(count, hot, own, other, full_a, full_b, low_a, low_b)


def branch(inputs, out_grad, router_score, route_index, block_count, w_in, w_out):
    picked = route_index[0]
    own_count = block_count[0]
    seq = lax.axis_index("seq")
    z = lax.axis_index("tensor")
    c = seq % 2
    y = (seq // 2) % SIDE
    x = seq // (2 * SIDE)

    w_out_t = w_out.T
    half = w_in.shape[1] // 2
    other_in, other_out = swap(w_in), swap(w_out_t)
    par_count = swap(block_count)

    xg, s_own = pick(
        block_count, route_index, router_score[None, :], inputs, out_grad
    )
    z_own = zdir(xg)
    xg_par = swap(xg)
    s_par = swap(s_own)
    z_par = zdir(xg_par)
    z_two = zdir(z_own)
    far_par = swap(z_own)
    far_own = swap(z_par)
    two_par = swap(z_two)
    own_rows = (xg, z_own, far_own, z_two)
    par_rows = (xg_par, z_par, far_par, two_par)

    def cut(w):
        return lax.dynamic_slice_in_dim(w, c * half, half, axis=1)

    def joined(w, other):
        a, b = cut(w), cut(other)
        return jnp.where(c == 0, jnp.concatenate([a, b], 0), jnp.concatenate([b, a], 0))

    s = jnp.stack([joined(w_in, other_in), joined(w_out_t, other_out)])
    p_f, p_b = hop(s, 1, 0), hop(s, -1, 0)
    y0f, y0b = hop(s, 1, 1), hop(s, -1, 1)
    h_in, h_out = hop(p_f[0], 1, 0), hop(p_b[1], -1, 0)
    r = jnp.concatenate([p_f[:1], p_b[:1], p_f[1:], p_b[1:]], 0)
    yrf, yrb = hop(r, 1, 1), hop(r, -1, 1)
    h = jnp.stack([h_in, h_out])
    yhf, yhb = hop(h, 1, 1), hop(h, -1, 1)
    a_in, a_out = hop(y0f[0], 1, 1), hop(y0b[1], -1, 1)
    r_in, r_out = hop(yrf[:2], 1, 1), hop(yrb[2:], -1, 1)
    low, high = yhf[0], yhb[1]
    b_in, b_out = hop(low, 1, 1), hop(high, -1, 1)

    rels = jnp.array(RELS, jnp.int32)
    grid_1 = jnp.tile(rels, SIDE)
    grid_2 = jnp.repeat(rels, SIDE)
    px = (x + jnp.where(c == 0, grid_1, grid_2)) % SIDE
    py = (y + jnp.where(c == 0, grid_2, grid_1)) % SIDE
    at = jnp.arange(CHIPS, dtype=jnp.int32)
    where = px * SIDE + py
    inverse = jnp.sum(jnp.where(where[None, :] == at[:, None], at[None, :], 0), axis=1)
    near = jnp.where(c == 0, 3, 1)
    order = jnp.stack([2 * jnp.ones_like(z), jnp.ones_like(z), 3 * jnp.ones_like(z), 0 * z])
    came = jnp.stack([0 * z, near, 4 - near, 2 * jnp.ones_like(z)])
    meta = jnp.concatenate(
        [px, py, inverse, block_count, par_count, (z + order) % SIDE, (z + came) % SIDE]
    ).astype(jnp.int32)

    pieces = (s, p_f, p_b, h_in, h_out, y0f, y0b, yrf, yrb, yhf, yhb)
    pieces = pieces + (a_in, r_in, b_in, a_out, r_out, b_out)
    o_par, o_par_0, score_par = half_stage(1, meta, par_rows, s_par, pieces)
    other = swap(o_par)
    other_0 = swap(o_par_0)
    score_other = swap(score_par[:, 0])
    o_own, o_own_0, score_own = half_stage(0, meta, own_rows, s_own, pieces)

    mid = ROWS // 2

    def both(k, a, b, extra=None):
        total = o_own[k, a:b].astype(jnp.float32) + other[k, a:b].astype(jnp.float32)
        if extra is not None:
            total = total + extra.astype(jnp.float32)
        return total.astype(jnp.bfloat16)

    through_f = zhop(both(0, 0, mid), 1)
    through_b = zhop(both(0, mid, ROWS), -1)
    low_b = zhop(both(1, mid, ROWS), 1)
    low_a = zhop(both(2, 0, mid), -1)

    row_scores = score_own[:, 0] + score_other
    up_one, down_one = zhop(row_scores, 1), zhop(row_scores, -1)
    row_scores = (row_scores + zhop(row_scores, 2)) + (up_one + down_one)

    full_a = zhop(both(1, 0, mid, through_f), 1)
    full_b = zhop(both(2, mid, ROWS, through_b), -1)
    hot = marks(route_index)
    input_grad = place(block_count, hot, o_own_0, other_0, full_a, full_b, low_a, low_b)
    is_mine = jnp.arange(ROWS, dtype=jnp.int32) < own_count * BLK
    mine_scores = jnp.where(is_mine, row_scores, 0.0)
    score_grad = jnp.zeros(router_score.shape, jnp.float32)
    score_grad = score_grad.at[picked].set(
        mine_scores, mode="promise_in_bounds", unique_indices=True
    )
    return (input_grad, score_grad)


def solution(mesh):
    placed = (
        P("seq", "tensor"),
        P("seq", "tensor"),
        P("seq"),
        P("seq", None),
        P("seq"),
        P("seq", "tensor"),
        P("tensor", "seq"),
    )
    return jax.shard_map(
        branch,
        mesh=mesh,
        in_specs=placed,
        out_specs=(P("seq", "tensor"), P("seq")),
        check_vma=False,
    )
```

time: 263 us -> 159 us (0.60)
  the two profiles are of different devices: /device:TPU:1 before, /device:TPU:30 now
where the time goes in v1:
time: 159 us
  waiting for transfers between devices  56.1 us (35%)
  Pallas kernels  50.8 us (32%)
  starting transfers between devices  33.2 us (21%)
  local copies, waits for them, and re-layouts  11.4 us (7%)
  other arithmetic  5.3 us (3%)
  between operations  1.75 us (1%)
    ppermute x16, waiting for transfers between devices, hop(): return lax.ppermute(value, 'seq', ring(step, phase))  39.4 us
    pallas_call x2, Pallas kernels, half_stage(): pl.pallas_call(functools.partial(half_kernel, half), grid_spec=pltpu.Pref...  31.5 us
    ppermute x16, starting transfers between devices, hop(): return lax.ppermute(value, 'seq', ring(step, phase))  15.1 us
    ppermute x9, starting transfers between devices, zhop(): lax.ppermute(value, 'tensor', [(i, (i + step) % SIDE) for i in range(SIDE)])  10.8 us
    pallas_call x1, Pallas kernels, pick(): pl.pallas_call(pick_kernel, grid_spec=pltpu.PrefetchScalarGridSpec(num_sc...  8.88 us
    ppermute x9, waiting for transfers between devices, zhop(): lax.ppermute(value, 'tensor', [(i, (i + step) % SIDE) for i in range(SIDE)])  7.78 us
    pallas_call x1, Pallas kernels, place(): pl.pallas_call(place_kernel, grid_spec=pltpu.PrefetchScalarGridSpec(num_s...  6.92 us
    ppermute x11, starting transfers between devices, swap(): return lax.ppermute(value, 'seq', SWAP)  5.33 us
  transfers between devices with their start and end apart: 39, of which 16 were waited for; matrix products, arithmetic and copies ran while one was open for 8% of the time, Pallas kernels for 18%

profile of v1, /device:TPU:30, one launch (start us, length us, event | category | flops | bytes accessed | tf_op | source)
XLA Modules:
  0.0 158.6 jit_solution(11832547802122968644)
XLA Ops:
  1.2 0.9 dynamic-slice_bitcast_fusion.3
  2.1 0.9 dynamic-slice_bitcast_fusion.1
  3.3 0.5 collective-permute-start.8
  3.9 1.5 collective-permute-start.9
  6.3 8.9 %pick.1 = (bf16[2,512,512]{2,1,0:T(8,128)(2,1)}, f32[512,1]{1,0:T(8,128)}) custom-call(s32[1]{0:T(128)S(6)} %copy.10.count, s32[1,512]{1,0:T(1,128)} %idx_hbm.1, f32[1,4096]{1,0:T(1,128)} %bitcast.51, bf16[4096,512]{1,0:T(8,128)(2,1)} %x_hbm.1, bf16[4096,512]{1,0:T(8,128)(2,1)} %g_hbm.1), custom_call_target="tpu_custom_call" | custom-call | tf_op jit(solution)/shard_map/pick/pallas_call | solution.py:129
  15.2 2.0 %collective-permute-start.1 = (bf16[2,512,512]{2,1,0:T(8,128)(2,1)}, bf16[2,512,512]{2,1,0:T(8,128)(2,1)}, u32[]{:S(2)}, u32[]{:S(2)}) collective-permute-start(bf16[2,512,512]{2,1,0:T(8,128)(2,1)} %get-tuple-element.10.refs_0_), channel_id=1, source_target_pairs={{0,1},{4,7},{8,9},{12,15},{16,17},{20,23},{24,25},{28,31},{32,33},... | collective-permute-start | bytes 3145736 | tf_op jit(solution)/shard_map/ppermute | solution.py:64
  17.6 0.7 collective-permute-start.13
  18.5 1.8 %collective-permute-start.10 = (bf16[128,1024]{1,0:T(8,128)(2,1)S(1)}, bf16[128,1024]{1,0:T(8,128)(2,1)S(1)}, u32[]{:S(2)}, u32[]{:S(2)}) collective-permute-start(bf16[128,1024]{1,0:T(8,128)(2,1)S(1)} %get-tuple-element.28), channel_id=1, source_target_pairs={{0,32},{4,12},{8,40},{12,20},{16,48},{20,28},{24,56},{28,4},{32,64... | collective-permute-start | bytes 786440 | tf_op jit(solution)/shard_map/ppermute | solution.py:53
  20.7 1.0 slice_bitcast_fusion.3
  21.7 9.1 %collective-permute-done.13.refs_11_ = bf16[2,128,1024]{2,1,0:T(8,128)(2,1)S(1)} collective-permute-done((bf16[2,128,1024]{2,1,0:T(8,128)(2,1)S(1)}, bf16[2,128,1024]{2,1,0:T(8,128)(2,1)S(1)}, u32[]{:S(2)}, u32[]{:S(2)}) %collective-permute-start.13) | collective-permute-done | bytes 524320 | tf_op jit(solution)/shard_map/ppermute | solution.py:53
  30.8 1.7 %collective-permute-start.26 = (f32[512,1]{1,0:T(8,128)S(1)}, f32[512,1]{1,0:T(8,128)}, u32[]{:S(2)}, u32[]{:S(2)}) collective-permute-start(f32[512,1]{1,0:T(8,128)S(1)} %copy-done.16), channel_id=1, source_target_pairs={{0,4},{4,0},{8,12},{12,8},{16,20},{20,16},{24,28},{28,24},{32,36},... | collective-permute-start | bytes 6152 | tf_op jit(solution)/shard_map/ppermute | solution.py:49
  32.7 2.0 %collective-permute-start.21 = (bf16[128,1024]{1,0:T(8,128)(2,1)S(1)}, bf16[128,1024]{1,0:T(8,128)(2,1)S(1)}, u32[]{:S(2)}, u32[]{:S(2)}) collective-permute-start(bf16[128,1024]{1,0:T(8,128)(2,1)S(1)} %slice_bitcast_fusion.1), channel_id=1, source_target_pairs={{0,24},{4,100},{8,0},{12,108},{16,8},{20,116},{24,16},{28,124},{32... | collective-permute-start | bytes 786440 | tf_op jit(solution)/shard_map/ppermute | solution.py:53
  34.9 1.4 collective-permute-start.16
  36.4 2.6 %collective-permute-done.18.refs_16_ = bf16[128,1024]{1,0:T(8,128)(2,1)S(1)} collective-permute-done((bf16[128,1024]{1,0:T(8,128)(2,1)S(1)}, bf16[128,1024]{1,0:T(8,128)(2,1)S(1)}, u32[]{:S(2)}, u32[]{:S(2)}) %collective-permute-start.18) | collective-permute-done | bytes 262176 | tf_op jit(solution)/shard_map/ppermute | solution.py:53
  39.0 1.2 collective-permute-start.14
  40.3 0.7 collective-permute-start.15
  41.0 3.6 %collective-permute-done.16.refs_14_ = bf16[2,128,1024]{2,1,0:T(8,128)(2,1)S(1)} collective-permute-done((bf16[2,128,1024]{2,1,0:T(8,128)(2,1)S(1)}, bf16[2,128,1024]{2,1,0:T(8,128)(2,1)S(1)}, u32[]{:S(2)}, u32[]{:S(2)}) %collective-permute-start.16) | collective-permute-done | bytes 524320 | tf_op jit(solution)/shard_map/ppermute | solution.py:53
  45.0 0.7 slice_bitcast_fusion.2
  45.8 16.2 %collective-permute-done.17.refs_15_ = bf16[2,128,1024]{2,1,0:T(8,128)(2,1)S(1)} collective-permute-done((bf16[2,128,1024]{2,1,0:T(8,128)(2,1)S(1)}, bf16[2,128,1024]{2,1,0:T(8,128)(2,1)S(1)}, u32[]{:S(2)}, u32[]{:S(2)}) %collective-permute-start.17) | collective-permute-done | bytes 524320 | tf_op jit(solution)/shard_map/ppermute | solution.py:53
  62.0 1.7 %collective-permute-start.25 = (bf16[2,512,512]{2,1,0:T(8,128)(2,1)}, bf16[2,512,512]{2,1,0:T(8,128)(2,1)}, u32[]{:S(2)}, u32[]{:S(2)}) collective-permute-start(bf16[2,512,512]{2,1,0:T(8,128)(2,1)} %collective-permute-done.5.refs_3_), channel_id=1, source_target_pairs={{0,4},{4,0},{8,12},{12,8},{16,20},{20,16},{24,28},{28,24},{32,36},... | collective-permute-start | bytes 3145736 | tf_op jit(solution)/shard_map/ppermute | solution.py:49
  63.7 0.7 slice_bitcast_fusion
  64.5 2.1 %collective-permute-start.23 = (bf16[128,1024]{1,0:T(8,128)(2,1)}, bf16[128,1024]{1,0:T(8,128)(2,1)S(1)}, u32[]{:S(2)}, u32[]{:S(2)}) collective-permute-start(bf16[128,1024]{1,0:T(8,128)(2,1)} %slice_bitcast_fusion), channel_id=1, source_target_pairs={{0,24},{4,100},{8,0},{12,108},{16,8},{20,116},{24,16},{28,124},{32... | collective-permute-start | bytes 786440 | tf_op jit(solution)/shard_map/ppermute | solution.py:53
  66.8 0.8 slice.95
  67.6 0.8 slice.98
  68.4 2.6 %collective-permute-done.20.refs_18_ = bf16[128,1024]{1,0:T(8,128)(2,1)S(1)} collective-permute-done((bf16[128,1024]{1,0:T(8,128)(2,1)}, bf16[128,1024]{1,0:T(8,128)(2,1)S(1)}, u32[]{:S(2)}, u32[]{:S(2)}) %collective-permute-start.20) | collective-permute-done | bytes 262176 | tf_op jit(solution)/shard_map/ppermute | solution.py:53
  71.0 1.2 collective-permute-start.19
  72.3 0.8 collective-permute-start.22
  73.3 1.2 concatenate.54.meta
  74.6 3.7 %collective-permute-done.3.refs_1_ = bf16[2,512,512]{2,1,0:T(8,128)(2,1)} collective-permute-done((bf16[2,512,512]{2,1,0:T(8,128)(2,1)}, bf16[2,512,512]{2,1,0:T(8,128)(2,1)}, u32[]{:S(2)}, u32[]{:S(2)}) %collective-permute-start.3) | collective-permute-done | bytes 1048608 | tf_op jit(solution)/shard_map/ppermute | solution.py:64
  78.3 2.1 %collective-permute-done.19.refs_17_ = bf16[2,128,1024]{2,1,0:T(8,128)(2,1)S(1)} collective-permute-done((bf16[2,128,1024]{2,1,0:T(8,128)(2,1)}, bf16[2,128,1024]{2,1,0:T(8,128)(2,1)S(1)}, u32[]{:S(2)}, u32[]{:S(2)}) %collective-permute-start.19) | collective-permute-done | bytes 524320 | tf_op jit(solution)/shard_map/ppermute | solution.py:53
  80.4 2.6 %collective-permute-done.22.refs_20_ = bf16[2,128,1024]{2,1,0:T(8,128)(2,1)} collective-permute-done((bf16[2,128,1024]{2,1,0:T(8,128)(2,1)}, bf16[2,128,1024]{2,1,0:T(8,128)(2,1)}, u32[]{:S(2)}, u32[]{:S(2)}) %collective-permute-start.22) | collective-permute-done | bytes 524320 | tf_op jit(solution)/shard_map/ppermute | solution.py:53
  83.1 15.8 %half_stage.3 = (bf16[3,512,512]{2,1,0:T(8,128)(2,1)}, bf16[512,512]{1,0:T(8,128)(2,1)}, f32[512,1]{1,0:T(8,128)}) custom-call(s32[58]{0:T(128)} %concatenate.54.meta, bf16[2,512,512]{2,1,0:T(8,128)(2,1)} %collective-permute-done.2.refs_0_, bf16[2,512,512]{2,1,0:T(8,128)(2,1)} %collective-permute-done.3.refs_1_, ...), custom_call_target="tpu_custom_call" | custom-call | tf_op jit(solution)/shard_map/half_stage/pallas_call | solution.py:227
  99.5 4.7 %collective-permute-done.4.refs_2_ = bf16[2,512,512]{2,1,0:T(8,128)(2,1)} collective-permute-done((bf16[2,512,512]{2,1,0:T(8,128)(2,1)}, bf16[2,512,512]{2,1,0:T(8,128)(2,1)}, u32[]{:S(2)}, u32[]{:S(2)}) %collective-permute-start.4) | collective-permute-done | bytes 1048608 | tf_op jit(solution)/shard_map/ppermute | solution.py:49
  104.2 15.7 %half_stage.2 = (bf16[3,512,512]{2,1,0:T(8,128)(2,1)}, bf16[512,512]{1,0:T(8,128)(2,1)}, f32[512,1]{1,0:T(8,128)}) custom-call(s32[58]{0:T(128)} %concatenate.54.meta, bf16[2,512,512]{2,1,0:T(8,128)(2,1)} %get-tuple-element.10.refs_0_, bf16[2,512,512]{2,1,0:T(8,128)(2,1)} %collective-permute-done.1.refs_1_, ...), custom_call_target="tpu_custom_call" | custom-call | tf_op jit(solution)/shard_map/half_stage/pallas_call | solution.py:227
  120.0 2.3 %fusion.5 = (bf16[256,512]{1,0:T(8,128)(2,1)S(1)}, bf16[256,512]{1,0:T(8,128)(2,1)}, bf16[256,512]{1,0:T(8,128)(2,1)S(1)}, bf16[256,512]{1,0:T(8,128)(2,1)S(1)}) fusion(bf16[3,512,512]{2,1,0:T(8,128)(2,1)S(1)} %collective-permute-done.28, bf16[3,512,512]{2,1,0:T(8,128)(2,1)} %get-tuple-element.14), kind=kLoop, calls=%fused_computation.15 | loop fusion | flops 2097152 | bytes 3145728 | tf_op jit(solution)/shard_map/convert_element_type | solution.py:386
  122.2 3.2 %collective-permute-start.31 = (bf16[256,512]{1,0:T(8,128)(2,1)S(1)}, bf16[256,512]{1,0:T(8,128)(2,1)}, u32[]{:S(2)}, u32[]{:S(2)}) collective-permute-start(bf16[256,512]{1,0:T(8,128)(2,1)S(1)} %get-tuple-element.23), channel_id=1, source_target_pairs={{0,3},{1,0},{2,1},{3,2},{4,7},{5,4},{6,5},{7,6},{8,11},{9,8},{10,9... | collective-permute-start | bytes 786440 | tf_op jit(solution)/shard_map/ppermute | solution.py:68
  125.9 0.6 collective-permute-start.27
  127.3 0.7 collective-permute-start.37
  128.0 3.8 %collective-permute-done.29 = bf16[256,512]{1,0:T(8,128)(2,1)S(1)} collective-permute-done((bf16[256,512]{1,0:T(8,128)(2,1)S(1)}, bf16[256,512]{1,0:T(8,128)(2,1)S(1)}, u32[]{:S(2)}, u32[]{:S(2)}) %collective-permute-start.29) | collective-permute-done | bytes 262176 | tf_op jit(solution)/shard_map/ppermute | solution.py:68
  132.2 2.7 %collective-permute-start.33 = (bf16[256,512]{1,0:T(8,128)(2,1)}, bf16[256,512]{1,0:T(8,128)(2,1)}, u32[]{:S(2)}, u32[]{:S(2)}) collective-permute-start(bf16[256,512]{1,0:T(8,128)(2,1)} %get-tuple-element.22), channel_id=1, source_target_pairs={{0,3},{1,0},{2,1},{3,2},{4,7},{5,4},{6,5},{7,6},{8,11},{9,8},{10,9... | collective-permute-start | bytes 786440 | tf_op jit(solution)/shard_map/ppermute | solution.py:68
  134.9 2.1 %fusion = (bf16[256,512]{1,0:T(8,128)(2,1)}, bf16[256,512]{1,0:T(8,128)(2,1)}) fusion(bf16[256,512]{1,0:T(8,128)(2,1)} %collective-permute-done.31, bf16[3,512,512]{2,1,0:T(8,128)(2,1)S(1)} %collective-permute-done.28, bf16[3,512,512]{2,1,0:T(8,128)(2,1)} %get-tuple-element.14, bf16[256,512]{1,0:T(8,128)(2,1)S(1)} %collective-permute-done.29), kind=kLoop, calls=%fused_computation.5 | loop fusion | flops 1572864 | bytes 2097152 | tf_op jit(solution)/shard_map/convert_element_type | solution.py:386
  137.1 1.0 collective-permute-start.30
  138.1 2.3 %collective-permute-start.32 = (bf16[256,512]{1,0:T(8,128)(2,1)}, bf16[256,512]{1,0:T(8,128)(2,1)S(1)}, u32[]{:S(2)}, u32[]{:S(2)}) collective-permute-start(bf16[256,512]{1,0:T(8,128)(2,1)} %get-tuple-element.25), channel_id=1, source_target_pairs={{0,3},{1,0},{2,1},{3,2},{4,7},{5,4},{6,5},{7,6},{8,11},{9,8},{10,9... | collective-permute-start | bytes 786440 | tf_op jit(solution)/shard_map/ppermute | solution.py:68
  140.4 3.5 %marks.1.hot = bf16[4096,512]{1,0:T(8,128)(2,1)} custom-call(s32[1,512]{1,0:T(1,128)} %idx_hbm.1), custom_call_target="tpu_custom_call" | custom-call | tf_op jit(solution)/shard_map/marks/pallas_call | solution.py:264
  143.9 3.0 %scatter_custom_fusion = f32[4096]{0:T(1024)} fusion(s32[512]{0:T(512)S(1)} %bitcast.52, f32[512]{0:T(512)S(1)} %add_select_fusion, f32[]{:T(128)} %constant.105.clone.1), kind=kCustom, calls=%fused_computation.27 | custom fusion | bytes 16388 | tf_op jit(solution)/shard_map/scatter | solution.py:404
  147.5 3.4 %collective-permute-done.30.full_a = bf16[256,512]{1,0:T(8,128)(2,1)S(1)} collective-permute-done((bf16[256,512]{1,0:T(8,128)(2,1)}, bf16[256,512]{1,0:T(8,128)(2,1)S(1)}, u32[]{:S(2)}, u32[]{:S(2)}) %collective-permute-start.30) | collective-permute-done | bytes 262176 | tf_op jit(solution)/shard_map/ppermute | solution.py:68
  150.9 0.7 copy-done.20
  151.7 6.9 %place.1 = bf16[4096,512]{1,0:T(8,128)(2,1)} custom-call(s32[1]{0:T(128)S(6)} %copy.10.count, bf16[4096,512]{1,0:T(8,128)(2,1)} %marks.1.hot, bf16[512,512]{1,0:T(8,128)(2,1)} %get-tuple-element.12.own, bf16[512,512]{1,0:T(8,128)(2,1)} %collective-permute-done.27.other, bf16[256,512]{1,0:T(8,128)(2,1)} %copy-done.20, bf16[256,512]{1,0:T(8,128)(2,1)} %copy-done.21, ...), custom_call_target="tpu_custom_call" | custom-call | tf_op jit(solution)/shard_map/place/pallas_call | solution.py:294
  (117 shorter events, 6.4 us)
Async XLA Ops:
  0.6 2.4 %collective-permute-start.6 = (bf16[64,2048]{1,0:T(8,128)(2,1)}, bf16[64,2048]{1,0:T(8,128)(2,1)S(1)}, u32[]{:S(2)}, u32[]{:S(2)}) collective-permute-start(bf16[64,2048]{1,0:T(8,128)(2,1)} %param.13), channel_id=1, source_target_pairs={{0,4},{4,0},{8,12},{12,8},{16,20},{20,16},{24,28},{28,24},{32,36},... | collective-permute-start | bytes 786440 | tf_op jit(solution)/shard_map/ppermute | solution.py:49
  0.7 2.4 %collective-permute-start.7 = (bf16[64,2048]{1,0:T(8,128)(2,1)}, bf16[64,2048]{1,0:T(8,128)(2,1)S(1)}, u32[]{:S(2)}, u32[]{:S(2)}) collective-permute-start(bf16[64,2048]{1,0:T(8,128)(2,1)} %bitcast.50), channel_id=1, source_target_pairs={{0,4},{4,0},{8,12},{12,8},{16,20},{20,16},{24,28},{28,24},{32,36},... | collective-permute-start | bytes 786440 | tf_op jit(solution)/shard_map/ppermute | solution.py:49
  3.3 14.3 %collective-permute-start.8 = (bf16[2,128,1024]{2,1,0:T(8,128)(2,1)S(1)}, bf16[2,128,1024]{2,1,0:T(8,128)(2,1)S(1)}, u32[]{:S(2)}, u32[]{:S(2)}) collective-permute-start(bf16[2,128,1024]{2,1,0:T(8,128)(2,1)S(1)} %pad_maximum_fusion.1.refs_5_), channel_id=1, source_target_pairs={{0,32},{4,12},{8,40},{12,20},{16,48},{20,28},{24,56},{28,4},{32,64... | collective-permute-start | bytes 1572872 | tf_op jit(solution)/shard_map/ppermute | solution.py:53
  3.9 14.6 %collective-permute-start.9 = (bf16[2,128,1024]{2,1,0:T(8,128)(2,1)S(1)}, bf16[2,128,1024]{2,1,0:T(8,128)(2,1)S(1)}, u32[]{:S(2)}, u32[]{:S(2)}) collective-permute-start(bf16[2,128,1024]{2,1,0:T(8,128)(2,1)S(1)} %pad_maximum_fusion.1.refs_5_), channel_id=1, source_target_pairs={{0,96},{4,28},{8,104},{12,4},{16,112},{20,12},{24,120},{28,20},{32... | collective-permute-start | bytes 1572872 | tf_op jit(solution)/shard_map/ppermute | solution.py:53
  5.4 14.9 %collective-permute-start.12 = (bf16[2,128,1024]{2,1,0:T(8,128)(2,1)S(1)}, bf16[2,128,1024]{2,1,0:T(8,128)(2,1)}, u32[]{:S(2)}, u32[]{:S(2)}) collective-permute-start(bf16[2,128,1024]{2,1,0:T(8,128)(2,1)S(1)} %pad_maximum_fusion.1.refs_5_), channel_id=1, source_target_pairs={{0,8},{4,36},{8,16},{12,44},{16,24},{20,52},{24,0},{28,60},{32,40}... | collective-permute-start | bytes 1572872 | tf_op jit(solution)/shard_map/ppermute | solution.py:53
  5.6 29.1 %collective-permute-start = (s32[1]{0:T(128)}, s32[1]{0:T(128)}, u32[]{:S(2)}, u32[]{:S(2)}) collective-permute-start(s32[1]{0:T(128)} %param.12), channel_id=1, source_target_pairs={{0,4},{4,0},{8,12},{12,8},{16,20},{20,16},{24,28},{28,24},{32,36},... | collective-permute-start | bytes 20 | tf_op jit(solution)/shard_map/ppermute | solution.py:49
  15.2 21.1 %collective-permute-start.1 = (bf16[2,512,512]{2,1,0:T(8,128)(2,1)}, bf16[2,512,512]{2,1,0:T(8,128)(2,1)}, u32[]{:S(2)}, u32[]{:S(2)}) collective-permute-start(bf16[2,512,512]{2,1,0:T(8,128)(2,1)} %get-tuple-element.10.refs_0_), channel_id=1, source_target_pairs={{0,1},{4,7},{8,9},{12,15},{16,17},{20,23},{24,25},{28,31},{32,33},... | collective-permute-start | bytes 3145736 | tf_op jit(solution)/shard_map/ppermute | solution.py:64
  17.6 13.2 %collective-permute-start.13 = (bf16[2,128,1024]{2,1,0:T(8,128)(2,1)S(1)}, bf16[2,128,1024]{2,1,0:T(8,128)(2,1)S(1)}, u32[]{:S(2)}, u32[]{:S(2)}) collective-permute-start(bf16[2,128,1024]{2,1,0:T(8,128)(2,1)S(1)} %pad_maximum_fusion.1.refs_5_), channel_id=1, source_target_pairs={{0,24},{4,100},{8,0},{12,108},{16,8},{20,116},{24,16},{28,124},{32... | collective-permute-start | bytes 1572872 | tf_op jit(solution)/shard_map/ppermute | solution.py:53
  18.5 16.3 %copy-start.4 = (bf16[2,128,1024]{2,1,0:T(8,128)(2,1)}, bf16[2,128,1024]{2,1,0:T(8,128)(2,1)S(1)}, u32[]{:S(2)}) copy-start(bf16[2,128,1024]{2,1,0:T(8,128)(2,1)S(1)} %collective-permute-done.9.refs_7_) | copy-start | bytes 1572868
  18.5 16.3 %copy-start.11 = (bf16[2,512,512]{2,1,0:T(8,128)(2,1)S(1)}, bf16[2,512,512]{2,1,0:T(8,128)(2,1)}, u32[]{:S(2)}) copy-start(bf16[2,512,512]{2,1,0:T(8,128)(2,1)} %get-tuple-element.10.refs_0_) | copy-start | bytes 3145732
  18.5 14.1 %collective-permute-start.10 = (bf16[128,1024]{1,0:T(8,128)(2,1)S(1)}, bf16[128,1024]{1,0:T(8,128)(2,1)S(1)}, u32[]{:S(2)}, u32[]{:S(2)}) collective-permute-start(bf16[128,1024]{1,0:T(8,128)(2,1)S(1)} %get-tuple-element.28), channel_id=1, source_target_pairs={{0,32},{4,12},{8,40},{12,20},{16,48},{20,28},{24,56},{28,4},{32,64... | collective-permute-start | bytes 786440 | tf_op jit(solution)/shard_map/ppermute | solution.py:53
  20.3 12.3 %collective-permute-start.11 = (bf16[128,1024]{1,0:T(8,128)(2,1)S(1)}, bf16[128,1024]{1,0:T(8,128)(2,1)S(1)}, u32[]{:S(2)}, u32[]{:S(2)}) collective-permute-start(bf16[128,1024]{1,0:T(8,128)(2,1)S(1)} %get-tuple-element.31), channel_id=1, source_target_pairs={{0,96},{4,28},{8,104},{12,4},{16,112},{20,12},{24,120},{28,20},{32... | collective-permute-start | bytes 786440 | tf_op jit(solution)/shard_map/ppermute | solution.py:53
  30.8 4.0 %collective-permute-start.26 = (f32[512,1]{1,0:T(8,128)S(1)}, f32[512,1]{1,0:T(8,128)}, u32[]{:S(2)}, u32[]{:S(2)}) collective-permute-start(f32[512,1]{1,0:T(8,128)S(1)} %copy-done.16), channel_id=1, source_target_pairs={{0,4},{4,0},{8,12},{12,8},{16,20},{20,16},{24,28},{28,24},{32,36},... | collective-permute-start | bytes 6152 | tf_op jit(solution)/shard_map/ppermute | solution.py:49
  32.6 6.4 %collective-permute-start.18 = (bf16[128,1024]{1,0:T(8,128)(2,1)S(1)}, bf16[128,1024]{1,0:T(8,128)(2,1)S(1)}, u32[]{:S(2)}, u32[]{:S(2)}) collective-permute-start(bf16[128,1024]{1,0:T(8,128)(2,1)S(1)} %slice_bitcast_fusion.3), channel_id=1, source_target_pairs={{0,8},{4,36},{8,16},{12,44},{16,24},{20,52},{24,0},{28,60},{32,40}... | collective-permute-start | bytes 786440 | tf_op jit(solution)/shard_map/ppermute | solution.py:53
  32.7 7.7 %collective-permute-start.21 = (bf16[128,1024]{1,0:T(8,128)(2,1)S(1)}, bf16[128,1024]{1,0:T(8,128)(2,1)S(1)}, u32[]{:S(2)}, u32[]{:S(2)}) collective-permute-start(bf16[128,1024]{1,0:T(8,128)(2,1)S(1)} %slice_bitcast_fusion.1), channel_id=1, source_target_pairs={{0,24},{4,100},{8,0},{12,108},{16,8},{20,116},{24,16},{28,124},{32... | collective-permute-start | bytes 786440 | tf_op jit(solution)/shard_map/ppermute | solution.py:53
  34.8 11.0 %collective-permute-start.2 = (bf16[2,512,512]{2,1,0:T(8,128)(2,1)S(1)}, bf16[2,512,512]{2,1,0:T(8,128)(2,1)}, u32[]{:S(2)}, u32[]{:S(2)}) collective-permute-start(bf16[2,512,512]{2,1,0:T(8,128)(2,1)S(1)} %copy-done.11), channel_id=1, source_target_pairs={{0,4},{4,0},{8,12},{12,8},{16,20},{20,16},{24,28},{28,24},{32,36},... | collective-permute-start | bytes 3145736 | tf_op jit(solution)/shard_map/ppermute | solution.py:49
  34.9 9.7 %collective-permute-start.16 = (bf16[2,128,1024]{2,1,0:T(8,128)(2,1)S(1)}, bf16[2,128,1024]{2,1,0:T(8,128)(2,1)S(1)}, u32[]{:S(2)}, u32[]{:S(2)}) collective-permute-start(bf16[2,128,1024]{2,1,0:T(8,128)(2,1)S(1)} %pad_maximum_fusion.2), channel_id=1, source_target_pairs={{0,8},{4,36},{8,16},{12,44},{16,24},{20,52},{24,0},{28,60},{32,40}... | collective-permute-start | bytes 1572872 | tf_op jit(solution)/shard_map/ppermute | solution.py:53
  36.2 25.7 %collective-permute-start.5 = (bf16[2,512,512]{2,1,0:T(8,128)(2,1)}, bf16[2,512,512]{2,1,0:T(8,128)(2,1)}, u32[]{:S(2)}, u32[]{:S(2)}) collective-permute-start(bf16[2,512,512]{2,1,0:T(8,128)(2,1)} %collective-permute-done.1.refs_1_), channel_id=1, source_target_pairs={{0,1},{4,7},{8,9},{12,15},{16,17},{20,23},{24,25},{28,31},{32,33},... | collective-permute-start | bytes 3145736 | tf_op jit(solution)/shard_map/ppermute | solution.py:64
  36.3 30.3 %copy-start.23 = (s32[4]{0:T(128)S(1)}, s32[4]{0:T(128)}, u32[]{:S(2)}) copy-start(s32[4]{0:T(128)} %constant.108.clone) | copy-start | bytes 52
  36.4 36.8 %copy-start.24 = (s32[4]{0:T(128)S(1)}, s32[4]{0:T(128)}, u32[]{:S(2)}) copy-start(s32[4]{0:T(128)} %constant.100.clone.1) | copy-start | bytes 52
  39.0 25.4 %copy-start.12 = (bf16[128,1024]{1,0:T(8,128)(2,1)}, bf16[128,1024]{1,0:T(8,128)(2,1)S(1)}, u32[]{:S(2)}) copy-start(bf16[128,1024]{1,0:T(8,128)(2,1)S(1)} %collective-permute-done.18.refs_16_) | copy-start | bytes 786436
  39.0 25.4 %collective-permute-start.14 = (bf16[4,128,1024]{2,1,0:T(8,128)(2,1)S(1)}, bf16[4,128,1024]{2,1,0:T(8,128)(2,1)S(1)}, u32[]{:S(2)}, u32[]{:S(2)}) collective-permute-start(bf16[4,128,1024]{2,1,0:T(8,128)(2,1)S(1)} %pad_maximum_fusion), channel_id=1, source_target_pairs={{0,8},{4,36},{8,16},{12,44},{16,24},{20,52},{24,0},{28,60},{32,40}... | collective-permute-start | bytes 3145736 | tf_op jit(solution)/shard_map/ppermute | solution.py:53
  40.3 24.1 %copy-start.13 = (bf16[128,1024]{1,0:T(8,128)(2,1)}, bf16[128,1024]{1,0:T(8,128)(2,1)S(1)}, u32[]{:S(2)}) copy-start(bf16[128,1024]{1,0:T(8,128)(2,1)S(1)} %collective-permute-done.21.refs_19_) | copy-start | bytes 786436
  40.3 24.1 %collective-permute-start.15 = (bf16[4,128,1024]{2,1,0:T(8,128)(2,1)S(1)}, bf16[4,128,1024]{2,1,0:T(8,128)(2,1)S(1)}, u32[]{:S(2)}, u32[]{:S(2)}) collective-permute-start(bf16[4,128,1024]{2,1,0:T(8,128)(2,1)S(1)} %pad_maximum_fusion), channel_id=1, source_target_pairs={{0,24},{4,100},{8,0},{12,108},{16,8},{20,116},{24,16},{28,124},{32... | collective-permute-start | bytes 3145736 | tf_op jit(solution)/shard_map/ppermute | solution.py:53
  44.6 23.8 %copy-start.6 = (bf16[2,128,1024]{2,1,0:T(8,128)(2,1)}, bf16[2,128,1024]{2,1,0:T(8,128)(2,1)S(1)}, u32[]{:S(2)}) copy-start(bf16[2,128,1024]{2,1,0:T(8,128)(2,1)S(1)} %collective-permute-done.16.refs_14_) | copy-start | bytes 1572868
  44.6 17.3 %collective-permute-start.17 = (bf16[2,128,1024]{2,1,0:T(8,128)(2,1)S(1)}, bf16[2,128,1024]{2,1,0:T(8,128)(2,1)S(1)}, u32[]{:S(2)}, u32[]{:S(2)}) collective-permute-start(bf16[2,128,1024]{2,1,0:T(8,128)(2,1)S(1)} %pad_maximum_fusion.2), channel_id=1, source_target_pairs={{0,24},{4,100},{8,0},{12,108},{16,8},{20,116},{24,16},{28,124},{32... | collective-permute-start | bytes 1572872 | tf_op jit(solution)/shard_map/ppermute | solution.py:53
  45.8 28.8 %collective-permute-start.24 = (bf16[2,512,512]{2,1,0:T(8,128)(2,1)}, bf16[2,512,512]{2,1,0:T(8,128)(2,1)}, u32[]{:S(2)}, u32[]{:S(2)}) collective-permute-start(bf16[2,512,512]{2,1,0:T(8,128)(2,1)} %collective-permute-done.1.refs_1_), channel_id=1, source_target_pairs={{0,4},{4,0},{8,12},{12,8},{16,20},{20,16},{24,28},{28,24},{32,36},... | collective-permute-start | bytes 3145736 | tf_op jit(solution)/shard_map/ppermute | solution.py:49
  61.9 16.3 %collective-permute-start.3 = (bf16[2,512,512]{2,1,0:T(8,128)(2,1)}, bf16[2,512,512]{2,1,0:T(8,128)(2,1)}, u32[]{:S(2)}, u32[]{:S(2)}) collective-permute-start(bf16[2,512,512]{2,1,0:T(8,128)(2,1)} %collective-permute-done.2.refs_0_), channel_id=1, source_target_pairs={{0,1},{4,7},{8,9},{12,15},{16,17},{20,23},{24,25},{28,31},{32,33},... | collective-permute-start | bytes 3145736 | tf_op jit(solution)/shard_map/ppermute | solution.py:64
  62.0 21.1 %collective-permute-start.25 = (bf16[2,512,512]{2,1,0:T(8,128)(2,1)}, bf16[2,512,512]{2,1,0:T(8,128)(2,1)}, u32[]{:S(2)}, u32[]{:S(2)}) collective-permute-start(bf16[2,512,512]{2,1,0:T(8,128)(2,1)} %collective-permute-done.5.refs_3_), channel_id=1, source_target_pairs={{0,4},{4,0},{8,12},{12,8},{16,20},{20,16},{24,28},{28,24},{32,36},... | collective-permute-start | bytes 3145736 | tf_op jit(solution)/shard_map/ppermute | solution.py:49
  64.4 18.6 %copy-start = (bf16[4,128,1024]{2,1,0:T(8,128)(2,1)}, bf16[4,128,1024]{2,1,0:T(8,128)(2,1)S(1)}, u32[]{:S(2)}) copy-start(bf16[4,128,1024]{2,1,0:T(8,128)(2,1)S(1)} %collective-permute-done.14.refs_12_) | copy-start | bytes 3145732
  64.4 6.6 %collective-permute-start.20 = (bf16[128,1024]{1,0:T(8,128)(2,1)}, bf16[128,1024]{1,0:T(8,128)(2,1)S(1)}, u32[]{:S(2)}, u32[]{:S(2)}) collective-permute-start(bf16[128,1024]{1,0:T(8,128)(2,1)} %slice_bitcast_fusion.2), channel_id=1, source_target_pairs={{0,8},{4,36},{8,16},{12,44},{16,24},{20,52},{24,0},{28,60},{32,40}... | collective-permute-start | bytes 786440 | tf_op jit(solution)/shard_map/ppermute | solution.py:53
  64.5 7.9 %collective-permute-start.23 = (bf16[128,1024]{1,0:T(8,128)(2,1)}, bf16[128,1024]{1,0:T(8,128)(2,1)S(1)}, u32[]{:S(2)}, u32[]{:S(2)}) collective-permute-start(bf16[128,1024]{1,0:T(8,128)(2,1)} %slice_bitcast_fusion), channel_id=1, source_target_pairs={{0,24},{4,100},{8,0},{12,108},{16,8},{20,116},{24,16},{28,124},{32... | collective-permute-start | bytes 786440 | tf_op jit(solution)/shard_map/ppermute | solution.py:53
  71.0 9.4 %collective-permute-start.19 = (bf16[2,128,1024]{2,1,0:T(8,128)(2,1)}, bf16[2,128,1024]{2,1,0:T(8,128)(2,1)S(1)}, u32[]{:S(2)}, u32[]{:S(2)}) collective-permute-start(bf16[2,128,1024]{2,1,0:T(8,128)(2,1)} %slice.95), channel_id=1, source_target_pairs={{0,8},{4,36},{8,16},{12,44},{16,24},{20,52},{24,0},{28,60},{32,40}... | collective-permute-start | bytes 1572872 | tf_op jit(solution)/shard_map/ppermute | solution.py:53
  72.3 10.7 %collective-permute-start.22 = (bf16[2,128,1024]{2,1,0:T(8,128)(2,1)}, bf16[2,128,1024]{2,1,0:T(8,128)(2,1)}, u32[]{:S(2)}, u32[]{:S(2)}) collective-permute-start(bf16[2,128,1024]{2,1,0:T(8,128)(2,1)} %slice.98), channel_id=1, source_target_pairs={{0,24},{4,100},{8,0},{12,108},{16,8},{20,116},{24,16},{28,124},{32... | collective-permute-start | bytes 1572872 | tf_op jit(solution)/shard_map/ppermute | solution.py:53
  98.9 21.1 %collective-permute-start.28 = (bf16[3,512,512]{2,1,0:T(8,128)(2,1)}, bf16[3,512,512]{2,1,0:T(8,128)(2,1)S(1)}, u32[]{:S(2)}, u32[]{:S(2)}) collective-permute-start(bf16[3,512,512]{2,1,0:T(8,128)(2,1)} %get-tuple-element.15), channel_id=1, source_target_pairs={{0,4},{4,0},{8,12},{12,8},{16,20},{20,16},{24,28},{28,24},{32,36},... | collective-permute-start | bytes 4718600 | tf_op jit(solution)/shard_map/ppermute | solution.py:49
  99.0 5.2 %collective-permute-start.4 = (bf16[2,512,512]{2,1,0:T(8,128)(2,1)}, bf16[2,512,512]{2,1,0:T(8,128)(2,1)}, u32[]{:S(2)}, u32[]{:S(2)}) collective-permute-start(bf16[2,512,512]{2,1,0:T(8,128)(2,1)} %collective-permute-done.3.refs_1_), channel_id=1, source_target_pairs={{0,4},{4,0},{8,12},{12,8},{16,20},{20,16},{24,28},{28,24},{32,36},... | collective-permute-start | bytes 3145736 | tf_op jit(solution)/shard_map/ppermute | solution.py:49
  122.2 18.2 %copy-start.22 = (s32[1,512]{1,0:T(1,128)S(1)}, s32[1,512]{1,0:T(1,128)}, u32[]{:S(2)}) copy-start(s32[1,512]{1,0:T(1,128)} %idx_hbm.1) | copy-start | bytes 6148
  122.2 9.6 %collective-permute-start.29 = (bf16[256,512]{1,0:T(8,128)(2,1)S(1)}, bf16[256,512]{1,0:T(8,128)(2,1)S(1)}, u32[]{:S(2)}, u32[]{:S(2)}) collective-permute-start(bf16[256,512]{1,0:T(8,128)(2,1)S(1)} %get-tuple-element.24), channel_id=1, source_target_pairs={{0,1},{1,2},{2,3},{3,0},{4,5},{5,6},{6,7},{7,4},{8,9},{9,10},{10,1... | collective-permute-start | bytes 786440 | tf_op jit(solution)/shard_map/ppermute | solution.py:68
  122.2 10.0 %collective-permute-start.31 = (bf16[256,512]{1,0:T(8,128)(2,1)S(1)}, bf16[256,512]{1,0:T(8,128)(2,1)}, u32[]{:S(2)}, u32[]{:S(2)}) collective-permute-start(bf16[256,512]{1,0:T(8,128)(2,1)S(1)} %get-tuple-element.23), channel_id=1, source_target_pairs={{0,3},{1,0},{2,1},{3,2},{4,7},{5,4},{6,5},{7,6},{8,11},{9,8},{10,9... | collective-permute-start | bytes 786440 | tf_op jit(solution)/shard_map/ppermute | solution.py:68
  125.6 1.2 collective-permute-start.35
  125.9 21.1 %collective-permute-start.27 = (bf16[512,512]{1,0:T(8,128)(2,1)}, bf16[512,512]{1,0:T(8,128)(2,1)}, u32[]{:S(2)}, u32[]{:S(2)}) collective-permute-start(bf16[512,512]{1,0:T(8,128)(2,1)} %get-tuple-element.13), channel_id=1, source_target_pairs={{0,4},{4,0},{8,12},{12,8},{16,20},{20,16},{24,28},{28,24},{32,36},... | collective-permute-start | bytes 1572872 | tf_op jit(solution)/shard_map/ppermute | solution.py:49
  126.9 10.2 %collective-permute-start.36 = (f32[512]{0:T(512)S(1)}, f32[512]{0:T(512)S(1)}, u32[]{:S(2)}, u32[]{:S(2)}) collective-permute-start(f32[512]{0:T(512)S(1)} %add.174), channel_id=1, source_target_pairs={{0,2},{1,3},{2,0},{3,1},{4,6},{5,7},{6,4},{7,5},{8,10},{9,11},{10,... | collective-permute-start | bytes 6152 | tf_op jit(solution)/shard_map/ppermute | solution.py:68
  127.3 9.8 %collective-permute-start.37 = (f32[512]{0:T(512)S(1)}, f32[512]{0:T(512)S(1)}, u32[]{:S(2)}, u32[]{:S(2)}) collective-permute-start(f32[512]{0:T(512)S(1)} %add.174), channel_id=1, source_target_pairs={{0,1},{1,2},{2,3},{3,0},{4,5},{5,6},{6,7},{7,4},{8,9},{9,10},{10,1... | collective-permute-start | bytes 6152 | tf_op jit(solution)/shard_map/ppermute | solution.py:68
  131.9 6.2 %collective-permute-start.38 = (f32[512]{0:T(512)S(1)}, f32[512]{0:T(512)S(1)}, u32[]{:S(2)}, u32[]{:S(2)}) collective-permute-start(f32[512]{0:T(512)S(1)} %add.174), channel_id=1, source_target_pairs={{0,3},{1,0},{2,1},{3,2},{4,7},{5,4},{6,5},{7,6},{8,11},{9,8},{10,9... | collective-permute-start | bytes 6152 | tf_op jit(solution)/shard_map/ppermute | solution.py:68
  132.2 14.7 %collective-permute-start.33 = (bf16[256,512]{1,0:T(8,128)(2,1)}, bf16[256,512]{1,0:T(8,128)(2,1)}, u32[]{:S(2)}, u32[]{:S(2)}) collective-permute-start(bf16[256,512]{1,0:T(8,128)(2,1)} %get-tuple-element.22), channel_id=1, source_target_pairs={{0,3},{1,0},{2,1},{3,2},{4,7},{5,4},{6,5},{7,6},{8,11},{9,8},{10,9... | collective-permute-start | bytes 786440 | tf_op jit(solution)/shard_map/ppermute | solution.py:68
  137.1 10.4 %collective-permute-start.34 = (bf16[256,512]{1,0:T(8,128)(2,1)S(1)}, bf16[256,512]{1,0:T(8,128)(2,1)S(1)}, u32[]{:S(2)}, u32[]{:S(2)}) collective-permute-start(bf16[256,512]{1,0:T(8,128)(2,1)S(1)} %get-tuple-element.21), channel_id=1, source_target_pairs={{0,1},{1,2},{2,3},{3,0},{4,5},{5,6},{6,7},{7,4},{8,9},{9,10},{10,1... | collective-permute-start | bytes 786440 | tf_op jit(solution)/shard_map/ppermute | solution.py:68
  137.1 13.8 %collective-permute-start.30 = (bf16[256,512]{1,0:T(8,128)(2,1)}, bf16[256,512]{1,0:T(8,128)(2,1)S(1)}, u32[]{:S(2)}, u32[]{:S(2)}) collective-permute-start(bf16[256,512]{1,0:T(8,128)(2,1)} %get-tuple-element.26), channel_id=1, source_target_pairs={{0,1},{1,2},{2,3},{3,0},{4,5},{5,6},{6,7},{7,4},{8,9},{9,10},{10,1... | collective-permute-start | bytes 786440 | tf_op jit(solution)/shard_map/ppermute | solution.py:68
  138.1 12.8 %collective-permute-start.32 = (bf16[256,512]{1,0:T(8,128)(2,1)}, bf16[256,512]{1,0:T(8,128)(2,1)S(1)}, u32[]{:S(2)}, u32[]{:S(2)}) collective-permute-start(bf16[256,512]{1,0:T(8,128)(2,1)} %get-tuple-element.25), channel_id=1, source_target_pairs={{0,3},{1,0},{2,1},{3,2},{4,7},{5,4},{6,5},{7,6},{8,11},{9,8},{10,9... | collective-permute-start | bytes 786440 | tf_op jit(solution)/shard_map/ppermute | solution.py:68
  (16 other events, 88.6 us)

commit v2 on v1

v2 whole, which is shorter than its diff:
```python
import functools

import jax
import jax.numpy as jnp
from jax import lax
from jax.experimental import pallas as pl
from jax.experimental.pallas import tpu as pltpu
from jax.sharding import PartitionSpec as P


BLK = 128
SIDE = 4
CHIPS = SIDE * SIDE

gelu_coeff = 0.7978845608028654
cubic_coeff = 0.044715

RELS = (0, -1, 1, 2)


def gelu_pair(values):
    square = values * values
    inner = values * (gelu_coeff + gelu_coeff * cubic_coeff * square)
    h = 0.5 * jnp.tanh(inner) + 0.5
    forward = values * h
    bend = values * (2.0 * gelu_coeff + 6.0 * gelu_coeff * cubic_coeff * square)
    slope = h + h * ((1.0 - h) * bend)
    return (forward, slope)


def seq_pairs(target):
    pairs = []
    for x in range(SIDE):
        for y in range(SIDE):
            for c in range(2):
                tx, ty, tc = target(x, y, c)
                pairs.append((((x * SIDE) + y) * 2 + c, ((tx % SIDE) * SIDE + ty % SIDE) * 2 + tc))
    return pairs


def ring(step, phase):
    return seq_pairs(lambda x, y, c: (x + step, y, c) if (c == phase) else (x, y + step, c))


SWAP = seq_pairs(lambda x, y, c: (x, y, 1 - c))


def swap(value):
    return lax.ppermute(value, "seq", SWAP)


def hop(value, step, phase):
    return lax.ppermute(value, "seq", ring(step, phase))


ZPAIRS = []
for z_at in range(SIDE):
    for s_at in range(2 * CHIPS):
        to = (z_at + (1 if s_at % 2 == 0 else -1)) % SIDE
        ZPAIRS.append((s_at * SIDE + z_at, s_at * SIDE + to))


def zdir(value):
    return lax.ppermute(value, ("seq", "tensor"), ZPAIRS)


def zhop(value, step):
    return lax.ppermute(value, "tensor", [(i, (i + step) % SIDE) for i in range(SIDE)])


TILE = 256
ROWS = 512
TOK = 4096
DOT = functools.partial(lax.dot_general, preferred_element_type=jnp.float32)
NN = (((1,), (0,)), ((), ()))
NT = (((1,), (1,)), ((), ()))
ANY = pl.BlockSpec(memory_space=pl.ANY)
HBM = pl.BlockSpec(memory_space=pltpu.MemorySpace.HBM)


def params(mib):
    return pltpu.CompilerParams(vmem_limit_bytes=mib << 20)


VMEM = pl.BlockSpec(memory_space=pltpu.MemorySpace.VMEM)
SMEM = pl.BlockSpec(memory_space=pltpu.MemorySpace.SMEM)


def on_chip(value):
    return pltpu.with_memory_space_constraint(value, pltpu.MemorySpace.VMEM)


def off_chip(value):
    return pltpu.with_memory_space_constraint(value, pltpu.MemorySpace.HBM)


def whole(shape):
    return pl.BlockSpec(shape, lambda m, meta: (0,) * len(shape))


def pick_kernel(count, idx_hbm, score_hbm, x_hbm, g_hbm, out, s_out, idx, score, xv, gv, hot, sems):
    small = [
        pltpu.make_async_copy(idx_hbm, idx, sems.at[2]),
        pltpu.make_async_copy(score_hbm, score, sems.at[3]),
    ]
    copies = [
        pltpu.make_async_copy(x_hbm, xv, sems.at[0]),
        pltpu.make_async_copy(g_hbm, gv, sems.at[1]),
    ]
    for copy in small + copies:
        copy.start()
    for copy in small:
        copy.wait()
    column = jnp.broadcast_to(idx[...], (BLK, ROWS)).T
    for r in range(ROWS // BLK):

        @pl.when(r < count[0])
        def _(r=r):
            at = jnp.broadcast_to(column[r * BLK : (r + 1) * BLK, :1], (BLK, TOK))
            same = lax.broadcasted_iota(jnp.int32, (BLK, TOK), 1) == at
            hot[r * BLK : (r + 1) * BLK, :] = jnp.where(same, 1.0, 0.0).astype(jnp.bfloat16)
            s_out[r * BLK : (r + 1) * BLK, :] = jnp.sum(
                jnp.where(same, score[...], 0.0), axis=1, keepdims=True
            )

    for k, (copy, rows) in enumerate(zip(copies, (xv, gv))):
        copy.wait()

        @pl.when(count[0] <= 2)
        def _(k=k, rows=rows):
            at = pl.ds(0, TILE)
            out[k, at, :] = DOT(hot[at, :], rows[...], NN).astype(jnp.bfloat16)

        @pl.when(count[0] > 2)
        def _(k=k, rows=rows):
            out[k] = DOT(hot[...], rows[...], NN).astype(jnp.bfloat16)


def pick(count, idx, score, inputs, out_grad):
    return pl.pallas_call(
        pick_kernel,
        grid_spec=pltpu.PrefetchScalarGridSpec(
            num_scalar_prefetch=1,
            grid=(1,),
            in_specs=[HBM] * 4,
            out_specs=[whole((2, ROWS, 512)), whole((ROWS, 1))],
            scratch_shapes=[
                pltpu.VMEM((1, ROWS), jnp.int32),
                pltpu.VMEM((1, TOK), jnp.float32),
                pltpu.VMEM((TOK, 512), jnp.bfloat16),
                pltpu.VMEM((TOK, 512), jnp.bfloat16),
                pltpu.VMEM((ROWS, TOK), jnp.bfloat16),
                pltpu.SemaphoreType.DMA((4,)),
            ],
        ),
        out_shape=[
            jax.ShapeDtypeStruct((2, ROWS, 512), jnp.bfloat16),
            jax.ShapeDtypeStruct((ROWS, 1), jnp.float32),
        ],
        compiler_params=params(18),
        name="pick",
    )(count, idx, score, inputs, out_grad)


def positions():
    seq, z = lax.axis_index("seq"), lax.axis_index("tensor")
    c, y, x = seq & 1, (seq >> 1) & 3, seq >> 3
    quarters, blocks, turns = [], [], []
    for k in range(CHIPS):
        first, second = RELS[k % SIDE], RELS[k // SIDE]
        px = (x + jnp.where(c == 0, first, second) + SIDE) & 3
        rel = (px - z + SIDE) & 3
        turn = jnp.where(rel == 0, 3, jnp.where(rel == 1, 1, jnp.where(rel == 2, 0, 2)))
        quarters.append(px)
        blocks.append((y + jnp.where(c == 0, second, first) + SIDE) & 3)
        turns.append(turn)
    near = jnp.where(c == 0, 3, 1)
    return quarters, blocks, turns, (z, (z + near) & 3, (z - near + SIDE) & 3, (z + 2) & 3)


def half_kernel(count, *refs):
    rows, scale_ref = refs[:4], refs[4]
    quarters, blocks, turns, came = positions()
    (sw, p_f, p_b, h_in, h_out, y0f, y0b, yrf, yrb, yhf, yhb) = refs[5:16]
    last = (refs[16:19], refs[19:22])
    out, score, rv, hg = refs[22:]

    lines = []
    for w in range(2):
        line = [sw.at[w], p_f.at[w], p_b.at[w], (h_in, h_out)[w]]
        for y0, yr, yh in ((y0f, yrf, yhf), (y0b, yrb, yhb)):
            line += [y0.at[w], yr.at[2 * w], yr.at[2 * w + 1], yh.at[w]]
        lines.append(line + [last[w][0], last[w][1].at[0], last[w][1].at[1], last[w][2]])

    def weights(w, cols):
        return jnp.concatenate([piece[:, cols] for piece in lines[w]], axis=0)

    def columns(which):
        parts = []
        for k in range(CHIPS):
            lanes = pl.ds(pl.multiple_of(blocks[k] * BLK, BLK), BLK)
            parts.append(rv[which, quarters[k], :, lanes])
        return jnp.concatenate(parts, axis=1)

    @pl.loop(0, (count[0] + 1) // 2)
    def _(tile):
        at = pl.ds(pl.multiple_of(tile * TILE, TILE), TILE)
        for r in range(SIDE):
            rv[:, came[r]] = rows[r][:, at, :]
        xs, gs, scale = columns(0), columns(1), scale_ref[at, :]
        total = None
        for n in range(4):
            cols = pl.ds(n * 256, 256)
            hidden = DOT(xs, weights(0, cols), NN)
            upstream = DOT(gs, weights(1, cols), NN)
            forward, slope = gelu_pair(hidden)
            active = forward.astype(jnp.bfloat16).astype(jnp.float32)
            term = jnp.sum(upstream * active, axis=1, keepdims=True)
            total = term if total is None else total + term
            hg[:, cols] = (scale * upstream * slope).astype(jnp.bfloat16)
        score[:, at] = jnp.broadcast_to(total, (TILE, BLK)).T[:1]
        for k in range(0, CHIPS, 2):
            pair = jnp.concatenate([lines[0][k][...], lines[0][k + 1][...]], axis=0)
            result = DOT(hg[...], pair, NT).astype(jnp.bfloat16)
            for i in range(2):
                lanes = pl.ds(pl.multiple_of(blocks[k + i] * BLK, BLK), BLK)
                out[turns[k + i], at, lanes] = result[:, i * BLK : (i + 1) * BLK]


def half_stage(count, rows, s, pieces):
    return pl.pallas_call(
        half_kernel,
        in_specs=[SMEM] + [VMEM] * 22,
        out_specs=[VMEM, VMEM],
        scratch_shapes=[
            pltpu.VMEM((2, SIDE, TILE, 512), jnp.bfloat16),
            pltpu.VMEM((TILE, 1024), jnp.bfloat16),
        ],
        out_shape=[
            pltpu.VMEM((SIDE, ROWS, 512), jnp.bfloat16),
            pltpu.VMEM((1, ROWS), jnp.float32),
        ],
        compiler_params=params(12),
        name="half_stage",
    )(count, *[on_chip(v) for v in (*rows, s, *pieces)])


def marks_kernel(count, idx, scores, out, score_out):
    lane = lax.broadcasted_iota(jnp.int32, (1, ROWS), 1)
    value = jnp.where(lane < count[0] * BLK, scores[...], 0.0)
    terms = []
    for _ in range(3):
        terms.append(value.astype(jnp.bfloat16))
        value = value - terms[-1].astype(jnp.float32)
    terms = jnp.concatenate(
        [jnp.broadcast_to(term.astype(jnp.float32), (8, ROWS)) for term in terms], axis=0
    ).astype(jnp.bfloat16)
    for t in range(TOK // ROWS):
        here = pl.ds(t * ROWS, ROWS)
        token = lax.broadcasted_iota(jnp.int32, (ROWS, ROWS), 0) + t * ROWS
        hot = jnp.where(token == jnp.broadcast_to(idx[...], (ROWS, ROWS)), 1.0, 0.0)
        hot = hot.astype(jnp.bfloat16)
        out[here, :] = hot
        found = DOT(terms, hot, NT)
        score_out[:, here] = found[:1] + found[8:9] + found[16:17]


def marks(count, idx, scores):
    return pl.pallas_call(
        marks_kernel,
        in_specs=[SMEM, VMEM, VMEM],
        out_specs=[VMEM, VMEM],
        out_shape=[
            pltpu.VMEM((TOK, ROWS), jnp.bfloat16),
            jax.ShapeDtypeStruct((1, TOK), jnp.float32),
        ],
        compiler_params=params(8),
        name="marks",
    )(count, idx, scores)


def place_kernel(count, hot, own, other, full_a, full_b, low_a, low_b, out, rows, done, sems):
    mid = ROWS // 2
    for at, parts in ((0, (full_a, low_a)), (mid, (full_b, low_b))):
        here = pl.ds(at, mid)
        total = own[3, here, :].astype(jnp.float32) + other[3, here, :].astype(jnp.float32)
        for part in parts:
            total = total + part[...].astype(jnp.float32)
        at_row = lax.broadcasted_iota(jnp.int32, (mid, 512), 0) + at
        total = jnp.where(at_row < count[0] * BLK, total, 0.0)
        rows[here, :] = total.astype(jnp.bfloat16)
    copies = []
    for t in range(TOK // ROWS):
        here = pl.ds(t * ROWS, ROWS)
        done[here, :] = DOT(hot[here, :], rows[...], NN).astype(jnp.bfloat16)
        copies.append(pltpu.make_async_copy(done.at[here], out.at[here], sems.at[t]))
        copies[-1].start()
    for copy in copies:
        copy.wait()


def place(count, hot, own, other, full_a, full_b, low_a, low_b):
    held = [on_chip(v) for v in (hot, own, other, full_a, full_b, low_a, low_b)]
    return pl.pallas_call(
        place_kernel,
        in_specs=[SMEM] + [VMEM] * 7,
        out_specs=HBM,
        scratch_shapes=[
            pltpu.VMEM((ROWS, 512), jnp.bfloat16),
            pltpu.VMEM((TOK, 512), jnp.bfloat16),
            pltpu.SemaphoreType.DMA((TOK // ROWS,)),
        ],
        out_shape=jax.ShapeDtypeStruct((TOK, 512), jnp.bfloat16),
        compiler_params=params(12),
        name="place",
    )(count, *held)


def branch(inputs, out_grad, router_score, route_index, block_count, w_in, w_out):
    seq = lax.axis_index("seq")
    c = seq % 2

    w_out_t = w_out.T
    half = w_in.shape[1] // 2
    other_in, other_out = swap(w_in), swap(w_out_t)
    par_count = swap(block_count)

    xg, s_own = pick(
        block_count,
        *[off_chip(v) for v in (route_index, router_score[None, :], inputs, out_grad)],
    )
    z_own = zdir(xg)
    xg_par = swap(xg)
    s_par = swap(s_own)
    z_par = zdir(xg_par)
    z_two = zdir(z_own)
    far_par = swap(z_own)
    far_own = swap(z_par)
    two_par = swap(z_two)
    own_rows = (xg, z_own, far_own, z_two)
    par_rows = (xg_par, z_par, far_par, two_par)

    def cut(w):
        return lax.dynamic_slice_in_dim(w, c * half, half, axis=1)

    def joined(w, other):
        a, b = cut(w), cut(other)
        return jnp.where(c == 0, jnp.concatenate([a, b], 0), jnp.concatenate([b, a], 0))

    s = jnp.stack([joined(w_in, other_in), joined(w_out_t, other_out)])
    p_f, p_b = hop(s, 1, 0), hop(s, -1, 0)
    y0f, y0b = hop(s, 1, 1), hop(s, -1, 1)
    h_in, h_out = hop(p_f[0], 1, 0), hop(p_b[1], -1, 0)
    r = jnp.concatenate([p_f[:1], p_b[:1], p_f[1:], p_b[1:]], 0)
    yrf, yrb = hop(r, 1, 1), hop(r, -1, 1)
    h = jnp.stack([h_in, h_out])
    yhf, yhb = hop(h, 1, 1), hop(h, -1, 1)
    a_in, a_out = hop(y0f[0], 1, 1), hop(y0b[1], -1, 1)
    r_in, r_out = hop(yrf[:2], 1, 1), hop(yrb[2:], -1, 1)
    low, high = yhf[0], yhb[1]
    b_in, b_out = hop(low, 1, 1), hop(high, -1, 1)

    pieces = (s, p_f, p_b, h_in, h_out, y0f, y0b, yrf, yrb, yhf, yhb)
    pieces = pieces + (a_in, r_in, b_in, a_out, r_out, b_out)
    o_par, score_par = half_stage(par_count, par_rows, s_par, pieces)
    other = swap(o_par)
    score_other = swap(score_par)
    o_own, score_own = half_stage(block_count, own_rows, s_own, pieces)

    mid = ROWS // 2

    def both(k, a, b, extra=None):
        total = o_own[k, a:b].astype(jnp.float32) + other[k, a:b].astype(jnp.float32)
        if extra is not None:
            total = total + extra.astype(jnp.float32)
        return total.astype(jnp.bfloat16)

    through_f = zhop(both(0, 0, mid), 1)
    through_b = zhop(both(0, mid, ROWS), -1)
    low_b = zhop(both(1, mid, ROWS), 1)
    low_a = zhop(both(2, 0, mid), -1)

    row_scores = score_own + score_other
    up_one, down_one = zhop(row_scores, 1), zhop(row_scores, -1)
    row_scores = (row_scores + zhop(row_scores, 2)) + (up_one + down_one)

    full_a = zhop(both(1, 0, mid, through_f), 1)
    full_b = zhop(both(2, mid, ROWS, through_b), -1)
    hot, score_grad = marks(block_count, route_index, row_scores)
    input_grad = place(block_count, hot, o_own, other, full_a, full_b, low_a, low_b)
    return (input_grad, score_grad.reshape(router_score.shape))


def solution(mesh):
    placed = (
        P("seq", "tensor"),
        P("seq", "tensor"),
        P("seq"),
        P("seq", None),
        P("seq"),
        P("seq", "tensor"),
        P("tensor", "seq"),
    )
    return jax.shard_map(
        branch,
        mesh=mesh,
        in_specs=placed,
        out_specs=(P("seq", "tensor"), P("seq")),
        check_vma=False,
    )
```

time: 159 us -> 151 us (0.950)
  waiting for transfers between devices: 56.1 us -> 83.6 us
  Pallas kernels: 50.8 us -> 31.6 us
  local copies, waits for them, and re-layouts: 11.4 us -> 1.28 us
  other arithmetic: 5.3 us -> 0.84 us
    pallas_call x4, Pallas kernels: 42 us -> 23.8 us  [the longest x2 18.1 us: half_stage(): pl.pallas_call(half_kernel, in_specs=[SMEM] + [VMEM] * 22, out_specs=[VME...]
    ppermute x9, waiting for transfers between devices: 7.78 us -> 21.3 us  [zhop(): lax.ppermute(value, 'tensor', [(i, (i + step) % SIDE) for i in range(SIDE)])]
    ppermute x16, waiting for transfers between devices: 39.4 us -> 47.3 us  [hop(): return lax.ppermute(value, 'seq', ring(step, phase))]
    convert_element_type x2, other arithmetic: 4.38 us -> 0.49 us  [both(): return total.astype(jnp.bfloat16)]
    ppermute x3, waiting for transfers between devices: 3.7 us -> 7.37 us  [zdir(): return lax.ppermute(value, ('seq', 'tensor'), ZPAIRS)]
    scatter x1 -> x0, local copies, waits for them, and re-layouts: 3.02 us -> none  [branch(): score_grad.at[picked]]
    ppermute x11 -> x10, waiting for transfers between devices: 5.19 us -> 7.67 us  [swap(): return lax.ppermute(value, 'seq', SWAP)]
    ppermute x11 -> x10, starting transfers between devices: 5.33 us -> 4.26 us  [swap(): return lax.ppermute(value, 'seq', SWAP)]
  transfers between devices with their start and end apart: 39 -> 38, of which waited for: 16 -> 18; matrix products, arithmetic and copies ran while one was open for 8% -> 1% of each run, Pallas kernels for 18% -> 12%
where the time goes in v2:
time: 151 us
  waiting for transfers between devices  83.6 us (55%)
  starting transfers between devices  32 us (21%)
  Pallas kernels  31.6 us (21%)
  between operations  1.79 us (1%)
    ppermute x16, waiting for transfers between devices, hop(): return lax.ppermute(value, 'seq', ring(step, phase))  47.3 us
    ppermute x9, waiting for transfers between devices, zhop(): lax.ppermute(value, 'tensor', [(i, (i + step) % SIDE) for i in range(SIDE)])  21.3 us
    pallas_call x2, Pallas kernels, half_stage(): pl.pallas_call(half_kernel, in_specs=[SMEM] + [VMEM] * 22, out_specs=[VME...  18.1 us
    ppermute x16, starting transfers between devices, hop(): return lax.ppermute(value, 'seq', ring(step, phase))  15.9 us
    ppermute x9, starting transfers between devices, zhop(): lax.ppermute(value, 'tensor', [(i, (i + step) % SIDE) for i in range(SIDE)])  9.84 us
    pallas_call x1, Pallas kernels, pick(): pl.pallas_call(pick_kernel, grid_spec=pltpu.PrefetchScalarGridSpec(num_sc...  7.82 us
    ppermute x10, waiting for transfers between devices, swap(): return lax.ppermute(value, 'seq', SWAP)  7.67 us
    ppermute x3, waiting for transfers between devices, zdir(): return lax.ppermute(value, ('seq', 'tensor'), ZPAIRS)  7.37 us
  transfers between devices with their start and end apart: 38, of which 18 were waited for; matrix products, arithmetic and copies ran while one was open for 1% of the time, Pallas kernels for 12%

profile of v2, /device:TPU:30, one launch (start us, length us, event | category | flops | bytes accessed | tf_op | source)
XLA Modules:
  0.0 151.2 jit_solution(8445199794974627414)
XLA Ops:
  0.6 0.1 collective-permute-start.6
  1.4 7.8 %pick.1 = (bf16[2,512,512]{2,1,0:T(8,128)(2,1)S(1)}, f32[512,1]{1,0:T(8,128)S(1)}) custom-call(s32[1]{0:T(128)S(6)} %copy.9.count, s32[1,512]{1,0:T(1,128)} %idx.1, f32[1,4096]{1,0:T(1,128)} %bitcast.46, bf16[4096,512]{1,0:T(8,128)(2,1)} %x_hbm.1, bf16[4096,512]{1,0:T(8,128)(2,1)} %g_hbm.1), custom_call_target="tpu_custom_call" | custom-call | tf_op jit(solution)/shard_map/pick/pallas_call | solution.py:140
  9.2 2.0 %collective-permute-start = (bf16[2,512,512]{2,1,0:T(8,128)(2,1)S(1)}, bf16[2,512,512]{2,1,0:T(8,128)(2,1)S(1)}, u32[]{:S(2)}, u32[]{:S(2)}) collective-permute-start(bf16[2,512,512]{2,1,0:T(8,128)(2,1)S(1)} %get-tuple-element.10.refs_0_), channel_id=1, source_target_pairs={{0,1},{4,7},{8,9},{12,15},{16,17},{20,23},{24,25},{28,31},{32,33},... | collective-permute-start | bytes 3145736 | tf_op jit(solution)/shard_map/ppermute | solution.py:64
  11.2 3.1 %collective-permute-start.5 = (bf16[64,2048]{1,0:T(8,128)(2,1)S(1)}, bf16[64,2048]{1,0:T(8,128)(2,1)}, u32[]{:S(2)}, u32[]{:S(2)}) collective-permute-start(bf16[64,2048]{1,0:T(8,128)(2,1)S(1)} %copy-done.2), channel_id=1, source_target_pairs={{0,4},{4,0},{8,12},{12,8},{16,20},{20,16},{24,28},{28,24},{32,36},... | collective-permute-start | bytes 786440 | tf_op jit(solution)/shard_map/ppermute | solution.py:49
  14.4 1.2 collective-permute-done.5
  15.6 0.9 dynamic-slice_bitcast_fusion.2
  16.7 2.0 %collective-permute-start.8 = (bf16[2,128,1024]{2,1,0:T(8,128)(2,1)S(1)}, bf16[2,128,1024]{2,1,0:T(8,128)(2,1)S(1)}, u32[]{:S(2)}, u32[]{:S(2)}) collective-permute-start(bf16[2,128,1024]{2,1,0:T(8,128)(2,1)S(1)} %pad_maximum_fusion.1.refs_5_), channel_id=1, source_target_pairs={{0,96},{4,28},{8,104},{12,4},{16,112},{20,12},{24,120},{28,20},{32... | collective-permute-start | bytes 1572872 | tf_op jit(solution)/shard_map/ppermute | solution.py:53
  18.7 1.4 collective-permute-start.11
  20.1 9.8 %collective-permute-done.7.refs_6_ = bf16[2,128,1024]{2,1,0:T(8,128)(2,1)S(1)} collective-permute-done((bf16[2,128,1024]{2,1,0:T(8,128)(2,1)S(1)}, bf16[2,128,1024]{2,1,0:T(8,128)(2,1)S(1)}, u32[]{:S(2)}, u32[]{:S(2)}) %collective-permute-start.7) | collective-permute-done | bytes 524320 | tf_op jit(solution)/shard_map/ppermute | solution.py:53
  29.9 0.1 fusion.6
  30.0 0.1 collective-permute-start.23
  30.2 0.7 collective-permute-done.11.refs_10_
  30.9 0.4 collective-permute-start.26
  31.3 0.2 collective-permute-done.23.count
  31.5 1.2 collective-permute-start.9
  32.7 7.6 %collective-permute-done.12.refs_11_ = bf16[2,128,1024]{2,1,0:T(8,128)(2,1)S(1)} collective-permute-done((bf16[2,128,1024]{2,1,0:T(8,128)(2,1)S(1)}, bf16[2,128,1024]{2,1,0:T(8,128)(2,1)S(1)}, u32[]{:S(2)}, u32[]{:S(2)}) %collective-permute-start.12) | collective-permute-done | bytes 524320 | tf_op jit(solution)/shard_map/ppermute | solution.py:53
  40.3 0.1 collective-permute-start.10
  40.5 2.0 %collective-permute-start.20 = (bf16[128,1024]{1,0:T(8,128)(2,1)S(1)}, bf16[128,1024]{1,0:T(8,128)(2,1)S(1)}, u32[]{:S(2)}, u32[]{:S(2)}) collective-permute-start(bf16[128,1024]{1,0:T(8,128)(2,1)S(1)} %slice_bitcast_fusion.1), channel_id=1, source_target_pairs={{0,24},{4,100},{8,0},{12,108},{16,8},{20,116},{24,16},{28,124},{32... | collective-permute-start | bytes 786440 | tf_op jit(solution)/shard_map/ppermute | solution.py:53
  42.5 0.1 pad_maximum_fusion
  42.7 1.5 %collective-permute-start.13 = (bf16[4,128,1024]{2,1,0:T(8,128)(2,1)S(1)}, bf16[4,128,1024]{2,1,0:T(8,128)(2,1)S(1)}, u32[]{:S(2)}, u32[]{:S(2)}) collective-permute-start(bf16[4,128,1024]{2,1,0:T(8,128)(2,1)S(1)} %pad_maximum_fusion), channel_id=1, source_target_pairs={{0,8},{4,36},{8,16},{12,44},{16,24},{20,52},{24,0},{28,60},{32,40}... | collective-permute-start | bytes 3145736 | tf_op jit(solution)/shard_map/ppermute | solution.py:53
  44.2 3.7 %collective-permute-done.10.refs_9_ = bf16[128,1024]{1,0:T(8,128)(2,1)S(1)} collective-permute-done((bf16[128,1024]{1,0:T(8,128)(2,1)S(1)}, bf16[128,1024]{1,0:T(8,128)(2,1)S(1)}, u32[]{:S(2)}, u32[]{:S(2)}) %collective-permute-start.10) | collective-permute-done | bytes 262176 | tf_op jit(solution)/shard_map/ppermute | solution.py:53
  48.0 3.3 %collective-permute-start.15 = (bf16[2,128,1024]{2,1,0:T(8,128)(2,1)S(1)}, bf16[2,128,1024]{2,1,0:T(8,128)(2,1)S(1)}, u32[]{:S(2)}, u32[]{:S(2)}) collective-permute-start(bf16[2,128,1024]{2,1,0:T(8,128)(2,1)S(1)} %pad_maximum_fusion.2), channel_id=1, source_target_pairs={{0,8},{4,36},{8,16},{12,44},{16,24},{20,52},{24,0},{28,60},{32,40}... | collective-permute-start | bytes 1572872 | tf_op jit(solution)/shard_map/ppermute | solution.py:53
  51.3 12.5 %collective-permute-done.15.refs_14_ = bf16[2,128,1024]{2,1,0:T(8,128)(2,1)S(1)} collective-permute-done((bf16[2,128,1024]{2,1,0:T(8,128)(2,1)S(1)}, bf16[2,128,1024]{2,1,0:T(8,128)(2,1)S(1)}, u32[]{:S(2)}, u32[]{:S(2)}) %collective-permute-start.15) | collective-permute-done | bytes 524320 | tf_op jit(solution)/shard_map/ppermute | solution.py:53
  63.7 5.8 %collective-permute-done.16.refs_15_ = bf16[2,128,1024]{2,1,0:T(8,128)(2,1)S(1)} collective-permute-done((bf16[2,128,1024]{2,1,0:T(8,128)(2,1)S(1)}, bf16[2,128,1024]{2,1,0:T(8,128)(2,1)S(1)}, u32[]{:S(2)}, u32[]{:S(2)}) %collective-permute-start.16) | collective-permute-done | bytes 524320 | tf_op jit(solution)/shard_map/ppermute | solution.py:53
  69.6 1.0 collective-permute-start.19
  70.6 1.1 collective-permute-start.22
  71.8 4.3 %collective-permute-done.19.refs_18_ = bf16[128,1024]{1,0:T(8,128)(2,1)S(1)} collective-permute-done((bf16[128,1024]{1,0:T(8,128)(2,1)S(1)}, bf16[128,1024]{1,0:T(8,128)(2,1)S(1)}, u32[]{:S(2)}, u32[]{:S(2)}) %collective-permute-start.19) | collective-permute-done | bytes 262176 | tf_op jit(solution)/shard_map/ppermute | solution.py:53
  76.0 2.1 %collective-permute-start.18 = (bf16[2,128,1024]{2,1,0:T(8,128)(2,1)S(1)}, bf16[2,128,1024]{2,1,0:T(8,128)(2,1)S(1)}, u32[]{:S(2)}, u32[]{:S(2)}) collective-permute-start(bf16[2,128,1024]{2,1,0:T(8,128)(2,1)S(1)} %slice.95), channel_id=1, source_target_pairs={{0,8},{4,36},{8,16},{12,44},{16,24},{20,52},{24,0},{28,60},{32,40}... | collective-permute-start | bytes 1572872 | tf_op jit(solution)/shard_map/ppermute | solution.py:53
  78.2 7.4 %collective-permute-done.2.refs_1_ = bf16[2,512,512]{2,1,0:T(8,128)(2,1)S(1)} collective-permute-done((bf16[2,512,512]{2,1,0:T(8,128)(2,1)S(1)}, bf16[2,512,512]{2,1,0:T(8,128)(2,1)S(1)}, u32[]{:S(2)}, u32[]{:S(2)}) %collective-permute-start.2) | collective-permute-done | bytes 1048608 | tf_op jit(solution)/shard_map/ppermute | solution.py:64
  85.5 3.0 %collective-permute-done.21.refs_20_ = bf16[2,128,1024]{2,1,0:T(8,128)(2,1)S(1)} collective-permute-done((bf16[2,128,1024]{2,1,0:T(8,128)(2,1)S(1)}, bf16[2,128,1024]{2,1,0:T(8,128)(2,1)S(1)}, u32[]{:S(2)}, u32[]{:S(2)}) %collective-permute-start.21) | collective-permute-done | bytes 524320 | tf_op jit(solution)/shard_map/ppermute | solution.py:53
  88.5 9.4 %half_stage.3 = (bf16[4,512,512]{2,1,0:T(8,128)(2,1)S(1)}, f32[1,512]{1,0:T(1,128)S(1)}) custom-call(s32[1]{0:T(128)} %collective-permute-done.23.count, bf16[2,512,512]{2,1,0:T(8,128)(2,1)S(1)} %collective-permute-done.1.refs_0_, bf16[2,512,512]{2,1,0:T(8,128)(2,1)S(1)} %collective-permute-done.2.refs_1_, ...), custom_call_target="tpu_custom_call" | custom-call | tf_op jit(solution)/shard_map/half_stage/pallas_call | solution.py:231
  98.0 0.1 collective-permute-start.31
  98.0 0.5 collective-permute-start.3
  98.5 5.1 %collective-permute-done.3.refs_2_ = bf16[2,512,512]{2,1,0:T(8,128)(2,1)S(1)} collective-permute-done((bf16[2,512,512]{2,1,0:T(8,128)(2,1)S(1)}, bf16[2,512,512]{2,1,0:T(8,128)(2,1)S(1)}, u32[]{:S(2)}, u32[]{:S(2)}) %collective-permute-start.3) | collective-permute-done | bytes 1048608 | tf_op jit(solution)/shard_map/ppermute | solution.py:49
  103.7 8.7 %half_stage.2 = (bf16[4,512,512]{2,1,0:T(8,128)(2,1)S(1)}, f32[1,512]{1,0:T(1,128)S(1)}) custom-call(s32[1]{0:T(128)S(6)} %copy.9.count, bf16[2,512,512]{2,1,0:T(8,128)(2,1)S(1)} %get-tuple-element.10.refs_0_, bf16[2,512,512]{2,1,0:T(8,128)(2,1)S(1)} %collective-permute-done.refs_1_, bf16[2,512,512]{2,1,0:T(8,128)(2,1)S(1)} %collective-permute-done.3.refs_2_, ...), custom_call_target="tpu_custom_call" | custom-call | tf_op jit(solution)/shard_map/half_stage/pallas_call | solution.py:231
  112.4 0.3 fusion.5
  112.7 3.3 %collective-permute-start.34 = (bf16[256,512]{1,0:T(8,128)(2,1)S(1)}, bf16[256,512]{1,0:T(8,128)(2,1)S(1)}, u32[]{:S(2)}, u32[]{:S(2)}) collective-permute-start(bf16[256,512]{1,0:T(8,128)(2,1)S(1)} %get-tuple-element.20), channel_id=1, source_target_pairs={{0,3},{1,0},{2,1},{3,2},{4,7},{5,4},{6,5},{7,6},{8,11},{9,8},{10,9... | collective-permute-start | bytes 786440 | tf_op jit(solution)/shard_map/ppermute | solution.py:68
  116.0 3.2 %collective-permute-start.36 = (bf16[256,512]{1,0:T(8,128)(2,1)S(1)}, bf16[256,512]{1,0:T(8,128)(2,1)S(1)}, u32[]{:S(2)}, u32[]{:S(2)}) collective-permute-start(bf16[256,512]{1,0:T(8,128)(2,1)S(1)} %get-tuple-element.19), channel_id=1, source_target_pairs={{0,3},{1,0},{2,1},{3,2},{4,7},{5,4},{6,5},{7,6},{8,11},{9,8},{10,9... | collective-permute-start | bytes 786440 | tf_op jit(solution)/shard_map/ppermute | solution.py:68
  119.3 3.5 %collective-permute-done.34 = bf16[256,512]{1,0:T(8,128)(2,1)S(1)} collective-permute-done((bf16[256,512]{1,0:T(8,128)(2,1)S(1)}, bf16[256,512]{1,0:T(8,128)(2,1)S(1)}, u32[]{:S(2)}, u32[]{:S(2)}) %collective-permute-start.34) | collective-permute-done | bytes 262176 | tf_op jit(solution)/shard_map/ppermute | solution.py:68
  122.7 3.7 %collective-permute-done.32 = bf16[256,512]{1,0:T(8,128)(2,1)S(1)} collective-permute-done((bf16[256,512]{1,0:T(8,128)(2,1)S(1)}, bf16[256,512]{1,0:T(8,128)(2,1)S(1)}, u32[]{:S(2)}, u32[]{:S(2)}) %collective-permute-start.32) | collective-permute-done | bytes 262176 | tf_op jit(solution)/shard_map/ppermute | solution.py:68
  126.4 0.2 fusion
  126.7 3.2 %collective-permute-start.35 = (bf16[256,512]{1,0:T(8,128)(2,1)S(1)}, bf16[256,512]{1,0:T(8,128)(2,1)S(1)}, u32[]{:S(2)}, u32[]{:S(2)}) collective-permute-start(bf16[256,512]{1,0:T(8,128)(2,1)S(1)} %get-tuple-element.22), channel_id=1, source_target_pairs={{0,3},{1,0},{2,1},{3,2},{4,7},{5,4},{6,5},{7,6},{8,11},{9,8},{10,9... | collective-permute-start | bytes 786440 | tf_op jit(solution)/shard_map/ppermute | solution.py:68
  129.9 1.2 collective-permute-done.27
  131.1 5.5 %collective-permute-done.29 = f32[1,512]{1,0:T(1,128)S(1)} collective-permute-done((f32[1,512]{1,0:T(1,128)S(1)}, f32[1,512]{1,0:T(1,128)S(1)}, u32[]{:S(2)}, u32[]{:S(2)}) %collective-permute-start.29) | collective-permute-done | bytes 2080 | tf_op jit(solution)/shard_map/ppermute | solution.py:68
  136.6 3.6 %collective-permute-done.30 = f32[1,512]{1,0:T(1,128)S(1)} collective-permute-done((f32[1,512]{1,0:T(1,128)S(1)}, f32[1,512]{1,0:T(1,128)S(1)}, u32[]{:S(2)}, u32[]{:S(2)}) %collective-permute-start.30) | collective-permute-done | bytes 2080 | tf_op jit(solution)/shard_map/ppermute | solution.py:68
  140.2 5.1 %collective-permute-done.28 = f32[1,512]{1,0:T(1,128)S(1)} collective-permute-done((f32[1,512]{1,0:T(1,128)S(1)}, f32[1,512]{1,0:T(1,128)S(1)}, u32[]{:S(2)}, u32[]{:S(2)}) %collective-permute-start.28) | collective-permute-done | bytes 2080 | tf_op jit(solution)/shard_map/ppermute | solution.py:68
  145.3 2.3 %marks.1 = (bf16[4096,512]{1,0:T(8,128)(2,1)S(1)}, f32[1,4096]{1,0:T(1,128)}) custom-call(s32[1]{0:T(128)S(6)} %copy.9.count, s32[1,512]{1,0:T(1,128)S(1)} %copy-done, f32[1,512]{1,0:T(1,128)S(1)} %add_add_fusion.scores), custom_call_target="tpu_custom_call" | custom-call | tf_op jit(solution)/shard_map/marks/pallas_call | solution.py:269
  147.6 3.4 %place.1 = bf16[4096,512]{1,0:T(8,128)(2,1)} custom-call(s32[1]{0:T(128)S(6)} %copy.9.count, bf16[4096,512]{1,0:T(8,128)(2,1)S(1)} %get-tuple-element.14.hot, bf16[4,512,512]{2,1,0:T(8,128)(2,1)S(1)} %get-tuple-element.15.own, bf16[4,512,512]{2,1,0:T(8,128)(2,1)S(1)} %collective-permute-done.31.other, bf16[256,512]{1,0:T(8,128)(2,1)S(1)} %collective-permute-done.33.full_a, ...), custom_call_target="tpu_custom_call" | custom-call | tf_op jit(solution)/shard_map/place/pallas_call | solution.py:304
  (60 shorter events, 0.8 us)
Async XLA Ops:
  0.6 13.7 %collective-permute-start.6 = (bf16[64,2048]{1,0:T(8,128)(2,1)}, bf16[64,2048]{1,0:T(8,128)(2,1)S(1)}, u32[]{:S(2)}, u32[]{:S(2)}) collective-permute-start(bf16[64,2048]{1,0:T(8,128)(2,1)} %bitcast.45), channel_id=1, source_target_pairs={{0,4},{4,0},{8,12},{12,8},{16,20},{20,16},{24,28},{28,24},{32,36},... | collective-permute-start | bytes 786440 | tf_op jit(solution)/shard_map/ppermute | solution.py:49
  1.4 9.8 %copy-start.2 = (bf16[64,2048]{1,0:T(8,128)(2,1)S(1)}, bf16[64,2048]{1,0:T(8,128)(2,1)}, u32[]{:S(2)}) copy-start(bf16[64,2048]{1,0:T(8,128)(2,1)} %param.12) | copy-start | bytes 786436
  1.4 12.9 %copy-start.1 = (bf16[2048,64]{0,1:T(8,128)(2,1)S(1)}, bf16[2048,64]{0,1:T(8,128)(2,1)}, u32[]{:S(2)}) copy-start(bf16[2048,64]{0,1:T(8,128)(2,1)} %param.13) | copy-start | bytes 786436
  9.2 22.1 %collective-permute-start = (bf16[2,512,512]{2,1,0:T(8,128)(2,1)S(1)}, bf16[2,512,512]{2,1,0:T(8,128)(2,1)S(1)}, u32[]{:S(2)}, u32[]{:S(2)}) collective-permute-start(bf16[2,512,512]{2,1,0:T(8,128)(2,1)S(1)} %get-tuple-element.10.refs_0_), channel_id=1, source_target_pairs={{0,1},{4,7},{8,9},{12,15},{16,17},{20,23},{24,25},{28,31},{32,33},... | collective-permute-start | bytes 3145736 | tf_op jit(solution)/shard_map/ppermute | solution.py:64
  11.2 4.4 %collective-permute-start.5 = (bf16[64,2048]{1,0:T(8,128)(2,1)S(1)}, bf16[64,2048]{1,0:T(8,128)(2,1)}, u32[]{:S(2)}, u32[]{:S(2)}) collective-permute-start(bf16[64,2048]{1,0:T(8,128)(2,1)S(1)} %copy-done.2), channel_id=1, source_target_pairs={{0,4},{4,0},{8,12},{12,8},{16,20},{20,16},{24,28},{28,24},{32,36},... | collective-permute-start | bytes 786440 | tf_op jit(solution)/shard_map/ppermute | solution.py:49
  16.6 13.3 %collective-permute-start.7 = (bf16[2,128,1024]{2,1,0:T(8,128)(2,1)S(1)}, bf16[2,128,1024]{2,1,0:T(8,128)(2,1)S(1)}, u32[]{:S(2)}, u32[]{:S(2)}) collective-permute-start(bf16[2,128,1024]{2,1,0:T(8,128)(2,1)S(1)} %pad_maximum_fusion.1.refs_5_), channel_id=1, source_target_pairs={{0,32},{4,12},{8,40},{12,20},{16,48},{20,28},{24,56},{28,4},{32,64... | collective-permute-start | bytes 1572872 | tf_op jit(solution)/shard_map/ppermute | solution.py:53
  16.7 13.3 %collective-permute-start.8 = (bf16[2,128,1024]{2,1,0:T(8,128)(2,1)S(1)}, bf16[2,128,1024]{2,1,0:T(8,128)(2,1)S(1)}, u32[]{:S(2)}, u32[]{:S(2)}) collective-permute-start(bf16[2,128,1024]{2,1,0:T(8,128)(2,1)S(1)} %pad_maximum_fusion.1.refs_5_), channel_id=1, source_target_pairs={{0,96},{4,28},{8,104},{12,4},{16,112},{20,12},{24,120},{28,20},{32... | collective-permute-start | bytes 1572872 | tf_op jit(solution)/shard_map/ppermute | solution.py:53
  18.7 21.8 %collective-permute-start.1 = (bf16[2,512,512]{2,1,0:T(8,128)(2,1)S(1)}, bf16[2,512,512]{2,1,0:T(8,128)(2,1)S(1)}, u32[]{:S(2)}, u32[]{:S(2)}) collective-permute-start(bf16[2,512,512]{2,1,0:T(8,128)(2,1)S(1)} %get-tuple-element.10.refs_0_), channel_id=1, source_target_pairs={{0,4},{4,0},{8,12},{12,8},{16,20},{20,16},{24,28},{28,24},{32,36},... | collective-permute-start | bytes 3145736 | tf_op jit(solution)/shard_map/ppermute | solution.py:49
  18.7 12.2 %collective-permute-start.11 = (bf16[2,128,1024]{2,1,0:T(8,128)(2,1)S(1)}, bf16[2,128,1024]{2,1,0:T(8,128)(2,1)S(1)}, u32[]{:S(2)}, u32[]{:S(2)}) collective-permute-start(bf16[2,128,1024]{2,1,0:T(8,128)(2,1)S(1)} %pad_maximum_fusion.1.refs_5_), channel_id=1, source_target_pairs={{0,8},{4,36},{8,16},{12,44},{16,24},{20,52},{24,0},{28,60},{32,40}... | collective-permute-start | bytes 1572872 | tf_op jit(solution)/shard_map/ppermute | solution.py:53
  29.9 10.4 %collective-permute-start.12 = (bf16[2,128,1024]{2,1,0:T(8,128)(2,1)S(1)}, bf16[2,128,1024]{2,1,0:T(8,128)(2,1)S(1)}, u32[]{:S(2)}, u32[]{:S(2)}) collective-permute-start(bf16[2,128,1024]{2,1,0:T(8,128)(2,1)S(1)} %pad_maximum_fusion.1.refs_5_), channel_id=1, source_target_pairs={{0,24},{4,100},{8,0},{12,108},{16,8},{20,116},{24,16},{28,124},{32... | collective-permute-start | bytes 1572872 | tf_op jit(solution)/shard_map/ppermute | solution.py:53
  30.0 1.5 collective-permute-start.23
  30.9 9.5 %collective-permute-start.26 = (f32[512,1]{1,0:T(8,128)S(1)}, f32[512,1]{1,0:T(8,128)S(1)}, u32[]{:S(2)}, u32[]{:S(2)}) collective-permute-start(f32[512,1]{1,0:T(8,128)S(1)} %get-tuple-element.11.refs_4_), channel_id=1, source_target_pairs={{0,4},{4,0},{8,12},{12,8},{16,20},{20,16},{24,28},{28,24},{32,36},... | collective-permute-start | bytes 6152 | tf_op jit(solution)/shard_map/ppermute | solution.py:49
  31.3 38.2 %collective-permute-start.4 = (bf16[2,512,512]{2,1,0:T(8,128)(2,1)S(1)}, bf16[2,512,512]{2,1,0:T(8,128)(2,1)S(1)}, u32[]{:S(2)}, u32[]{:S(2)}) collective-permute-start(bf16[2,512,512]{2,1,0:T(8,128)(2,1)S(1)} %collective-permute-done.refs_1_), channel_id=1, source_target_pairs={{0,1},{4,7},{8,9},{12,15},{16,17},{20,23},{24,25},{28,31},{32,33},... | collective-permute-start | bytes 3145736 | tf_op jit(solution)/shard_map/ppermute | solution.py:64
  31.5 11.1 %collective-permute-start.9 = (bf16[128,1024]{1,0:T(8,128)(2,1)S(1)}, bf16[128,1024]{1,0:T(8,128)(2,1)S(1)}, u32[]{:S(2)}, u32[]{:S(2)}) collective-permute-start(bf16[128,1024]{1,0:T(8,128)(2,1)S(1)} %get-tuple-element.25), channel_id=1, source_target_pairs={{0,32},{4,12},{8,40},{12,20},{16,48},{20,28},{24,56},{28,4},{32,64... | collective-permute-start | bytes 786440 | tf_op jit(solution)/shard_map/ppermute | solution.py:53
  40.3 7.6 %collective-permute-start.10 = (bf16[128,1024]{1,0:T(8,128)(2,1)S(1)}, bf16[128,1024]{1,0:T(8,128)(2,1)S(1)}, u32[]{:S(2)}, u32[]{:S(2)}) collective-permute-start(bf16[128,1024]{1,0:T(8,128)(2,1)S(1)} %get-tuple-element.28), channel_id=1, source_target_pairs={{0,96},{4,28},{8,104},{12,4},{16,112},{20,12},{24,120},{28,20},{32... | collective-permute-start | bytes 786440 | tf_op jit(solution)/shard_map/ppermute | solution.py:53
  40.4 7.5 %collective-permute-start.17 = (bf16[128,1024]{1,0:T(8,128)(2,1)S(1)}, bf16[128,1024]{1,0:T(8,128)(2,1)S(1)}, u32[]{:S(2)}, u32[]{:S(2)}) collective-permute-start(bf16[128,1024]{1,0:T(8,128)(2,1)S(1)} %slice_bitcast_fusion.3), channel_id=1, source_target_pairs={{0,8},{4,36},{8,16},{12,44},{16,24},{20,52},{24,0},{28,60},{32,40}... | collective-permute-start | bytes 786440 | tf_op jit(solution)/shard_map/ppermute | solution.py:53
  40.5 10.7 %collective-permute-start.20 = (bf16[128,1024]{1,0:T(8,128)(2,1)S(1)}, bf16[128,1024]{1,0:T(8,128)(2,1)S(1)}, u32[]{:S(2)}, u32[]{:S(2)}) collective-permute-start(bf16[128,1024]{1,0:T(8,128)(2,1)S(1)} %slice_bitcast_fusion.1), channel_id=1, source_target_pairs={{0,24},{4,100},{8,0},{12,108},{16,8},{20,116},{24,16},{28,124},{32... | collective-permute-start | bytes 786440 | tf_op jit(solution)/shard_map/ppermute | solution.py:53
  42.7 26.9 %collective-permute-start.13 = (bf16[4,128,1024]{2,1,0:T(8,128)(2,1)S(1)}, bf16[4,128,1024]{2,1,0:T(8,128)(2,1)S(1)}, u32[]{:S(2)}, u32[]{:S(2)}) collective-permute-start(bf16[4,128,1024]{2,1,0:T(8,128)(2,1)S(1)} %pad_maximum_fusion), channel_id=1, source_target_pairs={{0,8},{4,36},{8,16},{12,44},{16,24},{20,52},{24,0},{28,60},{32,40}... | collective-permute-start | bytes 3145736 | tf_op jit(solution)/shard_map/ppermute | solution.py:53
  47.9 22.7 %collective-permute-start.14 = (bf16[4,128,1024]{2,1,0:T(8,128)(2,1)S(1)}, bf16[4,128,1024]{2,1,0:T(8,128)(2,1)S(1)}, u32[]{:S(2)}, u32[]{:S(2)}) collective-permute-start(bf16[4,128,1024]{2,1,0:T(8,128)(2,1)S(1)} %pad_maximum_fusion), channel_id=1, source_target_pairs={{0,24},{4,100},{8,0},{12,108},{16,8},{20,116},{24,16},{28,124},{32... | collective-permute-start | bytes 3145736 | tf_op jit(solution)/shard_map/ppermute | solution.py:53
  48.0 15.8 %collective-permute-start.15 = (bf16[2,128,1024]{2,1,0:T(8,128)(2,1)S(1)}, bf16[2,128,1024]{2,1,0:T(8,128)(2,1)S(1)}, u32[]{:S(2)}, u32[]{:S(2)}) collective-permute-start(bf16[2,128,1024]{2,1,0:T(8,128)(2,1)S(1)} %pad_maximum_fusion.2), channel_id=1, source_target_pairs={{0,8},{4,36},{8,16},{12,44},{16,24},{20,52},{24,0},{28,60},{32,40}... | collective-permute-start | bytes 1572872 | tf_op jit(solution)/shard_map/ppermute | solution.py:53
  51.3 18.3 %collective-permute-start.16 = (bf16[2,128,1024]{2,1,0:T(8,128)(2,1)S(1)}, bf16[2,128,1024]{2,1,0:T(8,128)(2,1)S(1)}, u32[]{:S(2)}, u32[]{:S(2)}) collective-permute-start(bf16[2,128,1024]{2,1,0:T(8,128)(2,1)S(1)} %pad_maximum_fusion.2), channel_id=1, source_target_pairs={{0,24},{4,100},{8,0},{12,108},{16,8},{20,116},{24,16},{28,124},{32... | collective-permute-start | bytes 1572872 | tf_op jit(solution)/shard_map/ppermute | solution.py:53
  63.7 21.8 %collective-permute-start.24 = (bf16[2,512,512]{2,1,0:T(8,128)(2,1)S(1)}, bf16[2,512,512]{2,1,0:T(8,128)(2,1)S(1)}, u32[]{:S(2)}, u32[]{:S(2)}) collective-permute-start(bf16[2,512,512]{2,1,0:T(8,128)(2,1)S(1)} %collective-permute-done.refs_1_), channel_id=1, source_target_pairs={{0,4},{4,0},{8,12},{12,8},{16,20},{20,16},{24,28},{28,24},{32,36},... | collective-permute-start | bytes 3145736 | tf_op jit(solution)/shard_map/ppermute | solution.py:49
  69.5 16.0 %collective-permute-start.2 = (bf16[2,512,512]{2,1,0:T(8,128)(2,1)S(1)}, bf16[2,512,512]{2,1,0:T(8,128)(2,1)S(1)}, u32[]{:S(2)}, u32[]{:S(2)}) collective-permute-start(bf16[2,512,512]{2,1,0:T(8,128)(2,1)S(1)} %collective-permute-done.1.refs_0_), channel_id=1, source_target_pairs={{0,1},{4,7},{8,9},{12,15},{16,17},{20,23},{24,25},{28,31},{32,33},... | collective-permute-start | bytes 3145736 | tf_op jit(solution)/shard_map/ppermute | solution.py:64
  69.5 19.0 %collective-permute-start.25 = (bf16[2,512,512]{2,1,0:T(8,128)(2,1)S(1)}, bf16[2,512,512]{2,1,0:T(8,128)(2,1)S(1)}, u32[]{:S(2)}, u32[]{:S(2)}) collective-permute-start(bf16[2,512,512]{2,1,0:T(8,128)(2,1)S(1)} %collective-permute-done.4.refs_3_), channel_id=1, source_target_pairs={{0,4},{4,0},{8,12},{12,8},{16,20},{20,16},{24,28},{28,24},{32,36},... | collective-permute-start | bytes 3145736 | tf_op jit(solution)/shard_map/ppermute | solution.py:49
  69.6 6.4 %collective-permute-start.19 = (bf16[128,1024]{1,0:T(8,128)(2,1)S(1)}, bf16[128,1024]{1,0:T(8,128)(2,1)S(1)}, u32[]{:S(2)}, u32[]{:S(2)}) collective-permute-start(bf16[128,1024]{1,0:T(8,128)(2,1)S(1)} %slice_bitcast_fusion.2), channel_id=1, source_target_pairs={{0,8},{4,36},{8,16},{12,44},{16,24},{20,52},{24,0},{28,60},{32,40}... | collective-permute-start | bytes 786440 | tf_op jit(solution)/shard_map/ppermute | solution.py:53
  70.6 7.6 %collective-permute-start.22 = (bf16[128,1024]{1,0:T(8,128)(2,1)S(1)}, bf16[128,1024]{1,0:T(8,128)(2,1)S(1)}, u32[]{:S(2)}, u32[]{:S(2)}) collective-permute-start(bf16[128,1024]{1,0:T(8,128)(2,1)S(1)} %slice_bitcast_fusion), channel_id=1, source_target_pairs={{0,24},{4,100},{8,0},{12,108},{16,8},{20,116},{24,16},{28,124},{32... | collective-permute-start | bytes 786440 | tf_op jit(solution)/shard_map/ppermute | solution.py:53
  76.0 9.5 %collective-permute-start.18 = (bf16[2,128,1024]{2,1,0:T(8,128)(2,1)S(1)}, bf16[2,128,1024]{2,1,0:T(8,128)(2,1)S(1)}, u32[]{:S(2)}, u32[]{:S(2)}) collective-permute-start(bf16[2,128,1024]{2,1,0:T(8,128)(2,1)S(1)} %slice.95), channel_id=1, source_target_pairs={{0,8},{4,36},{8,16},{12,44},{16,24},{20,52},{24,0},{28,60},{32,40}... | collective-permute-start | bytes 1572872 | tf_op jit(solution)/shard_map/ppermute | solution.py:53
  78.2 10.4 %collective-permute-start.21 = (bf16[2,128,1024]{2,1,0:T(8,128)(2,1)S(1)}, bf16[2,128,1024]{2,1,0:T(8,128)(2,1)S(1)}, u32[]{:S(2)}, u32[]{:S(2)}) collective-permute-start(bf16[2,128,1024]{2,1,0:T(8,128)(2,1)S(1)} %slice.98), channel_id=1, source_target_pairs={{0,24},{4,100},{8,0},{12,108},{16,8},{20,116},{24,16},{28,124},{32... | collective-permute-start | bytes 1572872 | tf_op jit(solution)/shard_map/ppermute | solution.py:53
  98.0 14.5 %collective-permute-start.31 = (bf16[4,512,512]{2,1,0:T(8,128)(2,1)S(1)}, bf16[4,512,512]{2,1,0:T(8,128)(2,1)S(1)}, u32[]{:S(2)}, u32[]{:S(2)}) collective-permute-start(bf16[4,512,512]{2,1,0:T(8,128)(2,1)S(1)} %get-tuple-element.16), channel_id=1, source_target_pairs={{0,4},{4,0},{8,12},{12,8},{16,20},{20,16},{24,28},{28,24},{32,36},... | collective-permute-start | bytes 6291464 | tf_op jit(solution)/shard_map/ppermute | solution.py:49
  98.0 5.6 %collective-permute-start.3 = (bf16[2,512,512]{2,1,0:T(8,128)(2,1)S(1)}, bf16[2,512,512]{2,1,0:T(8,128)(2,1)S(1)}, u32[]{:S(2)}, u32[]{:S(2)}) collective-permute-start(bf16[2,512,512]{2,1,0:T(8,128)(2,1)S(1)} %collective-permute-done.2.refs_1_), channel_id=1, source_target_pairs={{0,4},{4,0},{8,12},{12,8},{16,20},{20,16},{24,28},{28,24},{32,36},... | collective-permute-start | bytes 3145736 | tf_op jit(solution)/shard_map/ppermute | solution.py:49
  112.4 32.9 %copy-start = (s32[1,512]{1,0:T(1,128)S(1)}, s32[1,512]{1,0:T(1,128)}, u32[]{:S(2)}) copy-start(s32[1,512]{1,0:T(1,128)} %idx.1) | copy-start | bytes 6148
  112.7 10.0 %collective-permute-start.34 = (bf16[256,512]{1,0:T(8,128)(2,1)S(1)}, bf16[256,512]{1,0:T(8,128)(2,1)S(1)}, u32[]{:S(2)}, u32[]{:S(2)}) collective-permute-start(bf16[256,512]{1,0:T(8,128)(2,1)S(1)} %get-tuple-element.20), channel_id=1, source_target_pairs={{0,3},{1,0},{2,1},{3,2},{4,7},{5,4},{6,5},{7,6},{8,11},{9,8},{10,9... | collective-permute-start | bytes 786440 | tf_op jit(solution)/shard_map/ppermute | solution.py:68
  116.0 10.4 %collective-permute-start.32 = (bf16[256,512]{1,0:T(8,128)(2,1)S(1)}, bf16[256,512]{1,0:T(8,128)(2,1)S(1)}, u32[]{:S(2)}, u32[]{:S(2)}) collective-permute-start(bf16[256,512]{1,0:T(8,128)(2,1)S(1)} %get-tuple-element.21), channel_id=1, source_target_pairs={{0,1},{1,2},{2,3},{3,0},{4,5},{5,6},{6,7},{7,4},{8,9},{9,10},{10,1... | collective-permute-start | bytes 786440 | tf_op jit(solution)/shard_map/ppermute | solution.py:68
  116.0 31.5 %collective-permute-start.36 = (bf16[256,512]{1,0:T(8,128)(2,1)S(1)}, bf16[256,512]{1,0:T(8,128)(2,1)S(1)}, u32[]{:S(2)}, u32[]{:S(2)}) collective-permute-start(bf16[256,512]{1,0:T(8,128)(2,1)S(1)} %get-tuple-element.19), channel_id=1, source_target_pairs={{0,3},{1,0},{2,1},{3,2},{4,7},{5,4},{6,5},{7,6},{8,11},{9,8},{10,9... | collective-permute-start | bytes 786440 | tf_op jit(solution)/shard_map/ppermute | solution.py:68
  119.3 28.3 %collective-permute-start.37 = (bf16[256,512]{1,0:T(8,128)(2,1)S(1)}, bf16[256,512]{1,0:T(8,128)(2,1)S(1)}, u32[]{:S(2)}, u32[]{:S(2)}) collective-permute-start(bf16[256,512]{1,0:T(8,128)(2,1)S(1)} %get-tuple-element.18), channel_id=1, source_target_pairs={{0,1},{1,2},{2,3},{3,0},{4,5},{5,6},{6,7},{7,4},{8,9},{9,10},{10,1... | collective-permute-start | bytes 786440 | tf_op jit(solution)/shard_map/ppermute | solution.py:68
  126.6 21.0 %collective-permute-start.33 = (bf16[256,512]{1,0:T(8,128)(2,1)S(1)}, bf16[256,512]{1,0:T(8,128)(2,1)S(1)}, u32[]{:S(2)}, u32[]{:S(2)}) collective-permute-start(bf16[256,512]{1,0:T(8,128)(2,1)S(1)} %get-tuple-element.23), channel_id=1, source_target_pairs={{0,1},{1,2},{2,3},{3,0},{4,5},{5,6},{6,7},{7,4},{8,9},{9,10},{10,1... | collective-permute-start | bytes 786440 | tf_op jit(solution)/shard_map/ppermute | solution.py:68
  126.7 20.9 %collective-permute-start.35 = (bf16[256,512]{1,0:T(8,128)(2,1)S(1)}, bf16[256,512]{1,0:T(8,128)(2,1)S(1)}, u32[]{:S(2)}, u32[]{:S(2)}) collective-permute-start(bf16[256,512]{1,0:T(8,128)(2,1)S(1)} %get-tuple-element.22), channel_id=1, source_target_pairs={{0,3},{1,0},{2,1},{3,2},{4,7},{5,4},{6,5},{7,6},{8,11},{9,8},{10,9... | collective-permute-start | bytes 786440 | tf_op jit(solution)/shard_map/ppermute | solution.py:68
  129.9 1.2 collective-permute-start.27
  131.1 5.5 %collective-permute-start.29 = (f32[1,512]{1,0:T(1,128)S(1)}, f32[1,512]{1,0:T(1,128)S(1)}, u32[]{:S(2)}, u32[]{:S(2)}) collective-permute-start(f32[1,512]{1,0:T(1,128)S(1)} %add.58), channel_id=1, source_target_pairs={{0,1},{1,2},{2,3},{3,0},{4,5},{5,6},{6,7},{7,4},{8,9},{9,10},{10,1... | collective-permute-start | bytes 6152 | tf_op jit(solution)/shard_map/ppermute | solution.py:68
  136.6 3.6 %collective-permute-start.30 = (f32[1,512]{1,0:T(1,128)S(1)}, f32[1,512]{1,0:T(1,128)S(1)}, u32[]{:S(2)}, u32[]{:S(2)}) collective-permute-start(f32[1,512]{1,0:T(1,128)S(1)} %add.58), channel_id=1, source_target_pairs={{0,3},{1,0},{2,1},{3,2},{4,7},{5,4},{6,5},{7,6},{8,11},{9,8},{10,9... | collective-permute-start | bytes 6152 | tf_op jit(solution)/shard_map/ppermute | solution.py:68
  140.2 5.1 %collective-permute-start.28 = (f32[1,512]{1,0:T(1,128)S(1)}, f32[1,512]{1,0:T(1,128)S(1)}, u32[]{:S(2)}, u32[]{:S(2)}) collective-permute-start(f32[1,512]{1,0:T(1,128)S(1)} %add.58), channel_id=1, source_target_pairs={{0,2},{1,3},{2,0},{3,1},{4,6},{5,7},{6,4},{7,5},{8,10},{9,11},{10,... | collective-permute-start | bytes 6152 | tf_op jit(solution)/shard_map/ppermute | solution.py:68

commit v3 on v2

--- a/solution.py
+++ b/solution.py
@@ -94,37 +94,35 @@
     return pltpu.with_memory_space_constraint(value, pltpu.MemorySpace.HBM)
 
 
-def whole(shape):
-    return pl.BlockSpec(shape, lambda m, meta: (0,) * len(shape))
-
-
-def pick_kernel(count, idx_hbm, score_hbm, x_hbm, g_hbm, out, s_out, idx, score, xv, gv, hot, sems):
-    small = [
-        pltpu.make_async_copy(idx_hbm, idx, sems.at[2]),
-        pltpu.make_async_copy(score_hbm, score, sems.at[3]),
-    ]
-    copies = [
-        pltpu.make_async_copy(x_hbm, xv, sems.at[0]),
-        pltpu.make_async_copy(g_hbm, gv, sems.at[1]),
-    ]
-    for copy in small + copies:
+def pick_kernel(count, idx_hbm, x_hbm, g_hbm, out, idx, xv, gv, hot, sems):
+    first = pltpu.make_async_copy(idx_hbm, idx, sems.at[8])
+    copies = []
+    for k, (far, near) in enumerate(((x_hbm, xv), (g_hbm, gv))):
+        parts = [pl.ds(t * (TOK // 4), TOK // 4) for t in range(4)]
+        copies.append(
+            [
+                pltpu.make_async_copy(far.at[at], near.at[at], sems.at[4 * k + t])
+                for t, at in enumerate(parts)
+            ]
+        )
+    for copy in [first] + copies[0] + copies[1]:
         copy.start()
-    for copy in small:
-        copy.wait()
-    column = jnp.broadcast_to(idx[...], (BLK, ROWS)).T
+    first.wait()
+    column = jnp.broadcast_to(idx[...], (BLK, ROWS)).T.astype(jnp.int16)
+    lane = lax.broadcasted_iota(jnp.int32, (BLK, BLK), 1).astype(jnp.int16)
+    one, none = jnp.ones((BLK, BLK), jnp.bfloat16), jnp.zeros((BLK, BLK), jnp.bfloat16)
     for r in range(ROWS // BLK):
 
         @pl.when(r < count[0])
         def _(r=r):
-            at = jnp.broadcast_to(column[r * BLK : (r + 1) * BLK, :1], (BLK, TOK))
-            same = lax.broadcasted_iota(jnp.int32, (BLK, TOK), 1) == at
-            hot[r * BLK : (r + 1) * BLK, :] = jnp.where(same, 1.0, 0.0).astype(jnp.bfloat16)
-            s_out[r * BLK : (r + 1) * BLK, :] = jnp.sum(
-                jnp.where(same, score[...], 0.0), axis=1, keepdims=True
-            )
-
-    for k, (copy, rows) in enumerate(zip(copies, (xv, gv))):
-        copy.wait()
+            here = slice(r * BLK, (r + 1) * BLK)
+            for t in range(TOK // BLK):
+                same = column[here, :] == lane + jnp.int16(t * BLK)
+                hot[here, t * BLK : (t + 1) * BLK] = jnp.where(same, one, none)
+
+    for k, (parts, rows) in enumerate(zip(copies, (xv, gv))):
+        for copy in parts:
+            copy.wait()
 
         @pl.when(count[0] <= 2)
         def _(k=k, rows=rows):
@@ -136,30 +134,45 @@
             out[k] = DOT(hot[...], rows[...], NN).astype(jnp.bfloat16)
 
 
-def pick(count, idx, score, inputs, out_grad):
+def pick(count, idx, inputs, out_grad):
     return pl.pallas_call(
         pick_kernel,
-        grid_spec=pltpu.PrefetchScalarGridSpec(
-            num_scalar_prefetch=1,
-            grid=(1,),
-            in_specs=[HBM] * 4,
-            out_specs=[whole((2, ROWS, 512)), whole((ROWS, 1))],
-            scratch_shapes=[
-                pltpu.VMEM((1, ROWS), jnp.int32),
-                pltpu.VMEM((1, TOK), jnp.float32),
-                pltpu.VMEM((TOK, 512), jnp.bfloat16),
-                pltpu.VMEM((TOK, 512), jnp.bfloat16),
-                pltpu.VMEM((ROWS, TOK), jnp.bfloat16),
-                pltpu.SemaphoreType.DMA((4,)),
-            ],
-        ),
-        out_shape=[
-            jax.ShapeDtypeStruct((2, ROWS, 512), jnp.bfloat16),
-            jax.ShapeDtypeStruct((ROWS, 1), jnp.float32),
+        in_specs=[SMEM, HBM, HBM, HBM],
+        out_specs=VMEM,
+        scratch_shapes=[
+            pltpu.VMEM((1, ROWS), jnp.int32),
+            pltpu.VMEM((TOK, 512), jnp.bfloat16),
+            pltpu.VMEM((TOK, 512), jnp.bfloat16),
+            pltpu.VMEM((ROWS, TOK), jnp.bfloat16),
+            pltpu.SemaphoreType.DMA((9,)),
         ],
+        out_shape=pltpu.VMEM((2, ROWS, 512), jnp.bfloat16),
         compiler_params=params(18),
         name="pick",
-    )(count, idx, score, inputs, out_grad)
+    )(count, *[off_chip(v) for v in (idx, inputs, out_grad)])
+
+
+def scale_kernel(count, idx, score, out):
+    column = jnp.broadcast_to(idx[...], (BLK, ROWS)).T
+    for r in range(ROWS // BLK):
+
+        @pl.when(r < count[0])
+        def _(r=r):
+            here = slice(r * BLK, (r + 1) * BLK)
+            at = jnp.broadcast_to(column[here, :1], (BLK, TOK))
+            same = lax.broadcasted_iota(jnp.int32, (BLK, TOK), 1) == at
+            out[here, :] = jnp.sum(jnp.where(same, score[...], 0.0), axis=1, keepdims=True)
+
+
+def scale(count, idx, score):
+    return pl.pallas_call(
+        scale_kernel,
+        in_specs=[SMEM, VMEM, VMEM],
+        out_specs=VMEM,
+        out_shape=pltpu.VMEM((ROWS, 1), jnp.float32),
+        compiler_params=params(8),
+        name="scale",
+    )(count, idx, score)
 
 
 def positions():
@@ -178,12 +191,14 @@
     return quarters, blocks, turns, (z, (z + near) & 3, (z - near + SIDE) & 3, (z + 2) & 3)
 
 
-def half_kernel(count, *refs):
+def half_kernel(tiles, count, *refs):
     rows, scale_ref = refs[:4], refs[4]
     quarters, blocks, turns, came = positions()
     (sw, p_f, p_b, h_in, h_out, y0f, y0b, yrf, yrb, yhf, yhb) = refs[5:16]
     last = (refs[16:19], refs[19:22])
-    out, score, rv, hg = refs[22:]
+    before, (out, score, rv, hg) = refs[22:-4], refs[-4:]
+    if before:
+        score[...] = before[0][...]
 
     lines = []
     for w in range(2):
@@ -202,17 +217,25 @@
             parts.append(rv[which, quarters[k], :, lanes])
         return jnp.concatenate(parts, axis=1)
 
-    @pl.loop(0, (count[0] + 1) // 2)
+    @pl.loop(tiles[0], jnp.minimum((count[0] + 1) // 2, tiles[1]))
     def _(tile):
         at = pl.ds(pl.multiple_of(tile * TILE, TILE), TILE)
+        to = pl.ds(pl.multiple_of((tile - tiles[0]) * TILE, TILE), TILE)
         for r in range(SIDE):
             rv[:, came[r]] = rows[r][:, at, :]
         xs, gs, scale = columns(0), columns(1), scale_ref[at, :]
         total = None
+
+        def products(n):
+            cols = pl.ds(n * 256, 256)
+            return DOT(xs, weights(0, cols), NN), DOT(gs, weights(1, cols), NN)
+
+        ahead = products(0)
         for n in range(4):
             cols = pl.ds(n * 256, 256)
-            hidden = DOT(xs, weights(0, cols), NN)
-            upstream = DOT(gs, weights(1, cols), NN)
+            hidden, upstream = ahead
+            if n < 3:
+                ahead = products(n + 1)
             forward, slope = gelu_pair(hidden)
             active = forward.astype(jnp.bfloat16).astype(jnp.float32)
             term = jnp.sum(upstream * active, axis=1, keepdims=True)
@@ -224,25 +247,45 @@
             result = DOT(hg[...], pair, NT).astype(jnp.bfloat16)
             for i in range(2):
                 lanes = pl.ds(pl.multiple_of(blocks[k + i] * BLK, BLK), BLK)
-                out[turns[k + i], at, lanes] = result[:, i * BLK : (i + 1) * BLK]
-
-
-def half_stage(count, rows, s, pieces):
-    return pl.pallas_call(
-        half_kernel,
-        in_specs=[SMEM] + [VMEM] * 22,
+                out[turns[k + i], to, lanes] = result[:, i * BLK : (i + 1) * BLK]
+
+
+def half_stage(tiles, count, rows, s, pieces, before=()):
+    return pl.pallas_call(
+        functools.partial(half_kernel, tiles),
+        in_specs=[SMEM] + [VMEM] * (22 + len(before)),
         out_specs=[VMEM, VMEM],
         scratch_shapes=[
             pltpu.VMEM((2, SIDE, TILE, 512), jnp.bfloat16),
             pltpu.VMEM((TILE, 1024), jnp.bfloat16),
         ],
         out_shape=[
-            pltpu.VMEM((SIDE, ROWS, 512), jnp.bfloat16),
+            pltpu.VMEM((SIDE, (tiles[1] - tiles[0]) * TILE, 512), jnp.bfloat16),
             pltpu.VMEM((1, ROWS), jnp.float32),
         ],
         compiler_params=params(12),
         name="half_stage",
-    )(count, *[on_chip(v) for v in (*rows, s, *pieces)])
+    )(count, *[on_chip(v) for v in (*rows, s, *pieces, *before)])
+
+
+def merge_kernel(turns, at, own, other, *refs):
+    extra, outs = refs[: -len(turns)], refs[-len(turns) :]
+    for k, out in zip(turns, outs):
+        total = own[k].astype(jnp.float32) + other[k, at : at + TILE].astype(jnp.float32)
+        for part in extra:
+            total = total + part[...].astype(jnp.float32)
+        out[...] = total.astype(jnp.bfloat16)
+
+
+def merge(turns, at, *parts):
+    return pl.pallas_call(
+        functools.partial(merge_kernel, turns, at),
+        in_specs=[VMEM] * len(parts),
+        out_specs=[VMEM] * len(turns),
+        out_shape=[pltpu.VMEM((TILE, 512), jnp.bfloat16)] * len(turns),
+        compiler_params=params(4),
+        name="merge",
+    )(*[on_chip(v) for v in parts])
 
 
 def marks_kernel(count, idx, scores, out, score_out):
@@ -279,11 +322,11 @@
     )(count, idx, scores)
 
 
-def place_kernel(count, hot, own, other, full_a, full_b, low_a, low_b, out, rows, done, sems):
+def place_kernel(count, hot, own_a, own_b, other, full_a, full_b, low_a, low_b, out, rows, done, sems):
     mid = ROWS // 2
-    for at, parts in ((0, (full_a, low_a)), (mid, (full_b, low_b))):
+    for at, own, parts in ((0, own_a, (full_a, low_a)), (mid, own_b, (full_b, low_b))):
         here = pl.ds(at, mid)
-        total = own[3, here, :].astype(jnp.float32) + other[3, here, :].astype(jnp.float32)
+        total = own[3].astype(jnp.float32) + other[3, here, :].astype(jnp.float32)
         for part in parts:
             total = total + part[...].astype(jnp.float32)
         at_row = lax.broadcasted_iota(jnp.int32, (mid, 512), 0) + at
@@ -299,11 +342,11 @@
         copy.wait()
 
 
-def place(count, hot, own, other, full_a, full_b, low_a, low_b):
-    held = [on_chip(v) for v in (hot, own, other, full_a, full_b, low_a, low_b)]
+def place(count, hot, own_a, own_b, other, full_a, full_b, low_a, low_b):
+    held = [on_chip(v) for v in (hot, own_a, own_b, other, full_a, full_b, low_a, low_b)]
     return pl.pallas_call(
         place_kernel,
-        in_specs=[SMEM] + [VMEM] * 7,
+        in_specs=[SMEM] + [VMEM] * 8,
         out_specs=HBM,
         scratch_shapes=[
             pltpu.VMEM((ROWS, 512), jnp.bfloat16),
@@ -325,10 +368,8 @@
     other_in, other_out = swap(w_in), swap(w_out_t)
     par_count = swap(block_count)
 
-    xg, s_own = pick(
-        block_count,
-        *[off_chip(v) for v in (route_index, router_score[None, :], inputs, out_grad)],
-    )
+    xg = pick(block_count, route_index, inputs, out_grad)
+    s_own = scale(block_count, route_index, router_score[None, :])
     z_own = zdir(xg)
     xg_par = swap(xg)
     s_par = swap(s_own)
@@ -362,32 +403,27 @@
 
     pieces = (s, p_f, p_b, h_in, h_out, y0f, y0b, yrf, yrb, yhf, yhb)
     pieces = pieces + (a_in, r_in, b_in, a_out, r_out, b_out)
-    o_par, score_par = half_stage(par_count, par_rows, s_par, pieces)
+    o_par, score_par = half_stage((0, 2), par_count, par_rows, s_par, pieces)
     other = swap(o_par)
     score_other = swap(score_par)
-    o_own, score_own = half_stage(block_count, own_rows, s_own, pieces)
+    o_a, score_a = half_stage((0, 1), block_count, own_rows, s_own, pieces)
+    o_b, score_own = half_stage((1, 2), block_count, own_rows, s_own, pieces, (score_a,))
 
     mid = ROWS // 2
-
-    def both(k, a, b, extra=None):
-        total = o_own[k, a:b].astype(jnp.float32) + other[k, a:b].astype(jnp.float32)
-        if extra is not None:
-            total = total + extra.astype(jnp.float32)
-        return total.astype(jnp.bfloat16)
-
-    through_f = zhop(both(0, 0, mid), 1)
-    through_b = zhop(both(0, mid, ROWS), -1)
-    low_b = zhop(both(1, mid, ROWS), 1)
-    low_a = zhop(both(2, 0, mid), -1)
+    add_a, sent_a = merge((0, 2), 0, o_a, other)
+    through_f, low_a = zhop(add_a, 1), zhop(sent_a, -1)
+    add_b, sent_b = merge((0, 1), mid, o_b, other)
+    through_b, low_b = zhop(add_b, -1), zhop(sent_b, 1)
 
     row_scores = score_own + score_other
     up_one, down_one = zhop(row_scores, 1), zhop(row_scores, -1)
     row_scores = (row_scores + zhop(row_scores, 2)) + (up_one + down_one)
 
-    full_a = zhop(both(1, 0, mid, through_f), 1)
-    full_b = zhop(both(2, mid, ROWS, through_b), -1)
+    (more_a,) = merge((1,), 0, o_a, other, through_f)
+    (more_b,) = merge((2,), mid, o_b, other, through_b)
+    full_a, full_b = zhop(more_a, 1), zhop(more_b, -1)
     hot, score_grad = marks(block_count, route_index, row_scores)
-    input_grad = place(block_count, hot, o_own, other, full_a, full_b, low_a, low_b)
+    input_grad = place(block_count, hot, o_a, o_b, other, full_a, full_b, low_a, low_b)
     return (input_grad, score_grad.reshape(router_score.shape))
 
 

time: 151 us -> 146 us (0.967)
  waiting for transfers between devices: 83.6 us -> 76.8 us
  starting transfers between devices: 32 us -> 33.9 us
    ppermute x9, waiting for transfers between devices: 21.3 us -> 16.5 us  [zhop(): lax.ppermute(value, 'tensor', [(i, (i + step) % SIDE) for i in range(SIDE)])]
    ppermute x9, starting transfers between devices: 9.84 us -> 11.7 us  [zhop(): lax.ppermute(value, 'tensor', [(i, (i + step) % SIDE) for i in range(SIDE)])]
    ppermute x16, waiting for transfers between devices: 47.3 us -> 45.5 us  [hop(): return lax.ppermute(value, 'seq', ring(step, phase))]
    pallas_call x4 -> x10, Pallas kernels: 29.3 us -> 30.7 us  [the longest x3 18.6 us: half_stage(): pl.pallas_call(functools.partial(half_kernel, tiles), in_specs=[SMEM] + [...]
  transfers between devices with their start and end apart: 38 -> 38, of which waited for: 18 -> 17; matrix products, arithmetic and copies ran while one was open for 1% -> 0% of each run, Pallas kernels for 12% -> 14%
where the time goes in v3:
time: 146 us
  waiting for transfers between devices  76.8 us (53%)
  starting transfers between devices  33.9 us (23%)
  Pallas kernels  33 us (23%)
  between operations  1.8 us (1%)
    ppermute x16, waiting for transfers between devices, hop(): return lax.ppermute(value, 'seq', ring(step, phase))  45.5 us
    pallas_call x3, Pallas kernels, half_stage(): pl.pallas_call(functools.partial(half_kernel, tiles), in_specs=[SMEM] + [...  18.6 us
    ppermute x16, starting transfers between devices, hop(): return lax.ppermute(value, 'seq', ring(step, phase))  16.5 us
    ppermute x9, waiting for transfers between devices, zhop(): lax.ppermute(value, 'tensor', [(i, (i + step) % SIDE) for i in range(SIDE)])  16.5 us
    ppermute x9, starting transfers between devices, zhop(): lax.ppermute(value, 'tensor', [(i, (i + step) % SIDE) for i in range(SIDE)])  11.7 us
    ppermute x10, waiting for transfers between devices, swap(): return lax.ppermute(value, 'seq', SWAP)  7.54 us
    ppermute x3, waiting for transfers between devices, zdir(): return lax.ppermute(value, ('seq', 'tensor'), ZPAIRS)  7.2 us
    pallas_call x1, Pallas kernels, pick(): pl.pallas_call(pick_kernel, in_specs=[SMEM, HBM, HBM, HBM], out_specs=VME...  6.98 us
  transfers between devices with their start and end apart: 38, of which 17 were waited for; matrix products, arithmetic and copies ran while one was open for 0% of the time, Pallas kernels for 14%

profile of v3, /device:TPU:30, one launch (start us, length us, event | category | flops | bytes accessed | tf_op | source)
XLA Modules:
  0.0 146.1 jit_solution(10146930361305117780)
XLA Ops:
  1.4 7.0 %pick.1.refs_0_ = bf16[2,512,512]{2,1,0:T(8,128)(2,1)S(1)} custom-call(s32[1]{0:T(128)S(6)} %copy.9.count, s32[1,512]{1,0:T(1,128)} %idx.3, bf16[4096,512]{1,0:T(8,128)(2,1)} %x_hbm.1, bf16[4096,512]{1,0:T(8,128)(2,1)} %g_hbm.1), custom_call_target="tpu_custom_call" | custom-call | tf_op jit(solution)/shard_map/pick/pallas_call | solution.py:138
  8.4 2.0 %collective-permute-start = (bf16[2,512,512]{2,1,0:T(8,128)(2,1)S(1)}, bf16[2,512,512]{2,1,0:T(8,128)(2,1)S(1)}, u32[]{:S(2)}, u32[]{:S(2)}) collective-permute-start(bf16[2,512,512]{2,1,0:T(8,128)(2,1)S(1)} %pick.1.refs_0_), channel_id=1, source_target_pairs={{0,1},{4,7},{8,9},{12,15},{16,17},{20,23},{24,25},{28,31},{32,33},... | collective-permute-start | bytes 3145736 | tf_op jit(solution)/shard_map/ppermute | solution.py:64
  10.4 2.3 %collective-permute-start.5 = (bf16[64,2048]{1,0:T(8,128)(2,1)S(1)}, bf16[64,2048]{1,0:T(8,128)(2,1)S(1)}, u32[]{:S(2)}, u32[]{:S(2)}) collective-permute-start(bf16[64,2048]{1,0:T(8,128)(2,1)S(1)} %copy-done.3), channel_id=1, source_target_pairs={{0,4},{4,0},{8,12},{12,8},{16,20},{20,16},{24,28},{28,24},{32,36},... | collective-permute-start | bytes 786440 | tf_op jit(solution)/shard_map/ppermute | solution.py:49
  12.9 1.0 collective-permute-done.5
  14.1 2.0 %collective-permute-start.8 = (bf16[2,128,1024]{2,1,0:T(8,128)(2,1)S(1)}, bf16[2,128,1024]{2,1,0:T(8,128)(2,1)S(1)}, u32[]{:S(2)}, u32[]{:S(2)}) collective-permute-start(bf16[2,128,1024]{2,1,0:T(8,128)(2,1)S(1)} %pad_maximum_fusion.1.refs_5_), channel_id=1, source_target_pairs={{0,96},{4,28},{8,104},{12,4},{16,112},{20,12},{24,120},{28,20},{32... | collective-permute-start | bytes 1572872 | tf_op jit(solution)/shard_map/ppermute | solution.py:53
  16.1 1.4 collective-permute-start.11
  17.5 1.3 scale.1.refs_4_
  18.9 8.5 %collective-permute-done.7.refs_6_ = bf16[2,128,1024]{2,1,0:T(8,128)(2,1)S(1)} collective-permute-done((bf16[2,128,1024]{2,1,0:T(8,128)(2,1)S(1)}, bf16[2,128,1024]{2,1,0:T(8,128)(2,1)S(1)}, u32[]{:S(2)}, u32[]{:S(2)}) %collective-permute-start.7) | collective-permute-done | bytes 524320 | tf_op jit(solution)/shard_map/ppermute | solution.py:53
  27.6 0.7 collective-permute-done.11.refs_10_
  28.3 0.4 collective-permute-start.26
  28.7 0.2 collective-permute-done.23.count
  28.9 1.2 collective-permute-start.9
  30.1 7.6 %collective-permute-done.12.refs_11_ = bf16[2,128,1024]{2,1,0:T(8,128)(2,1)S(1)} collective-permute-done((bf16[2,128,1024]{2,1,0:T(8,128)(2,1)S(1)}, bf16[2,128,1024]{2,1,0:T(8,128)(2,1)S(1)}, u32[]{:S(2)}, u32[]{:S(2)}) %collective-permute-start.12) | collective-permute-done | bytes 524320 | tf_op jit(solution)/shard_map/ppermute | solution.py:53
  37.7 0.8 collective-permute-start.10
  38.7 2.0 %collective-permute-start.20 = (bf16[128,1024]{1,0:T(8,128)(2,1)S(1)}, bf16[128,1024]{1,0:T(8,128)(2,1)S(1)}, u32[]{:S(2)}, u32[]{:S(2)}) collective-permute-start(bf16[128,1024]{1,0:T(8,128)(2,1)S(1)} %slice_bitcast_fusion.1), channel_id=1, source_target_pairs={{0,24},{4,100},{8,0},{12,108},{16,8},{20,116},{24,16},{28,124},{32... | collective-permute-start | bytes 786440 | tf_op jit(solution)/shard_map/ppermute | solution.py:53
  40.8 1.4 collective-permute-start.13
  42.2 3.1 %collective-permute-done.10.refs_9_ = bf16[128,1024]{1,0:T(8,128)(2,1)S(1)} collective-permute-done((bf16[128,1024]{1,0:T(8,128)(2,1)S(1)}, bf16[128,1024]{1,0:T(8,128)(2,1)S(1)}, u32[]{:S(2)}, u32[]{:S(2)}) %collective-permute-start.10) | collective-permute-done | bytes 262176 | tf_op jit(solution)/shard_map/ppermute | solution.py:53
  45.4 3.3 %collective-permute-start.15 = (bf16[2,128,1024]{2,1,0:T(8,128)(2,1)S(1)}, bf16[2,128,1024]{2,1,0:T(8,128)(2,1)S(1)}, u32[]{:S(2)}, u32[]{:S(2)}) collective-permute-start(bf16[2,128,1024]{2,1,0:T(8,128)(2,1)S(1)} %pad_maximum_fusion.2), channel_id=1, source_target_pairs={{0,8},{4,36},{8,16},{12,44},{16,24},{20,52},{24,0},{28,60},{32,40}... | collective-permute-start | bytes 1572872 | tf_op jit(solution)/shard_map/ppermute | solution.py:53
  48.7 13.2 %collective-permute-done.15.refs_14_ = bf16[2,128,1024]{2,1,0:T(8,128)(2,1)S(1)} collective-permute-done((bf16[2,128,1024]{2,1,0:T(8,128)(2,1)S(1)}, bf16[2,128,1024]{2,1,0:T(8,128)(2,1)S(1)}, u32[]{:S(2)}, u32[]{:S(2)}) %collective-permute-start.15) | collective-permute-done | bytes 524320 | tf_op jit(solution)/shard_map/ppermute | solution.py:53
  61.9 5.1 %collective-permute-done.16.refs_15_ = bf16[2,128,1024]{2,1,0:T(8,128)(2,1)S(1)} collective-permute-done((bf16[2,128,1024]{2,1,0:T(8,128)(2,1)S(1)}, bf16[2,128,1024]{2,1,0:T(8,128)(2,1)S(1)}, u32[]{:S(2)}, u32[]{:S(2)}) %collective-permute-start.16) | collective-permute-done | bytes 524320 | tf_op jit(solution)/shard_map/ppermute | solution.py:53
  66.9 0.2 collective-permute-start.2
  67.2 1.0 collective-permute-start.19
  68.2 1.1 collective-permute-start.22
  69.3 4.3 %collective-permute-done.19.refs_18_ = bf16[128,1024]{1,0:T(8,128)(2,1)S(1)} collective-permute-done((bf16[128,1024]{1,0:T(8,128)(2,1)S(1)}, bf16[128,1024]{1,0:T(8,128)(2,1)S(1)}, u32[]{:S(2)}, u32[]{:S(2)}) %collective-permute-start.19) | collective-permute-done | bytes 262176 | tf_op jit(solution)/shard_map/ppermute | solution.py:53
  73.6 2.1 %collective-permute-start.18 = (bf16[2,128,1024]{2,1,0:T(8,128)(2,1)S(1)}, bf16[2,128,1024]{2,1,0:T(8,128)(2,1)S(1)}, u32[]{:S(2)}, u32[]{:S(2)}) collective-permute-start(bf16[2,128,1024]{2,1,0:T(8,128)(2,1)S(1)} %slice.47), channel_id=1, source_target_pairs={{0,8},{4,36},{8,16},{12,44},{16,24},{20,52},{24,0},{28,60},{32,40}... | collective-permute-start | bytes 1572872 | tf_op jit(solution)/shard_map/ppermute | solution.py:53
  75.7 7.2 %collective-permute-done.2.refs_1_ = bf16[2,512,512]{2,1,0:T(8,128)(2,1)S(1)} collective-permute-done((bf16[2,512,512]{2,1,0:T(8,128)(2,1)S(1)}, bf16[2,512,512]{2,1,0:T(8,128)(2,1)S(1)}, u32[]{:S(2)}, u32[]{:S(2)}) %collective-permute-start.2) | collective-permute-done | bytes 1048608 | tf_op jit(solution)/shard_map/ppermute | solution.py:64
  82.9 3.2 %collective-permute-done.21.refs_20_ = bf16[2,128,1024]{2,1,0:T(8,128)(2,1)S(1)} collective-permute-done((bf16[2,128,1024]{2,1,0:T(8,128)(2,1)S(1)}, bf16[2,128,1024]{2,1,0:T(8,128)(2,1)S(1)}, u32[]{:S(2)}, u32[]{:S(2)}) %collective-permute-start.21) | collective-permute-done | bytes 524320 | tf_op jit(solution)/shard_map/ppermute | solution.py:53
  86.1 9.5 %half_stage.5 = (bf16[4,512,512]{2,1,0:T(8,128)(2,1)S(1)}, f32[1,512]{1,0:T(1,128)S(1)}) custom-call(s32[1]{0:T(128)} %collective-permute-done.23.count, bf16[2,512,512]{2,1,0:T(8,128)(2,1)S(1)} %collective-permute-done.1.refs_0_, bf16[2,512,512]{2,1,0:T(8,128)(2,1)S(1)} %collective-permute-done.2.refs_1_, ...), custom_call_target="tpu_custom_call" | custom-call | tf_op jit(solution)/shard_map/half_stage/pallas_call | solution.py:254
  95.7 0.5 collective-permute-start.3
  96.2 5.1 %collective-permute-done.3.refs_2_ = bf16[2,512,512]{2,1,0:T(8,128)(2,1)S(1)} collective-permute-done((bf16[2,512,512]{2,1,0:T(8,128)(2,1)S(1)}, bf16[2,512,512]{2,1,0:T(8,128)(2,1)S(1)}, u32[]{:S(2)}, u32[]{:S(2)}) %collective-permute-start.3) | collective-permute-done | bytes 1048608 | tf_op jit(solution)/shard_map/ppermute | solution.py:49
  101.4 4.3 %half_stage.3 = (bf16[4,256,512]{2,1,0:T(8,128)(2,1)S(1)}, f32[1,512]{1,0:T(1,128)S(1)}) custom-call(s32[1]{0:T(128)S(6)} %copy.9.count, bf16[2,512,512]{2,1,0:T(8,128)(2,1)S(1)} %pick.1.refs_0_, bf16[2,512,512]{2,1,0:T(8,128)(2,1)S(1)} %collective-permute-done.refs_1_, bf16[2,512,512]{2,1,0:T(8,128)(2,1)S(1)} %collective-permute-done.3.refs_2_, ...), custom_call_target="tpu_custom_call" | custom-call | tf_op jit(solution)/shard_map/half_stage/pallas_call | solution.py:254
  105.7 4.7 %half_stage.4 = (bf16[4,256,512]{2,1,0:T(8,128)(2,1)S(1)}, f32[1,512]{1,0:T(1,128)S(1)}) custom-call(s32[1]{0:T(128)S(6)} %copy.9.count, bf16[2,512,512]{2,1,0:T(8,128)(2,1)S(1)} %pick.1.refs_0_, bf16[2,512,512]{2,1,0:T(8,128)(2,1)S(1)} %collective-permute-done.refs_1_, bf16[2,512,512]{2,1,0:T(8,128)(2,1)S(1)} %collective-permute-done.3.refs_2_, ...), custom_call_target="tpu_custom_call" | custom-call | tf_op jit(solution)/shard_map/half_stage/pallas_call | solution.py:254
  110.6 1.7 %collective-permute-start.32 = (bf16[256,512]{1,0:T(8,128)(2,1)S(1)}, bf16[256,512]{1,0:T(8,128)(2,1)S(1)}, u32[]{:S(2)}, u32[]{:S(2)}) collective-permute-start(bf16[256,512]{1,0:T(8,128)(2,1)S(1)} %get-tuple-element.21), channel_id=1, source_target_pairs={{0,1},{1,2},{2,3},{3,0},{4,5},{5,6},{6,7},{7,4},{8,9},{9,10},{10,1... | collective-permute-start | bytes 786440 | tf_op jit(solution)/shard_map/ppermute | solution.py:68
  112.3 0.1 merge.6
  112.4 1.7 %collective-permute-start.34 = (bf16[256,512]{1,0:T(8,128)(2,1)S(1)}, bf16[256,512]{1,0:T(8,128)(2,1)S(1)}, u32[]{:S(2)}, u32[]{:S(2)}) collective-permute-start(bf16[256,512]{1,0:T(8,128)(2,1)S(1)} %get-tuple-element.22), channel_id=1, source_target_pairs={{0,3},{1,0},{2,1},{3,2},{4,7},{5,4},{6,5},{7,6},{8,11},{9,8},{10,9... | collective-permute-start | bytes 786440 | tf_op jit(solution)/shard_map/ppermute | solution.py:68
  114.1 1.8 %collective-permute-start.36 = (bf16[256,512]{1,0:T(8,128)(2,1)S(1)}, bf16[256,512]{1,0:T(8,128)(2,1)S(1)}, u32[]{:S(2)}, u32[]{:S(2)}) collective-permute-start(bf16[256,512]{1,0:T(8,128)(2,1)S(1)} %get-tuple-element.23), channel_id=1, source_target_pairs={{0,3},{1,0},{2,1},{3,2},{4,7},{5,4},{6,5},{7,6},{8,11},{9,8},{10,9... | collective-permute-start | bytes 786440 | tf_op jit(solution)/shard_map/ppermute | solution.py:68
  115.9 0.2 collective-permute-start.37
  116.1 4.9 %collective-permute-done.32.refs_0_ = bf16[256,512]{1,0:T(8,128)(2,1)S(1)} collective-permute-done((bf16[256,512]{1,0:T(8,128)(2,1)S(1)}, bf16[256,512]{1,0:T(8,128)(2,1)S(1)}, u32[]{:S(2)}, u32[]{:S(2)}) %collective-permute-start.32) | collective-permute-done | bytes 262176 | tf_op jit(solution)/shard_map/ppermute | solution.py:68
  121.2 0.5 collective-permute-start.33
  121.8 2.9 %collective-permute-start.35 = (bf16[256,512]{1,0:T(8,128)(2,1)S(1)}, bf16[256,512]{1,0:T(8,128)(2,1)S(1)}, u32[]{:S(2)}, u32[]{:S(2)}) collective-permute-start(bf16[256,512]{1,0:T(8,128)(2,1)S(1)} %merge.7), channel_id=1, source_target_pairs={{0,3},{1,0},{2,1},{3,2},{4,7},{5,4},{6,5},{7,6},{8,11},{9,8},{10,9... | collective-permute-start | bytes 786440 | tf_op jit(solution)/shard_map/ppermute | solution.py:68
  124.7 1.2 collective-permute-done.27
  125.9 5.8 %collective-permute-done.29 = f32[1,512]{1,0:T(1,128)S(1)} collective-permute-done((f32[1,512]{1,0:T(1,128)S(1)}, f32[1,512]{1,0:T(1,128)S(1)}, u32[]{:S(2)}, u32[]{:S(2)}) %collective-permute-start.29) | collective-permute-done | bytes 2080 | tf_op jit(solution)/shard_map/ppermute | solution.py:68
  131.6 1.7 %collective-permute-start.30 = (f32[1,512]{1,0:T(1,128)S(1)}, f32[1,512]{1,0:T(1,128)S(1)}, u32[]{:S(2)}, u32[]{:S(2)}) collective-permute-start(f32[1,512]{1,0:T(1,128)S(1)} %add.24), channel_id=1, source_target_pairs={{0,3},{1,0},{2,1},{3,2},{4,7},{5,4},{6,5},{7,6},{8,11},{9,8},{10,9... | collective-permute-start | bytes 6152 | tf_op jit(solution)/shard_map/ppermute | solution.py:68
  133.4 1.8 %collective-permute-done.30 = f32[1,512]{1,0:T(1,128)S(1)} collective-permute-done((f32[1,512]{1,0:T(1,128)S(1)}, f32[1,512]{1,0:T(1,128)S(1)}, u32[]{:S(2)}, u32[]{:S(2)}) %collective-permute-start.30) | collective-permute-done | bytes 2080 | tf_op jit(solution)/shard_map/ppermute | solution.py:68
  135.2 1.2 collective-permute-start.28
  136.4 3.9 %collective-permute-done.28 = f32[1,512]{1,0:T(1,128)S(1)} collective-permute-done((f32[1,512]{1,0:T(1,128)S(1)}, f32[1,512]{1,0:T(1,128)S(1)}, u32[]{:S(2)}, u32[]{:S(2)}) %collective-permute-start.28) | collective-permute-done | bytes 2080 | tf_op jit(solution)/shard_map/ppermute | solution.py:68
  140.3 2.3 %marks.1 = (bf16[4096,512]{1,0:T(8,128)(2,1)S(1)}, f32[1,4096]{1,0:T(1,128)}) custom-call(s32[1]{0:T(128)S(6)} %copy.9.count, s32[1,512]{1,0:T(1,128)S(1)} %copy-done, f32[1,512]{1,0:T(1,128)S(1)} %add_add_fusion.scores), custom_call_target="tpu_custom_call" | custom-call | tf_op jit(solution)/shard_map/marks/pallas_call | solution.py:312
  142.6 3.3 %place.1 = bf16[4096,512]{1,0:T(8,128)(2,1)} custom-call(s32[1]{0:T(128)S(6)} %copy.9.count, bf16[4096,512]{1,0:T(8,128)(2,1)S(1)} %get-tuple-element.17.hot, bf16[4,256,512]{2,1,0:T(8,128)(2,1)S(1)} %get-tuple-element.18.own.own_a, bf16[4,256,512]{2,1,0:T(8,128)(2,1)S(1)} %get-tuple-element.19.own.own_b, ...), custom_call_target="tpu_custom_call" | custom-call | tf_op jit(solution)/shard_map/place/pallas_call | solution.py:347
  (66 shorter events, 1.6 us)
Async XLA Ops:
  0.6 12.1 %collective-permute-start.6 = (bf16[64,2048]{1,0:T(8,128)(2,1)}, bf16[64,2048]{1,0:T(8,128)(2,1)S(1)}, u32[]{:S(2)}, u32[]{:S(2)}) collective-permute-start(bf16[64,2048]{1,0:T(8,128)(2,1)} %bitcast.30), channel_id=1, source_target_pairs={{0,4},{4,0},{8,12},{12,8},{16,20},{20,16},{24,28},{28,24},{32,36},... | collective-permute-start | bytes 786440 | tf_op jit(solution)/shard_map/ppermute | solution.py:49
  1.4 9.0 %copy-start.3 = (bf16[64,2048]{1,0:T(8,128)(2,1)S(1)}, bf16[64,2048]{1,0:T(8,128)(2,1)}, u32[]{:S(2)}) copy-start(bf16[64,2048]{1,0:T(8,128)(2,1)} %param.12) | copy-start | bytes 786436
  1.4 11.4 %copy-start.2 = (bf16[2048,64]{0,1:T(8,128)(2,1)S(1)}, bf16[2048,64]{0,1:T(8,128)(2,1)}, u32[]{:S(2)}) copy-start(bf16[2048,64]{0,1:T(8,128)(2,1)} %param.13) | copy-start | bytes 786436
  1.4 16.1 %copy-start = (s32[1,512]{1,0:T(1,128)S(1)}, s32[1,512]{1,0:T(1,128)}, u32[]{:S(2)}) copy-start(s32[1,512]{1,0:T(1,128)} %idx.3) | copy-start | bytes 6148
  1.4 16.1 %copy-start.1 = (f32[4096]{0:T(1024)S(1)}, f32[4096]{0:T(1024)}, u32[]{:S(2)}) copy-start(f32[4096]{0:T(1024)} %param.9) | copy-start | bytes 49156
  8.4 20.3 %collective-permute-start = (bf16[2,512,512]{2,1,0:T(8,128)(2,1)S(1)}, bf16[2,512,512]{2,1,0:T(8,128)(2,1)S(1)}, u32[]{:S(2)}, u32[]{:S(2)}) collective-permute-start(bf16[2,512,512]{2,1,0:T(8,128)(2,1)S(1)} %pick.1.refs_0_), channel_id=1, source_target_pairs={{0,1},{4,7},{8,9},{12,15},{16,17},{20,23},{24,25},{28,31},{32,33},... | collective-permute-start | bytes 3145736 | tf_op jit(solution)/shard_map/ppermute | solution.py:64
  10.4 3.5 %collective-permute-start.5 = (bf16[64,2048]{1,0:T(8,128)(2,1)S(1)}, bf16[64,2048]{1,0:T(8,128)(2,1)S(1)}, u32[]{:S(2)}, u32[]{:S(2)}) collective-permute-start(bf16[64,2048]{1,0:T(8,128)(2,1)S(1)} %copy-done.3), channel_id=1, source_target_pairs={{0,4},{4,0},{8,12},{12,8},{16,20},{20,16},{24,28},{28,24},{32,36},... | collective-permute-start | bytes 786440 | tf_op jit(solution)/shard_map/ppermute | solution.py:49
  14.0 13.3 %collective-permute-start.7 = (bf16[2,128,1024]{2,1,0:T(8,128)(2,1)S(1)}, bf16[2,128,1024]{2,1,0:T(8,128)(2,1)S(1)}, u32[]{:S(2)}, u32[]{:S(2)}) collective-permute-start(bf16[2,128,1024]{2,1,0:T(8,128)(2,1)S(1)} %pad_maximum_fusion.1.refs_5_), channel_id=1, source_target_pairs={{0,32},{4,12},{8,40},{12,20},{16,48},{20,28},{24,56},{28,4},{32,64... | collective-permute-start | bytes 1572872 | tf_op jit(solution)/shard_map/ppermute | solution.py:53
  14.1 13.3 %collective-permute-start.8 = (bf16[2,128,1024]{2,1,0:T(8,128)(2,1)S(1)}, bf16[2,128,1024]{2,1,0:T(8,128)(2,1)S(1)}, u32[]{:S(2)}, u32[]{:S(2)}) collective-permute-start(bf16[2,128,1024]{2,1,0:T(8,128)(2,1)S(1)} %pad_maximum_fusion.1.refs_5_), channel_id=1, source_target_pairs={{0,96},{4,28},{8,104},{12,4},{16,112},{20,12},{24,120},{28,20},{32... | collective-permute-start | bytes 1572872 | tf_op jit(solution)/shard_map/ppermute | solution.py:53
  16.1 22.5 %collective-permute-start.1 = (bf16[2,512,512]{2,1,0:T(8,128)(2,1)S(1)}, bf16[2,512,512]{2,1,0:T(8,128)(2,1)S(1)}, u32[]{:S(2)}, u32[]{:S(2)}) collective-permute-start(bf16[2,512,512]{2,1,0:T(8,128)(2,1)S(1)} %pick.1.refs_0_), channel_id=1, source_target_pairs={{0,4},{4,0},{8,12},{12,8},{16,20},{20,16},{24,28},{28,24},{32,36},... | collective-permute-start | bytes 3145736 | tf_op jit(solution)/shard_map/ppermute | solution.py:49
  16.1 12.2 %collective-permute-start.11 = (bf16[2,128,1024]{2,1,0:T(8,128)(2,1)S(1)}, bf16[2,128,1024]{2,1,0:T(8,128)(2,1)S(1)}, u32[]{:S(2)}, u32[]{:S(2)}) collective-permute-start(bf16[2,128,1024]{2,1,0:T(8,128)(2,1)S(1)} %pad_maximum_fusion.1.refs_5_), channel_id=1, source_target_pairs={{0,8},{4,36},{8,16},{12,44},{16,24},{20,52},{24,0},{28,60},{32,40}... | collective-permute-start | bytes 1572872 | tf_op jit(solution)/shard_map/ppermute | solution.py:53
  27.3 10.4 %collective-permute-start.12 = (bf16[2,128,1024]{2,1,0:T(8,128)(2,1)S(1)}, bf16[2,128,1024]{2,1,0:T(8,128)(2,1)S(1)}, u32[]{:S(2)}, u32[]{:S(2)}) collective-permute-start(bf16[2,128,1024]{2,1,0:T(8,128)(2,1)S(1)} %pad_maximum_fusion.1.refs_5_), channel_id=1, source_target_pairs={{0,24},{4,100},{8,0},{12,108},{16,8},{20,116},{24,16},{28,124},{32... | collective-permute-start | bytes 1572872 | tf_op jit(solution)/shard_map/ppermute | solution.py:53
  27.4 1.5 %collective-permute-start.23 = (s32[1]{0:T(128)}, s32[1]{0:T(128)}, u32[]{:S(2)}, u32[]{:S(2)}) collective-permute-start(s32[1]{0:T(128)} %param.11), channel_id=1, source_target_pairs={{0,4},{4,0},{8,12},{12,8},{16,20},{20,16},{24,28},{28,24},{32,36},... | collective-permute-start | bytes 20 | tf_op jit(solution)/shard_map/ppermute | solution.py:49
  28.3 10.3 %collective-permute-start.26 = (f32[512,1]{1,0:T(8,128)S(1)}, f32[512,1]{1,0:T(8,128)S(1)}, u32[]{:S(2)}, u32[]{:S(2)}) collective-permute-start(f32[512,1]{1,0:T(8,128)S(1)} %scale.1.refs_4_), channel_id=1, source_target_pairs={{0,4},{4,0},{8,12},{12,8},{16,20},{20,16},{24,28},{28,24},{32,36},... | collective-permute-start | bytes 6152 | tf_op jit(solution)/shard_map/ppermute | solution.py:49
  28.7 38.4 %collective-permute-start.4 = (bf16[2,512,512]{2,1,0:T(8,128)(2,1)S(1)}, bf16[2,512,512]{2,1,0:T(8,128)(2,1)S(1)}, u32[]{:S(2)}, u32[]{:S(2)}) collective-permute-start(bf16[2,512,512]{2,1,0:T(8,128)(2,1)S(1)} %collective-permute-done.refs_1_), channel_id=1, source_target_pairs={{0,1},{4,7},{8,9},{12,15},{16,17},{20,23},{24,25},{28,31},{32,33},... | collective-permute-start | bytes 3145736 | tf_op jit(solution)/shard_map/ppermute | solution.py:64
  28.9 11.9 %collective-permute-start.9 = (bf16[128,1024]{1,0:T(8,128)(2,1)S(1)}, bf16[128,1024]{1,0:T(8,128)(2,1)S(1)}, u32[]{:S(2)}, u32[]{:S(2)}) collective-permute-start(bf16[128,1024]{1,0:T(8,128)(2,1)S(1)} %get-tuple-element.27), channel_id=1, source_target_pairs={{0,32},{4,12},{8,40},{12,20},{16,48},{20,28},{24,56},{28,4},{32,64... | collective-permute-start | bytes 786440 | tf_op jit(solution)/shard_map/ppermute | solution.py:53
  37.7 7.6 %collective-permute-start.10 = (bf16[128,1024]{1,0:T(8,128)(2,1)S(1)}, bf16[128,1024]{1,0:T(8,128)(2,1)S(1)}, u32[]{:S(2)}, u32[]{:S(2)}) collective-permute-start(bf16[128,1024]{1,0:T(8,128)(2,1)S(1)} %get-tuple-element.30), channel_id=1, source_target_pairs={{0,96},{4,28},{8,104},{12,4},{16,112},{20,12},{24,120},{28,20},{32... | collective-permute-start | bytes 786440 | tf_op jit(solution)/shard_map/ppermute | solution.py:53
  38.6 6.8 %collective-permute-start.17 = (bf16[128,1024]{1,0:T(8,128)(2,1)S(1)}, bf16[128,1024]{1,0:T(8,128)(2,1)S(1)}, u32[]{:S(2)}, u32[]{:S(2)}) collective-permute-start(bf16[128,1024]{1,0:T(8,128)(2,1)S(1)} %slice_bitcast_fusion.3), channel_id=1, source_target_pairs={{0,8},{4,36},{8,16},{12,44},{16,24},{20,52},{24,0},{28,60},{32,40}... | collective-permute-start | bytes 786440 | tf_op jit(solution)/shard_map/ppermute | solution.py:53
  38.7 10.0 %collective-permute-start.20 = (bf16[128,1024]{1,0:T(8,128)(2,1)S(1)}, bf16[128,1024]{1,0:T(8,128)(2,1)S(1)}, u32[]{:S(2)}, u32[]{:S(2)}) collective-permute-start(bf16[128,1024]{1,0:T(8,128)(2,1)S(1)} %slice_bitcast_fusion.1), channel_id=1, source_target_pairs={{0,24},{4,100},{8,0},{12,108},{16,8},{20,116},{24,16},{28,124},{32... | collective-permute-start | bytes 786440 | tf_op jit(solution)/shard_map/ppermute | solution.py:53
  40.8 26.3 %collective-permute-start.13 = (bf16[4,128,1024]{2,1,0:T(8,128)(2,1)S(1)}, bf16[4,128,1024]{2,1,0:T(8,128)(2,1)S(1)}, u32[]{:S(2)}, u32[]{:S(2)}) collective-permute-start(bf16[4,128,1024]{2,1,0:T(8,128)(2,1)S(1)} %pad_maximum_fusion), channel_id=1, source_target_pairs={{0,8},{4,36},{8,16},{12,44},{16,24},{20,52},{24,0},{28,60},{32,40}... | collective-permute-start | bytes 3145736 | tf_op jit(solution)/shard_map/ppermute | solution.py:53
  45.3 22.9 %collective-permute-start.14 = (bf16[4,128,1024]{2,1,0:T(8,128)(2,1)S(1)}, bf16[4,128,1024]{2,1,0:T(8,128)(2,1)S(1)}, u32[]{:S(2)}, u32[]{:S(2)}) collective-permute-start(bf16[4,128,1024]{2,1,0:T(8,128)(2,1)S(1)} %pad_maximum_fusion), channel_id=1, source_target_pairs={{0,24},{4,100},{8,0},{12,108},{16,8},{20,116},{24,16},{28,124},{32... | collective-permute-start | bytes 3145736 | tf_op jit(solution)/shard_map/ppermute | solution.py:53
  45.4 16.5 %collective-permute-start.15 = (bf16[2,128,1024]{2,1,0:T(8,128)(2,1)S(1)}, bf16[2,128,1024]{2,1,0:T(8,128)(2,1)S(1)}, u32[]{:S(2)}, u32[]{:S(2)}) collective-permute-start(bf16[2,128,1024]{2,1,0:T(8,128)(2,1)S(1)} %pad_maximum_fusion.2), channel_id=1, source_target_pairs={{0,8},{4,36},{8,16},{12,44},{16,24},{20,52},{24,0},{28,60},{32,40}... | collective-permute-start | bytes 1572872 | tf_op jit(solution)/shard_map/ppermute | solution.py:53
  48.7 18.3 %collective-permute-start.16 = (bf16[2,128,1024]{2,1,0:T(8,128)(2,1)S(1)}, bf16[2,128,1024]{2,1,0:T(8,128)(2,1)S(1)}, u32[]{:S(2)}, u32[]{:S(2)}) collective-permute-start(bf16[2,128,1024]{2,1,0:T(8,128)(2,1)S(1)} %pad_maximum_fusion.2), channel_id=1, source_target_pairs={{0,24},{4,100},{8,0},{12,108},{16,8},{20,116},{24,16},{28,124},{32... | collective-permute-start | bytes 1572872 | tf_op jit(solution)/shard_map/ppermute | solution.py:53
  61.9 21.1 %collective-permute-start.24 = (bf16[2,512,512]{2,1,0:T(8,128)(2,1)S(1)}, bf16[2,512,512]{2,1,0:T(8,128)(2,1)S(1)}, u32[]{:S(2)}, u32[]{:S(2)}) collective-permute-start(bf16[2,512,512]{2,1,0:T(8,128)(2,1)S(1)} %collective-permute-done.refs_1_), channel_id=1, source_target_pairs={{0,4},{4,0},{8,12},{12,8},{16,20},{20,16},{24,28},{28,24},{32,36},... | collective-permute-start | bytes 3145736 | tf_op jit(solution)/shard_map/ppermute | solution.py:49
  66.9 16.0 %collective-permute-start.2 = (bf16[2,512,512]{2,1,0:T(8,128)(2,1)S(1)}, bf16[2,512,512]{2,1,0:T(8,128)(2,1)S(1)}, u32[]{:S(2)}, u32[]{:S(2)}) collective-permute-start(bf16[2,512,512]{2,1,0:T(8,128)(2,1)S(1)} %collective-permute-done.1.refs_0_), channel_id=1, source_target_pairs={{0,1},{4,7},{8,9},{12,15},{16,17},{20,23},{24,25},{28,31},{32,33},... | collective-permute-start | bytes 3145736 | tf_op jit(solution)/shard_map/ppermute | solution.py:64
  67.1 19.0 %collective-permute-start.25 = (bf16[2,512,512]{2,1,0:T(8,128)(2,1)S(1)}, bf16[2,512,512]{2,1,0:T(8,128)(2,1)S(1)}, u32[]{:S(2)}, u32[]{:S(2)}) collective-permute-start(bf16[2,512,512]{2,1,0:T(8,128)(2,1)S(1)} %collective-permute-done.4.refs_3_), channel_id=1, source_target_pairs={{0,4},{4,0},{8,12},{12,8},{16,20},{20,16},{24,28},{28,24},{32,36},... | collective-permute-start | bytes 3145736 | tf_op jit(solution)/shard_map/ppermute | solution.py:49
  67.2 6.4 %collective-permute-start.19 = (bf16[128,1024]{1,0:T(8,128)(2,1)S(1)}, bf16[128,1024]{1,0:T(8,128)(2,1)S(1)}, u32[]{:S(2)}, u32[]{:S(2)}) collective-permute-start(bf16[128,1024]{1,0:T(8,128)(2,1)S(1)} %slice_bitcast_fusion.2), channel_id=1, source_target_pairs={{0,8},{4,36},{8,16},{12,44},{16,24},{20,52},{24,0},{28,60},{32,40}... | collective-permute-start | bytes 786440 | tf_op jit(solution)/shard_map/ppermute | solution.py:53
  68.2 7.6 %collective-permute-start.22 = (bf16[128,1024]{1,0:T(8,128)(2,1)S(1)}, bf16[128,1024]{1,0:T(8,128)(2,1)S(1)}, u32[]{:S(2)}, u32[]{:S(2)}) collective-permute-start(bf16[128,1024]{1,0:T(8,128)(2,1)S(1)} %slice_bitcast_fusion), channel_id=1, source_target_pairs={{0,24},{4,100},{8,0},{12,108},{16,8},{20,116},{24,16},{28,124},{32... | collective-permute-start | bytes 786440 | tf_op jit(solution)/shard_map/ppermute | solution.py:53
  73.6 9.3 %collective-permute-start.18 = (bf16[2,128,1024]{2,1,0:T(8,128)(2,1)S(1)}, bf16[2,128,1024]{2,1,0:T(8,128)(2,1)S(1)}, u32[]{:S(2)}, u32[]{:S(2)}) collective-permute-start(bf16[2,128,1024]{2,1,0:T(8,128)(2,1)S(1)} %slice.47), channel_id=1, source_target_pairs={{0,8},{4,36},{8,16},{12,44},{16,24},{20,52},{24,0},{28,60},{32,40}... | collective-permute-start | bytes 1572872 | tf_op jit(solution)/shard_map/ppermute | solution.py:53
  75.7 10.4 %collective-permute-start.21 = (bf16[2,128,1024]{2,1,0:T(8,128)(2,1)S(1)}, bf16[2,128,1024]{2,1,0:T(8,128)(2,1)S(1)}, u32[]{:S(2)}, u32[]{:S(2)}) collective-permute-start(bf16[2,128,1024]{2,1,0:T(8,128)(2,1)S(1)} %slice.50), channel_id=1, source_target_pairs={{0,24},{4,100},{8,0},{12,108},{16,8},{20,116},{24,16},{28,124},{32... | collective-permute-start | bytes 1572872 | tf_op jit(solution)/shard_map/ppermute | solution.py:53
  95.7 14.8 %collective-permute-start.31 = (bf16[4,512,512]{2,1,0:T(8,128)(2,1)S(1)}, bf16[4,512,512]{2,1,0:T(8,128)(2,1)S(1)}, u32[]{:S(2)}, u32[]{:S(2)}) collective-permute-start(bf16[4,512,512]{2,1,0:T(8,128)(2,1)S(1)} %get-tuple-element.20), channel_id=1, source_target_pairs={{0,4},{4,0},{8,12},{12,8},{16,20},{20,16},{24,28},{28,24},{32,36},... | collective-permute-start | bytes 6291464 | tf_op jit(solution)/shard_map/ppermute | solution.py:49
  95.7 5.6 %collective-permute-start.3 = (bf16[2,512,512]{2,1,0:T(8,128)(2,1)S(1)}, bf16[2,512,512]{2,1,0:T(8,128)(2,1)S(1)}, u32[]{:S(2)}, u32[]{:S(2)}) collective-permute-start(bf16[2,512,512]{2,1,0:T(8,128)(2,1)S(1)} %collective-permute-done.2.refs_1_), channel_id=1, source_target_pairs={{0,4},{4,0},{8,12},{12,8},{16,20},{20,16},{24,28},{28,24},{32,36},... | collective-permute-start | bytes 3145736 | tf_op jit(solution)/shard_map/ppermute | solution.py:49
  110.6 10.5 %collective-permute-start.32 = (bf16[256,512]{1,0:T(8,128)(2,1)S(1)}, bf16[256,512]{1,0:T(8,128)(2,1)S(1)}, u32[]{:S(2)}, u32[]{:S(2)}) collective-permute-start(bf16[256,512]{1,0:T(8,128)(2,1)S(1)} %get-tuple-element.21), channel_id=1, source_target_pairs={{0,1},{1,2},{2,3},{3,0},{4,5},{5,6},{6,7},{7,4},{8,9},{9,10},{10,1... | collective-permute-start | bytes 786440 | tf_op jit(solution)/shard_map/ppermute | solution.py:68
  112.4 9.2 %collective-permute-start.34 = (bf16[256,512]{1,0:T(8,128)(2,1)S(1)}, bf16[256,512]{1,0:T(8,128)(2,1)S(1)}, u32[]{:S(2)}, u32[]{:S(2)}) collective-permute-start(bf16[256,512]{1,0:T(8,128)(2,1)S(1)} %get-tuple-element.22), channel_id=1, source_target_pairs={{0,3},{1,0},{2,1},{3,2},{4,7},{5,4},{6,5},{7,6},{8,11},{9,8},{10,9... | collective-permute-start | bytes 786440 | tf_op jit(solution)/shard_map/ppermute | solution.py:68
  114.1 28.5 %collective-permute-start.36 = (bf16[256,512]{1,0:T(8,128)(2,1)S(1)}, bf16[256,512]{1,0:T(8,128)(2,1)S(1)}, u32[]{:S(2)}, u32[]{:S(2)}) collective-permute-start(bf16[256,512]{1,0:T(8,128)(2,1)S(1)} %get-tuple-element.23), channel_id=1, source_target_pairs={{0,3},{1,0},{2,1},{3,2},{4,7},{5,4},{6,5},{7,6},{8,11},{9,8},{10,9... | collective-permute-start | bytes 786440 | tf_op jit(solution)/shard_map/ppermute | solution.py:68
  115.9 26.7 %collective-permute-start.37 = (bf16[256,512]{1,0:T(8,128)(2,1)S(1)}, bf16[256,512]{1,0:T(8,128)(2,1)S(1)}, u32[]{:S(2)}, u32[]{:S(2)}) collective-permute-start(bf16[256,512]{1,0:T(8,128)(2,1)S(1)} %get-tuple-element.24), channel_id=1, source_target_pairs={{0,1},{1,2},{2,3},{3,0},{4,5},{5,6},{6,7},{7,4},{8,9},{9,10},{10,1... | collective-permute-start | bytes 786440 | tf_op jit(solution)/shard_map/ppermute | solution.py:68
  121.2 21.4 %collective-permute-start.33 = (bf16[256,512]{1,0:T(8,128)(2,1)S(1)}, bf16[256,512]{1,0:T(8,128)(2,1)S(1)}, u32[]{:S(2)}, u32[]{:S(2)}) collective-permute-start(bf16[256,512]{1,0:T(8,128)(2,1)S(1)} %merge.5), channel_id=1, source_target_pairs={{0,1},{1,2},{2,3},{3,0},{4,5},{5,6},{6,7},{7,4},{8,9},{9,10},{10,1... | collective-permute-start | bytes 786440 | tf_op jit(solution)/shard_map/ppermute | solution.py:68
  121.8 20.8 %collective-permute-start.35 = (bf16[256,512]{1,0:T(8,128)(2,1)S(1)}, bf16[256,512]{1,0:T(8,128)(2,1)S(1)}, u32[]{:S(2)}, u32[]{:S(2)}) collective-permute-start(bf16[256,512]{1,0:T(8,128)(2,1)S(1)} %merge.7), channel_id=1, source_target_pairs={{0,3},{1,0},{2,1},{3,2},{4,7},{5,4},{6,5},{7,6},{8,11},{9,8},{10,9... | collective-permute-start | bytes 786440 | tf_op jit(solution)/shard_map/ppermute | solution.py:68
  124.7 1.2 collective-permute-start.27
  125.9 5.8 %collective-permute-start.29 = (f32[1,512]{1,0:T(1,128)S(1)}, f32[1,512]{1,0:T(1,128)S(1)}, u32[]{:S(2)}, u32[]{:S(2)}) collective-permute-start(f32[1,512]{1,0:T(1,128)S(1)} %add.24), channel_id=1, source_target_pairs={{0,1},{1,2},{2,3},{3,0},{4,5},{5,6},{6,7},{7,4},{8,9},{9,10},{10,1... | collective-permute-start | bytes 6152 | tf_op jit(solution)/shard_map/ppermute | solution.py:68
  131.6 3.6 %collective-permute-start.30 = (f32[1,512]{1,0:T(1,128)S(1)}, f32[1,512]{1,0:T(1,128)S(1)}, u32[]{:S(2)}, u32[]{:S(2)}) collective-permute-start(f32[1,512]{1,0:T(1,128)S(1)} %add.24), channel_id=1, source_target_pairs={{0,3},{1,0},{2,1},{3,2},{4,7},{5,4},{6,5},{7,6},{8,11},{9,8},{10,9... | collective-permute-start | bytes 6152 | tf_op jit(solution)/shard_map/ppermute | solution.py:68
  135.2 5.1 %collective-permute-start.28 = (f32[1,512]{1,0:T(1,128)S(1)}, f32[1,512]{1,0:T(1,128)S(1)}, u32[]{:S(2)}, u32[]{:S(2)}) collective-permute-start(f32[1,512]{1,0:T(1,128)S(1)} %add.24), channel_id=1, source_target_pairs={{0,2},{1,3},{2,0},{3,1},{4,6},{5,7},{6,4},{7,5},{8,10},{9,11},{10,... | collective-permute-start | bytes 6152 | tf_op jit(solution)/shard_map/ppermute | solution.py:68

commit v4 on v3

--- a/solution.py
+++ b/solution.py
@@ -152,16 +152,15 @@
     )(count, *[off_chip(v) for v in (idx, inputs, out_grad)])
 
 
-def scale_kernel(count, idx, score, out):
-    column = jnp.broadcast_to(idx[...], (BLK, ROWS)).T
-    for r in range(ROWS // BLK):
-
-        @pl.when(r < count[0])
-        def _(r=r):
-            here = slice(r * BLK, (r + 1) * BLK)
-            at = jnp.broadcast_to(column[here, :1], (BLK, TOK))
-            same = lax.broadcasted_iota(jnp.int32, (BLK, TOK), 1) == at
-            out[here, :] = jnp.sum(jnp.where(same, score[...], 0.0), axis=1, keepdims=True)
+def scale_kernel(count, idx, score, out, column):
+    column[...] = jnp.broadcast_to(idx[...], (BLK, ROWS)).T
+
+    @pl.loop(0, count[0])
+    def _(r):
+        here = pl.ds(pl.multiple_of(r * BLK, BLK), BLK)
+        at = jnp.broadcast_to(column[here, :1], (BLK, TOK))
+        same = lax.broadcasted_iota(jnp.int32, (BLK, TOK), 1) == at
+        out[here, :] = jnp.sum(jnp.where(same, score[...], 0.0), axis=1, keepdims=True)
 
 
 def scale(count, idx, score):
@@ -169,6 +168,7 @@
         scale_kernel,
         in_specs=[SMEM, VMEM, VMEM],
         out_specs=VMEM,
+        scratch_shapes=[pltpu.VMEM((ROWS, BLK), jnp.int32)],
         out_shape=pltpu.VMEM((ROWS, 1), jnp.float32),
         compiler_params=params(8),
         name="scale",
@@ -322,41 +322,59 @@
     )(count, idx, scores)
 
 
-def place_kernel(count, hot, own_a, own_b, other, full_a, full_b, low_a, low_b, out, rows, done, sems):
-    mid = ROWS // 2
-    for at, own, parts in ((0, own_a, (full_a, low_a)), (mid, own_b, (full_b, low_b))):
-        here = pl.ds(at, mid)
-        total = own[3].astype(jnp.float32) + other[3, here, :].astype(jnp.float32)
-        for part in parts:
-            total = total + part[...].astype(jnp.float32)
-        at_row = lax.broadcasted_iota(jnp.int32, (mid, 512), 0) + at
-        total = jnp.where(at_row < count[0] * BLK, total, 0.0)
-        rows[here, :] = total.astype(jnp.bfloat16)
+def finished(count, at, own, other, full, low):
+    total = own[3].astype(jnp.float32) + other[3, at : at + TILE].astype(jnp.float32)
+    total = total + full[...].astype(jnp.float32) + low[...].astype(jnp.float32)
+    at_row = lax.broadcasted_iota(jnp.int32, (TILE, 512), 0) + at
+    return jnp.where(at_row < count[0] * BLK, total, 0.0).astype(jnp.bfloat16)
+
+
+def early_kernel(count, hot, own, other, full, low, held, rows):
+    rows[...] = finished(count, 0, own, other, full, low)
+    for t in range(TOK // ROWS):
+        here = pl.ds(t * ROWS, ROWS)
+        held[here, :] = DOT(hot[here, :TILE], rows[...], NN).astype(jnp.bfloat16)
+
+
+def place_kernel(count, hot, held, own, other, full, low, out, rows, done, sems):
+    rows[...] = finished(count, TILE, own, other, full, low)
     copies = []
     for t in range(TOK // ROWS):
         here = pl.ds(t * ROWS, ROWS)
-        done[here, :] = DOT(hot[here, :], rows[...], NN).astype(jnp.bfloat16)
+        total = DOT(hot[here, TILE:], rows[...], NN) + held[here, :].astype(jnp.float32)
+        done[here, :] = total.astype(jnp.bfloat16)
         copies.append(pltpu.make_async_copy(done.at[here], out.at[here], sems.at[t]))
         copies[-1].start()
     for copy in copies:
         copy.wait()
 
 
-def place(count, hot, own_a, own_b, other, full_a, full_b, low_a, low_b):
-    held = [on_chip(v) for v in (hot, own_a, own_b, other, full_a, full_b, low_a, low_b)]
+def early(count, *parts):
+    return pl.pallas_call(
+        early_kernel,
+        in_specs=[SMEM] + [VMEM] * 5,
+        out_specs=VMEM,
+        scratch_shapes=[pltpu.VMEM((TILE, 512), jnp.bfloat16)],
+        out_shape=pltpu.VMEM((TOK, 512), jnp.bfloat16),
+        compiler_params=params(4),
+        name="early",
+    )(count, *[on_chip(v) for v in parts])
+
+
+def place(count, *parts):
     return pl.pallas_call(
         place_kernel,
-        in_specs=[SMEM] + [VMEM] * 8,
+        in_specs=[SMEM] + [VMEM] * 6,
         out_specs=HBM,
         scratch_shapes=[
-            pltpu.VMEM((ROWS, 512), jnp.bfloat16),
+            pltpu.VMEM((TILE, 512), jnp.bfloat16),
             pltpu.VMEM((TOK, 512), jnp.bfloat16),
             pltpu.SemaphoreType.DMA((TOK // ROWS,)),
         ],
         out_shape=jax.ShapeDtypeStruct((TOK, 512), jnp.bfloat16),
         compiler_params=params(12),
         name="place",
-    )(count, *held)
+    )(count, *[on_chip(v) for v in parts])
 
 
 def branch(inputs, out_grad, router_score, route_index, block_count, w_in, w_out):
@@ -423,7 +441,8 @@
     (more_b,) = merge((2,), mid, o_b, other, through_b)
     full_a, full_b = zhop(more_a, 1), zhop(more_b, -1)
     hot, score_grad = marks(block_count, route_index, row_scores)
-    input_grad = place(block_count, hot, o_a, o_b, other, full_a, full_b, low_a, low_b)
+    held = early(block_count, hot, o_a, other, full_a, low_a)
+    input_grad = place(block_count, hot, held, o_b, other, full_b, low_b)
     return (input_grad, score_grad.reshape(router_score.shape))
 
 

time: 146 us -> 146 us (level)
  starting transfers between devices: 33.9 us -> 31.8 us
    ppermute x9, starting transfers between devices: 11.7 us -> 9.66 us  [zhop(): lax.ppermute(value, 'tensor', [(i, (i + step) % SIDE) for i in range(SIDE)])]
    pallas_call x1 -> x2, Pallas kernels: 3.34 us -> 3.87 us  [the longest x1 2.5 us: place(): pl.pallas_call(place_kernel, in_specs=[SMEM] + [VMEM] * 6, out_specs=HBM,...]
where the time goes in v4:
time: 146 us; the launch traced here: 145 us
  waiting for transfers between devices  78 us (53%)
  Pallas kernels  33.1 us (23%)
  starting transfers between devices  31.8 us (22%)
  between operations  1.81 us (1%)
    ppermute x16, waiting for transfers between devices, hop(): return lax.ppermute(value, 'seq', ring(step, phase))  45.6 us
    pallas_call x3, Pallas kernels, half_stage(): pl.pallas_call(functools.partial(half_kernel, tiles), in_specs=[SMEM] + [...  18.2 us
    ppermute x9, waiting for transfers between devices, zhop(): lax.ppermute(value, 'tensor', [(i, (i + step) % SIDE) for i in range(SIDE)])  17.7 us
    ppermute x16, starting transfers between devices, hop(): return lax.ppermute(value, 'seq', ring(step, phase))  16.5 us
    ppermute x9, starting transfers between devices, zhop(): lax.ppermute(value, 'tensor', [(i, (i + step) % SIDE) for i in range(SIDE)])  9.66 us
    ppermute x10, waiting for transfers between devices, swap(): return lax.ppermute(value, 'seq', SWAP)  7.54 us
    ppermute x3, waiting for transfers between devices, zdir(): return lax.ppermute(value, ('seq', 'tensor'), ZPAIRS)  7.2 us
    pallas_call x1, Pallas kernels, pick(): pl.pallas_call(pick_kernel, in_specs=[SMEM, HBM, HBM, HBM], out_specs=VME...  6.98 us
  transfers between devices with their start and end apart: 38, of which 17 were waited for; matrix products, arithmetic and copies ran while one was open for 0% of the time, Pallas kernels for 14%

profile of v4, /device:TPU:30, one launch (start us, length us, event | category | flops | bytes accessed | tf_op | source)
XLA Modules:
  0.0 145.5 jit_solution(798718223745978154)
XLA Ops:
  1.4 7.0 %pick.1.refs_0_ = bf16[2,512,512]{2,1,0:T(8,128)(2,1)S(1)} custom-call(s32[1]{0:T(128)S(6)} %copy.9.count, s32[1,512]{1,0:T(1,128)} %idx.3, bf16[4096,512]{1,0:T(8,128)(2,1)} %x_hbm.1, bf16[4096,512]{1,0:T(8,128)(2,1)} %g_hbm.1), custom_call_target="tpu_custom_call" | custom-call | tf_op jit(solution)/shard_map/pick/pallas_call | solution.py:138
  8.4 2.0 %collective-permute-start = (bf16[2,512,512]{2,1,0:T(8,128)(2,1)S(1)}, bf16[2,512,512]{2,1,0:T(8,128)(2,1)S(1)}, u32[]{:S(2)}, u32[]{:S(2)}) collective-permute-start(bf16[2,512,512]{2,1,0:T(8,128)(2,1)S(1)} %pick.1.refs_0_), channel_id=1, source_target_pairs={{0,1},{4,7},{8,9},{12,15},{16,17},{20,23},{24,25},{28,31},{32,33},... | collective-permute-start | bytes 3145736 | tf_op jit(solution)/shard_map/ppermute | solution.py:64
  10.4 2.3 %collective-permute-start.5 = (bf16[64,2048]{1,0:T(8,128)(2,1)S(1)}, bf16[64,2048]{1,0:T(8,128)(2,1)S(1)}, u32[]{:S(2)}, u32[]{:S(2)}) collective-permute-start(bf16[64,2048]{1,0:T(8,128)(2,1)S(1)} %copy-done.3), channel_id=1, source_target_pairs={{0,4},{4,0},{8,12},{12,8},{16,20},{20,16},{24,28},{28,24},{32,36},... | collective-permute-start | bytes 786440 | tf_op jit(solution)/shard_map/ppermute | solution.py:49
  12.9 1.0 collective-permute-done.5
  14.1 2.0 %collective-permute-start.8 = (bf16[2,128,1024]{2,1,0:T(8,128)(2,1)S(1)}, bf16[2,128,1024]{2,1,0:T(8,128)(2,1)S(1)}, u32[]{:S(2)}, u32[]{:S(2)}) collective-permute-start(bf16[2,128,1024]{2,1,0:T(8,128)(2,1)S(1)} %pad_maximum_fusion.1.refs_5_), channel_id=1, source_target_pairs={{0,96},{4,28},{8,104},{12,4},{16,112},{20,12},{24,120},{28,20},{32... | collective-permute-start | bytes 1572872 | tf_op jit(solution)/shard_map/ppermute | solution.py:53
  16.1 1.4 collective-permute-start.11
  17.5 1.3 scale.1.refs_4_
  18.9 8.5 %collective-permute-done.7.refs_6_ = bf16[2,128,1024]{2,1,0:T(8,128)(2,1)S(1)} collective-permute-done((bf16[2,128,1024]{2,1,0:T(8,128)(2,1)S(1)}, bf16[2,128,1024]{2,1,0:T(8,128)(2,1)S(1)}, u32[]{:S(2)}, u32[]{:S(2)}) %collective-permute-start.7) | collective-permute-done | bytes 524320 | tf_op jit(solution)/shard_map/ppermute | solution.py:53
  27.6 0.7 collective-permute-done.11.refs_10_
  28.3 0.4 collective-permute-start.26
  28.7 0.2 collective-permute-done.23.count
  28.9 1.2 collective-permute-start.9
  30.1 7.6 %collective-permute-done.12.refs_11_ = bf16[2,128,1024]{2,1,0:T(8,128)(2,1)S(1)} collective-permute-done((bf16[2,128,1024]{2,1,0:T(8,128)(2,1)S(1)}, bf16[2,128,1024]{2,1,0:T(8,128)(2,1)S(1)}, u32[]{:S(2)}, u32[]{:S(2)}) %collective-permute-start.12) | collective-permute-done | bytes 524320 | tf_op jit(solution)/shard_map/ppermute | solution.py:53
  37.7 0.8 collective-permute-start.10
  38.7 2.0 %collective-permute-start.20 = (bf16[128,1024]{1,0:T(8,128)(2,1)S(1)}, bf16[128,1024]{1,0:T(8,128)(2,1)S(1)}, u32[]{:S(2)}, u32[]{:S(2)}) collective-permute-start(bf16[128,1024]{1,0:T(8,128)(2,1)S(1)} %slice_bitcast_fusion.1), channel_id=1, source_target_pairs={{0,24},{4,100},{8,0},{12,108},{16,8},{20,116},{24,16},{28,124},{32... | collective-permute-start | bytes 786440 | tf_op jit(solution)/shard_map/ppermute | solution.py:53
  40.8 1.4 collective-permute-start.13
  42.2 3.1 %collective-permute-done.10.refs_9_ = bf16[128,1024]{1,0:T(8,128)(2,1)S(1)} collective-permute-done((bf16[128,1024]{1,0:T(8,128)(2,1)S(1)}, bf16[128,1024]{1,0:T(8,128)(2,1)S(1)}, u32[]{:S(2)}, u32[]{:S(2)}) %collective-permute-start.10) | collective-permute-done | bytes 262176 | tf_op jit(solution)/shard_map/ppermute | solution.py:53
  45.4 3.3 %collective-permute-start.15 = (bf16[2,128,1024]{2,1,0:T(8,128)(2,1)S(1)}, bf16[2,128,1024]{2,1,0:T(8,128)(2,1)S(1)}, u32[]{:S(2)}, u32[]{:S(2)}) collective-permute-start(bf16[2,128,1024]{2,1,0:T(8,128)(2,1)S(1)} %pad_maximum_fusion.2), channel_id=1, source_target_pairs={{0,8},{4,36},{8,16},{12,44},{16,24},{20,52},{24,0},{28,60},{32,40}... | collective-permute-start | bytes 1572872 | tf_op jit(solution)/shard_map/ppermute | solution.py:53
  48.7 13.2 %collective-permute-done.15.refs_14_ = bf16[2,128,1024]{2,1,0:T(8,128)(2,1)S(1)} collective-permute-done((bf16[2,128,1024]{2,1,0:T(8,128)(2,1)S(1)}, bf16[2,128,1024]{2,1,0:T(8,128)(2,1)S(1)}, u32[]{:S(2)}, u32[]{:S(2)}) %collective-permute-start.15) | collective-permute-done | bytes 524320 | tf_op jit(solution)/shard_map/ppermute | solution.py:53
  61.9 5.1 %collective-permute-done.16.refs_15_ = bf16[2,128,1024]{2,1,0:T(8,128)(2,1)S(1)} collective-permute-done((bf16[2,128,1024]{2,1,0:T(8,128)(2,1)S(1)}, bf16[2,128,1024]{2,1,0:T(8,128)(2,1)S(1)}, u32[]{:S(2)}, u32[]{:S(2)}) %collective-permute-start.16) | collective-permute-done | bytes 524320 | tf_op jit(solution)/shard_map/ppermute | solution.py:53
  66.9 0.2 collective-permute-start.2
  67.1 1.0 collective-permute-start.19
  68.2 1.1 collective-permute-start.22
  69.3 4.3 %collective-permute-done.19.refs_18_ = bf16[128,1024]{1,0:T(8,128)(2,1)S(1)} collective-permute-done((bf16[128,1024]{1,0:T(8,128)(2,1)S(1)}, bf16[128,1024]{1,0:T(8,128)(2,1)S(1)}, u32[]{:S(2)}, u32[]{:S(2)}) %collective-permute-start.19) | collective-permute-done | bytes 262176 | tf_op jit(solution)/shard_map/ppermute | solution.py:53
  73.6 2.1 %collective-permute-start.18 = (bf16[2,128,1024]{2,1,0:T(8,128)(2,1)S(1)}, bf16[2,128,1024]{2,1,0:T(8,128)(2,1)S(1)}, u32[]{:S(2)}, u32[]{:S(2)}) collective-permute-start(bf16[2,128,1024]{2,1,0:T(8,128)(2,1)S(1)} %slice.47), channel_id=1, source_target_pairs={{0,8},{4,36},{8,16},{12,44},{16,24},{20,52},{24,0},{28,60},{32,40}... | collective-permute-start | bytes 1572872 | tf_op jit(solution)/shard_map/ppermute | solution.py:53
  75.7 7.2 %collective-permute-done.2.refs_1_ = bf16[2,512,512]{2,1,0:T(8,128)(2,1)S(1)} collective-permute-done((bf16[2,512,512]{2,1,0:T(8,128)(2,1)S(1)}, bf16[2,512,512]{2,1,0:T(8,128)(2,1)S(1)}, u32[]{:S(2)}, u32[]{:S(2)}) %collective-permute-start.2) | collective-permute-done | bytes 1048608 | tf_op jit(solution)/shard_map/ppermute | solution.py:64
  82.9 3.2 %collective-permute-done.21.refs_20_ = bf16[2,128,1024]{2,1,0:T(8,128)(2,1)S(1)} collective-permute-done((bf16[2,128,1024]{2,1,0:T(8,128)(2,1)S(1)}, bf16[2,128,1024]{2,1,0:T(8,128)(2,1)S(1)}, u32[]{:S(2)}, u32[]{:S(2)}) %collective-permute-start.21) | collective-permute-done | bytes 524320 | tf_op jit(solution)/shard_map/ppermute | solution.py:53
  86.1 9.5 %half_stage.5 = (bf16[4,512,512]{2,1,0:T(8,128)(2,1)S(1)}, f32[1,512]{1,0:T(1,128)S(1)}) custom-call(s32[1]{0:T(128)} %collective-permute-done.23.count, bf16[2,512,512]{2,1,0:T(8,128)(2,1)S(1)} %collective-permute-done.1.refs_0_, bf16[2,512,512]{2,1,0:T(8,128)(2,1)S(1)} %collective-permute-done.2.refs_1_, ...), custom_call_target="tpu_custom_call" | custom-call | tf_op jit(solution)/shard_map/half_stage/pallas_call | solution.py:254
  95.7 0.5 collective-permute-start.3
  96.2 5.1 %collective-permute-done.3.refs_2_ = bf16[2,512,512]{2,1,0:T(8,128)(2,1)S(1)} collective-permute-done((bf16[2,512,512]{2,1,0:T(8,128)(2,1)S(1)}, bf16[2,512,512]{2,1,0:T(8,128)(2,1)S(1)}, u32[]{:S(2)}, u32[]{:S(2)}) %collective-permute-start.3) | collective-permute-done | bytes 1048608 | tf_op jit(solution)/shard_map/ppermute | solution.py:49
  101.4 4.4 %half_stage.3 = (bf16[4,256,512]{2,1,0:T(8,128)(2,1)S(1)}, f32[1,512]{1,0:T(1,128)S(1)}) custom-call(s32[1]{0:T(128)S(6)} %copy.9.count, bf16[2,512,512]{2,1,0:T(8,128)(2,1)S(1)} %pick.1.refs_0_, bf16[2,512,512]{2,1,0:T(8,128)(2,1)S(1)} %collective-permute-done.refs_1_, bf16[2,512,512]{2,1,0:T(8,128)(2,1)S(1)} %collective-permute-done.3.refs_2_, ...), custom_call_target="tpu_custom_call" | custom-call | tf_op jit(solution)/shard_map/half_stage/pallas_call | solution.py:254
  105.9 1.7 %collective-permute-start.32 = (bf16[256,512]{1,0:T(8,128)(2,1)S(1)}, bf16[256,512]{1,0:T(8,128)(2,1)S(1)}, u32[]{:S(2)}, u32[]{:S(2)}) collective-permute-start(bf16[256,512]{1,0:T(8,128)(2,1)S(1)} %get-tuple-element.20), channel_id=1, source_target_pairs={{0,1},{1,2},{2,3},{3,0},{4,5},{5,6},{6,7},{7,4},{8,9},{9,10},{10,1... | collective-permute-start | bytes 786440 | tf_op jit(solution)/shard_map/ppermute | solution.py:68
  107.6 4.4 %half_stage.4 = (bf16[4,256,512]{2,1,0:T(8,128)(2,1)S(1)}, f32[1,512]{1,0:T(1,128)S(1)}) custom-call(s32[1]{0:T(128)S(6)} %copy.9.count, bf16[2,512,512]{2,1,0:T(8,128)(2,1)S(1)} %pick.1.refs_0_, bf16[2,512,512]{2,1,0:T(8,128)(2,1)S(1)} %collective-permute-done.refs_1_, bf16[2,512,512]{2,1,0:T(8,128)(2,1)S(1)} %collective-permute-done.3.refs_2_, ...), custom_call_target="tpu_custom_call" | custom-call | tf_op jit(solution)/shard_map/half_stage/pallas_call | solution.py:254
  112.1 1.8 %collective-permute-start.35 = (bf16[256,512]{1,0:T(8,128)(2,1)S(1)}, bf16[256,512]{1,0:T(8,128)(2,1)S(1)}, u32[]{:S(2)}, u32[]{:S(2)}) collective-permute-start(bf16[256,512]{1,0:T(8,128)(2,1)S(1)} %get-tuple-element.23), channel_id=1, source_target_pairs={{0,3},{1,0},{2,1},{3,2},{4,7},{5,4},{6,5},{7,6},{8,11},{9,8},{10,9... | collective-permute-start | bytes 786440 | tf_op jit(solution)/shard_map/ppermute | solution.py:68
  113.9 1.7 %collective-permute-start.34 = (bf16[256,512]{1,0:T(8,128)(2,1)S(1)}, bf16[256,512]{1,0:T(8,128)(2,1)S(1)}, u32[]{:S(2)}, u32[]{:S(2)}) collective-permute-start(bf16[256,512]{1,0:T(8,128)(2,1)S(1)} %get-tuple-element.21), channel_id=1, source_target_pairs={{0,3},{1,0},{2,1},{3,2},{4,7},{5,4},{6,5},{7,6},{8,11},{9,8},{10,9... | collective-permute-start | bytes 786440 | tf_op jit(solution)/shard_map/ppermute | solution.py:68
  115.7 0.4 collective-permute-start.33
  116.1 0.4 collective-permute-start.37
  116.5 4.9 %collective-permute-done.35.refs_0_ = bf16[256,512]{1,0:T(8,128)(2,1)S(1)} collective-permute-done((bf16[256,512]{1,0:T(8,128)(2,1)S(1)}, bf16[256,512]{1,0:T(8,128)(2,1)S(1)}, u32[]{:S(2)}, u32[]{:S(2)}) %collective-permute-start.35) | collective-permute-done | bytes 262176 | tf_op jit(solution)/shard_map/ppermute | solution.py:68
  121.4 3.1 %collective-permute-start.36 = (bf16[256,512]{1,0:T(8,128)(2,1)S(1)}, bf16[256,512]{1,0:T(8,128)(2,1)S(1)}, u32[]{:S(2)}, u32[]{:S(2)}) collective-permute-start(bf16[256,512]{1,0:T(8,128)(2,1)S(1)} %merge.7), channel_id=1, source_target_pairs={{0,3},{1,0},{2,1},{3,2},{4,7},{5,4},{6,5},{7,6},{8,11},{9,8},{10,9... | collective-permute-start | bytes 786440 | tf_op jit(solution)/shard_map/ppermute | solution.py:68
  124.5 1.2 collective-permute-done.27
  125.6 4.8 %collective-permute-done.29 = f32[1,512]{1,0:T(1,128)S(1)} collective-permute-done((f32[1,512]{1,0:T(1,128)S(1)}, f32[1,512]{1,0:T(1,128)S(1)}, u32[]{:S(2)}, u32[]{:S(2)}) %collective-permute-start.29) | collective-permute-done | bytes 2080 | tf_op jit(solution)/shard_map/ppermute | solution.py:68
  130.4 0.3 collective-permute-start.30
  130.7 3.3 %collective-permute-done.30 = f32[1,512]{1,0:T(1,128)S(1)} collective-permute-done((f32[1,512]{1,0:T(1,128)S(1)}, f32[1,512]{1,0:T(1,128)S(1)}, u32[]{:S(2)}, u32[]{:S(2)}) %collective-permute-start.30) | collective-permute-done | bytes 2080 | tf_op jit(solution)/shard_map/ppermute | solution.py:68
  134.0 0.4 collective-permute-start.28
  134.4 4.7 %collective-permute-done.28 = f32[1,512]{1,0:T(1,128)S(1)} collective-permute-done((f32[1,512]{1,0:T(1,128)S(1)}, f32[1,512]{1,0:T(1,128)S(1)}, u32[]{:S(2)}, u32[]{:S(2)}) %collective-permute-start.28) | collective-permute-done | bytes 2080 | tf_op jit(solution)/shard_map/ppermute | solution.py:68
  139.1 2.3 %marks.1 = (bf16[4096,512]{1,0:T(8,128)(2,1)S(1)}, f32[1,4096]{1,0:T(1,128)}) custom-call(s32[1]{0:T(128)S(6)} %copy.9.count, s32[1,512]{1,0:T(1,128)S(1)} %copy-done, f32[1,512]{1,0:T(1,128)S(1)} %add_add_fusion.scores), custom_call_target="tpu_custom_call" | custom-call | tf_op jit(solution)/shard_map/marks/pallas_call | solution.py:312
  141.4 1.4 early.1.held
  142.8 2.5 %place.1 = bf16[4096,512]{1,0:T(8,128)(2,1)} custom-call(s32[1]{0:T(128)S(6)} %copy.9.count, bf16[4096,512]{1,0:T(8,128)(2,1)S(1)} %get-tuple-element.17.hot, bf16[4096,512]{1,0:T(8,128)(2,1)S(1)} %early.1.held, bf16[4,256,512]{2,1,0:T(8,128)(2,1)S(1)} %get-tuple-element.22.own, bf16[4,512,512]{2,1,0:T(8,128)(2,1)S(1)} %collective-permute-done.31.other, ...), custom_call_target="tpu_custom_call" | custom-call | tf_op jit(solution)/shard_map/place/pallas_call | solution.py:365
  (67 shorter events, 1.7 us)
Async XLA Ops:
  0.6 12.1 %collective-permute-start.6 = (bf16[64,2048]{1,0:T(8,128)(2,1)}, bf16[64,2048]{1,0:T(8,128)(2,1)S(1)}, u32[]{:S(2)}, u32[]{:S(2)}) collective-permute-start(bf16[64,2048]{1,0:T(8,128)(2,1)} %bitcast.30), channel_id=1, source_target_pairs={{0,4},{4,0},{8,12},{12,8},{16,20},{20,16},{24,28},{28,24},{32,36},... | collective-permute-start | bytes 786440 | tf_op jit(solution)/shard_map/ppermute | solution.py:49
  1.4 9.0 %copy-start.3 = (bf16[64,2048]{1,0:T(8,128)(2,1)S(1)}, bf16[64,2048]{1,0:T(8,128)(2,1)}, u32[]{:S(2)}) copy-start(bf16[64,2048]{1,0:T(8,128)(2,1)} %param.12) | copy-start | bytes 786436
  1.4 11.4 %copy-start.2 = (bf16[2048,64]{0,1:T(8,128)(2,1)S(1)}, bf16[2048,64]{0,1:T(8,128)(2,1)}, u32[]{:S(2)}) copy-start(bf16[2048,64]{0,1:T(8,128)(2,1)} %param.13) | copy-start | bytes 786436
  1.4 16.1 %copy-start = (s32[1,512]{1,0:T(1,128)S(1)}, s32[1,512]{1,0:T(1,128)}, u32[]{:S(2)}) copy-start(s32[1,512]{1,0:T(1,128)} %idx.3) | copy-start | bytes 6148
  1.4 16.1 %copy-start.1 = (f32[4096]{0:T(1024)S(1)}, f32[4096]{0:T(1024)}, u32[]{:S(2)}) copy-start(f32[4096]{0:T(1024)} %param.9) | copy-start | bytes 49156
  8.4 20.3 %collective-permute-start = (bf16[2,512,512]{2,1,0:T(8,128)(2,1)S(1)}, bf16[2,512,512]{2,1,0:T(8,128)(2,1)S(1)}, u32[]{:S(2)}, u32[]{:S(2)}) collective-permute-start(bf16[2,512,512]{2,1,0:T(8,128)(2,1)S(1)} %pick.1.refs_0_), channel_id=1, source_target_pairs={{0,1},{4,7},{8,9},{12,15},{16,17},{20,23},{24,25},{28,31},{32,33},... | collective-permute-start | bytes 3145736 | tf_op jit(solution)/shard_map/ppermute | solution.py:64
  10.4 3.5 %collective-permute-start.5 = (bf16[64,2048]{1,0:T(8,128)(2,1)S(1)}, bf16[64,2048]{1,0:T(8,128)(2,1)S(1)}, u32[]{:S(2)}, u32[]{:S(2)}) collective-permute-start(bf16[64,2048]{1,0:T(8,128)(2,1)S(1)} %copy-done.3), channel_id=1, source_target_pairs={{0,4},{4,0},{8,12},{12,8},{16,20},{20,16},{24,28},{28,24},{32,36},... | collective-permute-start | bytes 786440 | tf_op jit(solution)/shard_map/ppermute | solution.py:49
  14.0 13.3 %collective-permute-start.7 = (bf16[2,128,1024]{2,1,0:T(8,128)(2,1)S(1)}, bf16[2,128,1024]{2,1,0:T(8,128)(2,1)S(1)}, u32[]{:S(2)}, u32[]{:S(2)}) collective-permute-start(bf16[2,128,1024]{2,1,0:T(8,128)(2,1)S(1)} %pad_maximum_fusion.1.refs_5_), channel_id=1, source_target_pairs={{0,32},{4,12},{8,40},{12,20},{16,48},{20,28},{24,56},{28,4},{32,64... | collective-permute-start | bytes 1572872 | tf_op jit(solution)/shard_map/ppermute | solution.py:53
  14.1 13.3 %collective-permute-start.8 = (bf16[2,128,1024]{2,1,0:T(8,128)(2,1)S(1)}, bf16[2,128,1024]{2,1,0:T(8,128)(2,1)S(1)}, u32[]{:S(2)}, u32[]{:S(2)}) collective-permute-start(bf16[2,128,1024]{2,1,0:T(8,128)(2,1)S(1)} %pad_maximum_fusion.1.refs_5_), channel_id=1, source_target_pairs={{0,96},{4,28},{8,104},{12,4},{16,112},{20,12},{24,120},{28,20},{32... | collective-permute-start | bytes 1572872 | tf_op jit(solution)/shard_map/ppermute | solution.py:53
  16.1 22.5 %collective-permute-start.1 = (bf16[2,512,512]{2,1,0:T(8,128)(2,1)S(1)}, bf16[2,512,512]{2,1,0:T(8,128)(2,1)S(1)}, u32[]{:S(2)}, u32[]{:S(2)}) collective-permute-start(bf16[2,512,512]{2,1,0:T(8,128)(2,1)S(1)} %pick.1.refs_0_), channel_id=1, source_target_pairs={{0,4},{4,0},{8,12},{12,8},{16,20},{20,16},{24,28},{28,24},{32,36},... | collective-permute-start | bytes 3145736 | tf_op jit(solution)/shard_map/ppermute | solution.py:49
  16.1 12.2 %collective-permute-start.11 = (bf16[2,128,1024]{2,1,0:T(8,128)(2,1)S(1)}, bf16[2,128,1024]{2,1,0:T(8,128)(2,1)S(1)}, u32[]{:S(2)}, u32[]{:S(2)}) collective-permute-start(bf16[2,128,1024]{2,1,0:T(8,128)(2,1)S(1)} %pad_maximum_fusion.1.refs_5_), channel_id=1, source_target_pairs={{0,8},{4,36},{8,16},{12,44},{16,24},{20,52},{24,0},{28,60},{32,40}... | collective-permute-start | bytes 1572872 | tf_op jit(solution)/shard_map/ppermute | solution.py:53
  27.3 10.4 %collective-permute-start.12 = (bf16[2,128,1024]{2,1,0:T(8,128)(2,1)S(1)}, bf16[2,128,1024]{2,1,0:T(8,128)(2,1)S(1)}, u32[]{:S(2)}, u32[]{:S(2)}) collective-permute-start(bf16[2,128,1024]{2,1,0:T(8,128)(2,1)S(1)} %pad_maximum_fusion.1.refs_5_), channel_id=1, source_target_pairs={{0,24},{4,100},{8,0},{12,108},{16,8},{20,116},{24,16},{28,124},{32... | collective-permute-start | bytes 1572872 | tf_op jit(solution)/shard_map/ppermute | solution.py:53
  27.4 1.5 %collective-permute-start.23 = (s32[1]{0:T(128)}, s32[1]{0:T(128)}, u32[]{:S(2)}, u32[]{:S(2)}) collective-permute-start(s32[1]{0:T(128)} %param.11), channel_id=1, source_target_pairs={{0,4},{4,0},{8,12},{12,8},{16,20},{20,16},{24,28},{28,24},{32,36},... | collective-permute-start | bytes 20 | tf_op jit(solution)/shard_map/ppermute | solution.py:49
  28.3 10.3 %collective-permute-start.26 = (f32[512,1]{1,0:T(8,128)S(1)}, f32[512,1]{1,0:T(8,128)S(1)}, u32[]{:S(2)}, u32[]{:S(2)}) collective-permute-start(f32[512,1]{1,0:T(8,128)S(1)} %scale.1.refs_4_), channel_id=1, source_target_pairs={{0,4},{4,0},{8,12},{12,8},{16,20},{20,16},{24,28},{28,24},{32,36},... | collective-permute-start | bytes 6152 | tf_op jit(solution)/shard_map/ppermute | solution.py:49
  28.7 38.4 %collective-permute-start.4 = (bf16[2,512,512]{2,1,0:T(8,128)(2,1)S(1)}, bf16[2,512,512]{2,1,0:T(8,128)(2,1)S(1)}, u32[]{:S(2)}, u32[]{:S(2)}) collective-permute-start(bf16[2,512,512]{2,1,0:T(8,128)(2,1)S(1)} %collective-permute-done.refs_1_), channel_id=1, source_target_pairs={{0,1},{4,7},{8,9},{12,15},{16,17},{20,23},{24,25},{28,31},{32,33},... | collective-permute-start | bytes 3145736 | tf_op jit(solution)/shard_map/ppermute | solution.py:64
  28.9 11.9 %collective-permute-start.9 = (bf16[128,1024]{1,0:T(8,128)(2,1)S(1)}, bf16[128,1024]{1,0:T(8,128)(2,1)S(1)}, u32[]{:S(2)}, u32[]{:S(2)}) collective-permute-start(bf16[128,1024]{1,0:T(8,128)(2,1)S(1)} %get-tuple-element.27), channel_id=1, source_target_pairs={{0,32},{4,12},{8,40},{12,20},{16,48},{20,28},{24,56},{28,4},{32,64... | collective-permute-start | bytes 786440 | tf_op jit(solution)/shard_map/ppermute | solution.py:53
  37.7 7.6 %collective-permute-start.10 = (bf16[128,1024]{1,0:T(8,128)(2,1)S(1)}, bf16[128,1024]{1,0:T(8,128)(2,1)S(1)}, u32[]{:S(2)}, u32[]{:S(2)}) collective-permute-start(bf16[128,1024]{1,0:T(8,128)(2,1)S(1)} %get-tuple-element.30), channel_id=1, source_target_pairs={{0,96},{4,28},{8,104},{12,4},{16,112},{20,12},{24,120},{28,20},{32... | collective-permute-start | bytes 786440 | tf_op jit(solution)/shard_map/ppermute | solution.py:53
  38.6 6.8 %collective-permute-start.17 = (bf16[128,1024]{1,0:T(8,128)(2,1)S(1)}, bf16[128,1024]{1,0:T(8,128)(2,1)S(1)}, u32[]{:S(2)}, u32[]{:S(2)}) collective-permute-start(bf16[128,1024]{1,0:T(8,128)(2,1)S(1)} %slice_bitcast_fusion.3), channel_id=1, source_target_pairs={{0,8},{4,36},{8,16},{12,44},{16,24},{20,52},{24,0},{28,60},{32,40}... | collective-permute-start | bytes 786440 | tf_op jit(solution)/shard_map/ppermute | solution.py:53
  38.7 10.0 %collective-permute-start.20 = (bf16[128,1024]{1,0:T(8,128)(2,1)S(1)}, bf16[128,1024]{1,0:T(8,128)(2,1)S(1)}, u32[]{:S(2)}, u32[]{:S(2)}) collective-permute-start(bf16[128,1024]{1,0:T(8,128)(2,1)S(1)} %slice_bitcast_fusion.1), channel_id=1, source_target_pairs={{0,24},{4,100},{8,0},{12,108},{16,8},{20,116},{24,16},{28,124},{32... | collective-permute-start | bytes 786440 | tf_op jit(solution)/shard_map/ppermute | solution.py:53
  40.8 26.3 %collective-permute-start.13 = (bf16[4,128,1024]{2,1,0:T(8,128)(2,1)S(1)}, bf16[4,128,1024]{2,1,0:T(8,128)(2,1)S(1)}, u32[]{:S(2)}, u32[]{:S(2)}) collective-permute-start(bf16[4,128,1024]{2,1,0:T(8,128)(2,1)S(1)} %pad_maximum_fusion), channel_id=1, source_target_pairs={{0,8},{4,36},{8,16},{12,44},{16,24},{20,52},{24,0},{28,60},{32,40}... | collective-permute-start | bytes 3145736 | tf_op jit(solution)/shard_map/ppermute | solution.py:53
  45.3 22.9 %collective-permute-start.14 = (bf16[4,128,1024]{2,1,0:T(8,128)(2,1)S(1)}, bf16[4,128,1024]{2,1,0:T(8,128)(2,1)S(1)}, u32[]{:S(2)}, u32[]{:S(2)}) collective-permute-start(bf16[4,128,1024]{2,1,0:T(8,128)(2,1)S(1)} %pad_maximum_fusion), channel_id=1, source_target_pairs={{0,24},{4,100},{8,0},{12,108},{16,8},{20,116},{24,16},{28,124},{32... | collective-permute-start | bytes 3145736 | tf_op jit(solution)/shard_map/ppermute | solution.py:53
  45.4 16.5 %collective-permute-start.15 = (bf16[2,128,1024]{2,1,0:T(8,128)(2,1)S(1)}, bf16[2,128,1024]{2,1,0:T(8,128)(2,1)S(1)}, u32[]{:S(2)}, u32[]{:S(2)}) collective-permute-start(bf16[2,128,1024]{2,1,0:T(8,128)(2,1)S(1)} %pad_maximum_fusion.2), channel_id=1, source_target_pairs={{0,8},{4,36},{8,16},{12,44},{16,24},{20,52},{24,0},{28,60},{32,40}... | collective-permute-start | bytes 1572872 | tf_op jit(solution)/shard_map/ppermute | solution.py:53
  48.7 18.3 %collective-permute-start.16 = (bf16[2,128,1024]{2,1,0:T(8,128)(2,1)S(1)}, bf16[2,128,1024]{2,1,0:T(8,128)(2,1)S(1)}, u32[]{:S(2)}, u32[]{:S(2)}) collective-permute-start(bf16[2,128,1024]{2,1,0:T(8,128)(2,1)S(1)} %pad_maximum_fusion.2), channel_id=1, source_target_pairs={{0,24},{4,100},{8,0},{12,108},{16,8},{20,116},{24,16},{28,124},{32... | collective-permute-start | bytes 1572872 | tf_op jit(solution)/shard_map/ppermute | solution.py:53
  61.9 21.1 %collective-permute-start.24 = (bf16[2,512,512]{2,1,0:T(8,128)(2,1)S(1)}, bf16[2,512,512]{2,1,0:T(8,128)(2,1)S(1)}, u32[]{:S(2)}, u32[]{:S(2)}) collective-permute-start(bf16[2,512,512]{2,1,0:T(8,128)(2,1)S(1)} %collective-permute-done.refs_1_), channel_id=1, source_target_pairs={{0,4},{4,0},{8,12},{12,8},{16,20},{20,16},{24,28},{28,24},{32,36},... | collective-permute-start | bytes 3145736 | tf_op jit(solution)/shard_map/ppermute | solution.py:49
  66.9 16.0 %collective-permute-start.2 = (bf16[2,512,512]{2,1,0:T(8,128)(2,1)S(1)}, bf16[2,512,512]{2,1,0:T(8,128)(2,1)S(1)}, u32[]{:S(2)}, u32[]{:S(2)}) collective-permute-start(bf16[2,512,512]{2,1,0:T(8,128)(2,1)S(1)} %collective-permute-done.1.refs_0_), channel_id=1, source_target_pairs={{0,1},{4,7},{8,9},{12,15},{16,17},{20,23},{24,25},{28,31},{32,33},... | collective-permute-start | bytes 3145736 | tf_op jit(solution)/shard_map/ppermute | solution.py:64
  67.1 19.0 %collective-permute-start.25 = (bf16[2,512,512]{2,1,0:T(8,128)(2,1)S(1)}, bf16[2,512,512]{2,1,0:T(8,128)(2,1)S(1)}, u32[]{:S(2)}, u32[]{:S(2)}) collective-permute-start(bf16[2,512,512]{2,1,0:T(8,128)(2,1)S(1)} %collective-permute-done.4.refs_3_), channel_id=1, source_target_pairs={{0,4},{4,0},{8,12},{12,8},{16,20},{20,16},{24,28},{28,24},{32,36},... | collective-permute-start | bytes 3145736 | tf_op jit(solution)/shard_map/ppermute | solution.py:49
  67.1 6.4 %collective-permute-start.19 = (bf16[128,1024]{1,0:T(8,128)(2,1)S(1)}, bf16[128,1024]{1,0:T(8,128)(2,1)S(1)}, u32[]{:S(2)}, u32[]{:S(2)}) collective-permute-start(bf16[128,1024]{1,0:T(8,128)(2,1)S(1)} %slice_bitcast_fusion.2), channel_id=1, source_target_pairs={{0,8},{4,36},{8,16},{12,44},{16,24},{20,52},{24,0},{28,60},{32,40}... | collective-permute-start | bytes 786440 | tf_op jit(solution)/shard_map/ppermute | solution.py:53
  68.2 7.6 %collective-permute-start.22 = (bf16[128,1024]{1,0:T(8,128)(2,1)S(1)}, bf16[128,1024]{1,0:T(8,128)(2,1)S(1)}, u32[]{:S(2)}, u32[]{:S(2)}) collective-permute-start(bf16[128,1024]{1,0:T(8,128)(2,1)S(1)} %slice_bitcast_fusion), channel_id=1, source_target_pairs={{0,24},{4,100},{8,0},{12,108},{16,8},{20,116},{24,16},{28,124},{32... | collective-permute-start | bytes 786440 | tf_op jit(solution)/shard_map/ppermute | solution.py:53
  73.6 9.3 %collective-permute-start.18 = (bf16[2,128,1024]{2,1,0:T(8,128)(2,1)S(1)}, bf16[2,128,1024]{2,1,0:T(8,128)(2,1)S(1)}, u32[]{:S(2)}, u32[]{:S(2)}) collective-permute-start(bf16[2,128,1024]{2,1,0:T(8,128)(2,1)S(1)} %slice.47), channel_id=1, source_target_pairs={{0,8},{4,36},{8,16},{12,44},{16,24},{20,52},{24,0},{28,60},{32,40}... | collective-permute-start | bytes 1572872 | tf_op jit(solution)/shard_map/ppermute | solution.py:53
  75.7 10.4 %collective-permute-start.21 = (bf16[2,128,1024]{2,1,0:T(8,128)(2,1)S(1)}, bf16[2,128,1024]{2,1,0:T(8,128)(2,1)S(1)}, u32[]{:S(2)}, u32[]{:S(2)}) collective-permute-start(bf16[2,128,1024]{2,1,0:T(8,128)(2,1)S(1)} %slice.50), channel_id=1, source_target_pairs={{0,24},{4,100},{8,0},{12,108},{16,8},{20,116},{24,16},{28,124},{32... | collective-permute-start | bytes 1572872 | tf_op jit(solution)/shard_map/ppermute | solution.py:53
  95.6 10.1 %collective-permute-start.31 = (bf16[4,512,512]{2,1,0:T(8,128)(2,1)S(1)}, bf16[4,512,512]{2,1,0:T(8,128)(2,1)S(1)}, u32[]{:S(2)}, u32[]{:S(2)}) collective-permute-start(bf16[4,512,512]{2,1,0:T(8,128)(2,1)S(1)} %get-tuple-element.19), channel_id=1, source_target_pairs={{0,4},{4,0},{8,12},{12,8},{16,20},{20,16},{24,28},{28,24},{32,36},... | collective-permute-start | bytes 6291464 | tf_op jit(solution)/shard_map/ppermute | solution.py:49
  95.7 5.6 %collective-permute-start.3 = (bf16[2,512,512]{2,1,0:T(8,128)(2,1)S(1)}, bf16[2,512,512]{2,1,0:T(8,128)(2,1)S(1)}, u32[]{:S(2)}, u32[]{:S(2)}) collective-permute-start(bf16[2,512,512]{2,1,0:T(8,128)(2,1)S(1)} %collective-permute-done.2.refs_1_), channel_id=1, source_target_pairs={{0,4},{4,0},{8,12},{12,8},{16,20},{20,16},{24,28},{28,24},{32,36},... | collective-permute-start | bytes 3145736 | tf_op jit(solution)/shard_map/ppermute | solution.py:49
  105.9 9.7 %collective-permute-start.32 = (bf16[256,512]{1,0:T(8,128)(2,1)S(1)}, bf16[256,512]{1,0:T(8,128)(2,1)S(1)}, u32[]{:S(2)}, u32[]{:S(2)}) collective-permute-start(bf16[256,512]{1,0:T(8,128)(2,1)S(1)} %get-tuple-element.20), channel_id=1, source_target_pairs={{0,1},{1,2},{2,3},{3,0},{4,5},{5,6},{6,7},{7,4},{8,9},{9,10},{10,1... | collective-permute-start | bytes 786440 | tf_op jit(solution)/shard_map/ppermute | solution.py:68
  112.1 9.2 %collective-permute-start.35 = (bf16[256,512]{1,0:T(8,128)(2,1)S(1)}, bf16[256,512]{1,0:T(8,128)(2,1)S(1)}, u32[]{:S(2)}, u32[]{:S(2)}) collective-permute-start(bf16[256,512]{1,0:T(8,128)(2,1)S(1)} %get-tuple-element.23), channel_id=1, source_target_pairs={{0,3},{1,0},{2,1},{3,2},{4,7},{5,4},{6,5},{7,6},{8,11},{9,8},{10,9... | collective-permute-start | bytes 786440 | tf_op jit(solution)/shard_map/ppermute | solution.py:68
  113.9 27.5 %collective-permute-start.34 = (bf16[256,512]{1,0:T(8,128)(2,1)S(1)}, bf16[256,512]{1,0:T(8,128)(2,1)S(1)}, u32[]{:S(2)}, u32[]{:S(2)}) collective-permute-start(bf16[256,512]{1,0:T(8,128)(2,1)S(1)} %get-tuple-element.21), channel_id=1, source_target_pairs={{0,3},{1,0},{2,1},{3,2},{4,7},{5,4},{6,5},{7,6},{8,11},{9,8},{10,9... | collective-permute-start | bytes 786440 | tf_op jit(solution)/shard_map/ppermute | solution.py:68
  115.7 25.7 %collective-permute-start.33 = (bf16[256,512]{1,0:T(8,128)(2,1)S(1)}, bf16[256,512]{1,0:T(8,128)(2,1)S(1)}, u32[]{:S(2)}, u32[]{:S(2)}) collective-permute-start(bf16[256,512]{1,0:T(8,128)(2,1)S(1)} %merge.5), channel_id=1, source_target_pairs={{0,1},{1,2},{2,3},{3,0},{4,5},{5,6},{6,7},{7,4},{8,9},{9,10},{10,1... | collective-permute-start | bytes 786440 | tf_op jit(solution)/shard_map/ppermute | solution.py:68
  116.1 26.7 %collective-permute-start.37 = (bf16[256,512]{1,0:T(8,128)(2,1)S(1)}, bf16[256,512]{1,0:T(8,128)(2,1)S(1)}, u32[]{:S(2)}, u32[]{:S(2)}) collective-permute-start(bf16[256,512]{1,0:T(8,128)(2,1)S(1)} %get-tuple-element.24), channel_id=1, source_target_pairs={{0,1},{1,2},{2,3},{3,0},{4,5},{5,6},{6,7},{7,4},{8,9},{9,10},{10,1... | collective-permute-start | bytes 786440 | tf_op jit(solution)/shard_map/ppermute | solution.py:68
  121.4 21.4 %collective-permute-start.36 = (bf16[256,512]{1,0:T(8,128)(2,1)S(1)}, bf16[256,512]{1,0:T(8,128)(2,1)S(1)}, u32[]{:S(2)}, u32[]{:S(2)}) collective-permute-start(bf16[256,512]{1,0:T(8,128)(2,1)S(1)} %merge.7), channel_id=1, source_target_pairs={{0,3},{1,0},{2,1},{3,2},{4,7},{5,4},{6,5},{7,6},{8,11},{9,8},{10,9... | collective-permute-start | bytes 786440 | tf_op jit(solution)/shard_map/ppermute | solution.py:68
  124.5 1.2 collective-permute-start.27
  125.6 4.8 %collective-permute-start.29 = (f32[1,512]{1,0:T(1,128)S(1)}, f32[1,512]{1,0:T(1,128)S(1)}, u32[]{:S(2)}, u32[]{:S(2)}) collective-permute-start(f32[1,512]{1,0:T(1,128)S(1)} %add.24), channel_id=1, source_target_pairs={{0,1},{1,2},{2,3},{3,0},{4,5},{5,6},{6,7},{7,4},{8,9},{9,10},{10,1... | collective-permute-start | bytes 6152 | tf_op jit(solution)/shard_map/ppermute | solution.py:68
  130.4 3.6 %collective-permute-start.30 = (f32[1,512]{1,0:T(1,128)S(1)}, f32[1,512]{1,0:T(1,128)S(1)}, u32[]{:S(2)}, u32[]{:S(2)}) collective-permute-start(f32[1,512]{1,0:T(1,128)S(1)} %add.24), channel_id=1, source_target_pairs={{0,3},{1,0},{2,1},{3,2},{4,7},{5,4},{6,5},{7,6},{8,11},{9,8},{10,9... | collective-permute-start | bytes 6152 | tf_op jit(solution)/shard_map/ppermute | solution.py:68
  134.0 5.1 %collective-permute-start.28 = (f32[1,512]{1,0:T(1,128)S(1)}, f32[1,512]{1,0:T(1,128)S(1)}, u32[]{:S(2)}, u32[]{:S(2)}) collective-permute-start(f32[1,512]{1,0:T(1,128)S(1)} %add.24), channel_id=1, source_target_pairs={{0,2},{1,3},{2,0},{3,1},{4,6},{5,7},{6,4},{7,5},{8,10},{9,11},{10,... | collective-permute-start | bytes 6152 | tf_op jit(solution)/shard_map/ppermute | solution.py:68
